TPU v7x, 256 devices: a whole 4x4x8 slice. The times are simulated.
256 devices in a mesh: shot: 32 (over z_lo, y, core), sub: 8 (over x, z_hi).
Axes of the slice: x: 4, y: 4, z: 8 (z_hi: 2, z_lo: 4; z = z_hi * 4 + z_lo), core: 2. Of those that a mesh axis runs over, the one named last changes fastest.
Arguments:
- velocity_tiles: float32 [384, 64, 256], P('shot', 'sub'), may hold values from 0.05 to 0.2
- forward_state: bfloat16 [32, 2, 64, 64, 128], P('shot', None, 'sub'), may hold values from -1.5 to 1.5
- adjoint_state: bfloat16 [32, 2, 64, 64, 128], P('shot', None, 'sub'), may hold values from -1.5 to 1.5
- wavelet: float32 [32, 4], P('shot'), may hold values from -4 to 4
- source_cell: int32 [32], P('shot'), may hold values from 0 to 524287
- receiver_cell: int32 [32, 256], P('shot'), may hold values from 0 to 524287
- residual: float32 [32, 4, 256], P('shot'), may hold values from -4 to 4
- aperture_row: int32 [32], replicated, may hold values from 0 to 12, as said below
- aperture_col: int32 [32], replicated, may hold values from 1 to 255, as said below
Outputs:
- gradient: float32 [384, 64, 256], P('shot', 'sub')
Inputs may be any that keep to these rules, and one draw needn't show every extreme that they name: Every aperture lies in the model: rows aperture_row[s] to aperture_row[s] + 3 are model tile rows. aperture_col[s] is never a multiple of 16; the aperture's columns end inside the model.
All inputs are finite; a program needn't handle non-finite values.
Results may differ from a plain program's by a relative error of at most 0.0004.
Values sent between devices are 32-bit elements; how exact they have to be, the bound alone decides.
A program may use at most 64 MiB of HBM per device.

v0:
```python
import jax
import jax.numpy as jnp
from jax import lax
from jax.sharding import PartitionSpec as P
from jax.experimental import pallas as pl
from jax.experimental.pallas import tpu as pltpu

TILE = 16
RY = 3
SHOTS_DEV = 1
NT = 4
RADIUS = 4
AP_ROWS = 4
AP_COLS = 8
TILE_DEV = 12
AX = 64
AY = 128


COEFFS = (-205.0 / 72.0, 8.0 / 5.0, -1.0 / 5.0, 8.0 / 315.0, -1.0 / 560.0)
IMAGE_SCALE = 1.0 / 64.0


def padded_2(array, sides, width):
    for axis, dim in sides:
        size, length = (lax.axis_size(axis), array.shape[dim])
        up = [(i, (i + 1) % size) for i in range(size - 1)]
        down = [(j, i) for i, j in up]
        last = lax.slice_in_dim(array, length - width, length, axis=dim)
        first = lax.slice_in_dim(array, 0, width, axis=dim)
        before = lax.ppermute(last, axis, up)
        after = lax.ppermute(first, axis, down)
        array = jnp.concatenate([before, array, after], axis=dim)
    return array


def laplace(padded, depth_cells, row_cells, column_cells):
    r = 4
    center = padded[r : r + depth_cells, r : r + row_cells, r : r + column_cells]
    summed = 3.0 * COEFFS[0] * center
    for k in range(1, 5):
        nearby = padded[r + k : r + k + depth_cells, r : r + row_cells, r : r + column_cells]
        nearby = (
            nearby + padded[r - k : r - k + depth_cells, r : r + row_cells, r : r + column_cells]
        )
        nearby = (
            nearby + padded[r : r + depth_cells, r + k : r + k + row_cells, r : r + column_cells]
        )
        nearby = (
            nearby + padded[r : r + depth_cells, r - k : r - k + row_cells, r : r + column_cells]
        )
        nearby = (
            nearby + padded[r : r + depth_cells, r : r + row_cells, r + k : r + k + column_cells]
        )
        nearby = (
            nearby + padded[r : r + depth_cells, r : r + row_cells, r - k : r - k + column_cells]
        )
        summed = summed + COEFFS[k] * nearby
    return summed


def wave_operator(field):
    padded = padded_2(field, (("sub", 0),), RADIUS)
    padded = jnp.pad(padded, ((0, 0), (4, 4), (4, 4)))
    return laplace(padded, field.shape[0], AX, AY)


def adjoint_operator(field):
    padded = padded_2(field, (("sub", 0),), RADIUS)
    padded = jnp.pad(padded, ((0, 0), (4, 4), (4, 4)))
    return laplace(padded, field.shape[0], AX, AY)


def slot_layout(row_start, col_start, owner_row, owner_col, own_cols, caps):
    block_row = (owner_row - row_start) % AP_ROWS
    first_col = (owner_col - col_start // TILE) % own_cols
    block_col = first_col + own_cols * jnp.arange(caps, dtype=jnp.int32)
    usable = block_col <= AP_COLS
    return (block_row, block_col, usable)


def owner_slots(row_table, col_table, shot_list, groups, own_cols, caps):
    myself = lax.axis_index("shot")
    owner_row = myself // own_cols
    owner_col = myself % own_cols
    senders = jnp.arange(groups, dtype=jnp.int32)[:, None]
    picked = senders * SHOTS_DEV + jnp.asarray(shot_list, dtype=jnp.int32)[None, :]
    row_start = row_table[picked][..., None]
    col_start = col_table[picked][..., None]
    block_row, block_col, usable = slot_layout(
        row_start, col_start, owner_row, owner_col, own_cols, caps
    )
    tile_row = row_start + block_row
    tile_col = col_start // TILE + block_col
    local = tile_row // AP_ROWS * RY + tile_col // own_cols
    local = jnp.clip(local, 0, TILE_DEV - 1)
    return (local.reshape(-1), usable.reshape(-1))


def outgoing(velocity_tiles, row_table, col_table, shot_list, groups, own_cols, caps):
    local, usable = owner_slots(row_table, col_table, shot_list, groups, own_cols, caps)
    chosen = velocity_tiles[local]
    chosen = jnp.where(usable[:, None, None], chosen, 0.0)
    return chosen.reshape(
        groups, len(shot_list) * caps, velocity_tiles.shape[1], velocity_tiles.shape[2]
    )


def accumulate(gradient, returned, row_table, col_table, shot_list, groups, own_cols, caps):
    local, usable = owner_slots(row_table, col_table, shot_list, groups, own_cols, caps)
    pieces = returned.reshape(-1, gradient.shape[1], gradient.shape[2])
    return gradient.at[local].add(jnp.where(usable[:, None, None], pieces, 0.0))


def assemble(received, slot_base, row_start, col_start, own_cols):
    depth_cells = received.shape[2]
    slot_count = received.shape[1]
    rel_row = jnp.arange(AP_ROWS, dtype=jnp.int32)[:, None]
    rel_col = jnp.arange(AP_COLS + 1, dtype=jnp.int32)[None, :]
    source_owner = (row_start + rel_row) % AP_ROWS * own_cols + (
        col_start // TILE + rel_col
    ) % own_cols
    flat_index = (source_owner * slot_count + slot_base + rel_col // own_cols).reshape(-1)
    pieces = received.reshape(-1, depth_cells, TILE * TILE)[flat_index]
    block = pieces.reshape(AP_ROWS, AP_COLS + 1, depth_cells, TILE, TILE)
    block = block.transpose(2, 0, 3, 1, 4).reshape(depth_cells, AX, (AP_COLS + 1) * TILE)
    return lax.dynamic_slice_in_dim(block, col_start % TILE, AY, 2)


def disperse(image, row_start, col_start, groups, own_cols, caps):
    depth_cells = image.shape[0]
    wide = jnp.zeros((depth_cells, AX, (AP_COLS + 1) * TILE), jnp.float32)
    wide = lax.dynamic_update_slice_in_dim(wide, image, col_start % TILE, 2)
    pieces = wide.reshape(depth_cells, AP_ROWS, TILE, AP_COLS + 1, TILE)
    pieces = pieces.transpose(1, 3, 0, 2, 4).reshape(
        AP_ROWS * (AP_COLS + 1), depth_cells, TILE * TILE
    )
    owners = jnp.arange(groups, dtype=jnp.int32)[:, None]
    block_row, block_col, usable = slot_layout(
        row_start, col_start, owners // own_cols, owners % own_cols, own_cols, caps
    )
    position = jnp.clip(block_row * (AP_COLS + 1) + block_col, 0, AP_ROWS * (AP_COLS + 1) - 1)
    return jnp.where(usable[..., None, None], pieces[position], 0.0)


def shift_rows(c, k, rows):
    if k > 0:
        moved = pltpu.roll(c, AX - k, 0)
        return jnp.where(rows < AX - k, moved, 0.0)
    moved = pltpu.roll(c, -k, 0)
    return jnp.where(rows >= -k, moved, 0.0)


def shift_lanes(c, k, lanes):
    if k > 0:
        moved = pltpu.roll(c, AY - k, 1)
        return jnp.where(lanes < AY - k, moved, 0.0)
    moved = pltpu.roll(c, -k, 1)
    return jnp.where(lanes >= -k, moved, 0.0)


def plane_stencil(buf, r, p, rows, lanes):
    c = buf[r, p]
    summed = (3.0 * COEFFS[0]) * c
    for k in range(1, 5):
        nearby = buf[r, p + k] + buf[r, p - k]
        nearby = nearby + shift_rows(c, k, rows)
        nearby = nearby + shift_rows(c, -k, rows)
        nearby = nearby + shift_lanes(c, k, lanes)
        nearby = nearby + shift_lanes(c, -k, lanes)
        summed = summed + COEFFS[k] * nearby
    return summed


def migrate_kernel(model_ref, pf_ref, qa_ref, inj_ref, img_ref, pad_p, pad_q, lap, qs, send_sem, recv_sem):
    me = lax.axis_index("sub")
    n_sub = lax.axis_size("sub")
    depth = model_ref.shape[0]
    halo = jnp.zeros((RADIUS, AX, AY), jnp.float32)
    for r in range(NT):
        for buf in (pad_p, pad_q):
            buf[r, 0:RADIUS] = halo
            buf[r, RADIUS + depth : 2 * RADIUS + depth] = halo
    pad_p[0, RADIUS : RADIUS + depth] = pf_ref[0]
    pad_q[0, RADIUS : RADIUS + depth] = model_ref[...] * qa_ref[0]
    up_dev = lax.rem(me + 1, n_sub)
    down_dev = lax.rem(me + n_sub - 1, n_sub)
    barrier = pltpu.get_barrier_semaphore()
    pl.semaphore_signal(barrier, 1, device_id={"sub": up_dev}, device_id_type=pl.DeviceIdType.MESH)
    pl.semaphore_signal(barrier, 1, device_id={"sub": down_dev}, device_id_type=pl.DeviceIdType.MESH)
    pl.semaphore_wait(barrier, 2)
    rows = lax.broadcasted_iota(jnp.int32, (AX, AY), 0)
    lanes = lax.broadcasted_iota(jnp.int32, (AX, AY), 1)

    def exchange(r):
        descs = []
        for f, buf in enumerate((pad_p, pad_q)):
            down = pltpu.make_async_remote_copy(
                src_ref=buf.at[r, RADIUS : 2 * RADIUS],
                dst_ref=buf.at[r, RADIUS + depth : 2 * RADIUS + depth],
                send_sem=send_sem.at[r, f, 0],
                recv_sem=recv_sem.at[r, f, 0],
                device_id={"sub": down_dev},
                device_id_type=pl.DeviceIdType.MESH,
            )
            up = pltpu.make_async_remote_copy(
                src_ref=buf.at[r, depth : RADIUS + depth],
                dst_ref=buf.at[r, 0:RADIUS],
                send_sem=send_sem.at[r, f, 1],
                recv_sem=recv_sem.at[r, f, 1],
                device_id={"sub": up_dev},
                device_id_type=pl.DeviceIdType.MESH,
            )
            descs.append((down, up))

        @pl.when(me > 0)
        def _():
            for down, up in descs:
                down.start()

        @pl.when(me < n_sub - 1)
        def _():
            for down, up in descs:
                up.start()

        @pl.when(me > 0)
        def _():
            for down, up in descs:
                down.wait_send()
                up.wait_recv()

        @pl.when(me < n_sub - 1)
        def _():
            for down, up in descs:
                up.wait_send()
                down.wait_recv()

    for r in range(NT):
        exchange(r)

        def plane(j, carry, r=r):
            p = j + RADIUS
            lp = plane_stencil(pad_p, r, p, rows, lanes)
            lap[r, j] = lp
            if r < NT - 1:
                before = pf_ref[1, j] if r == 0 else pad_p[r - 1, p]
                following = 2.0 * pad_p[r, p] - before + model_ref[j] * lp
                pad_p[r + 1, p] = following + inj_ref[r, j]
            lq = plane_stencil(pad_q, r, p, rows, lanes)
            now = qa_ref[0, j] if r == 0 else qs[r - 1, j]
            if r == 0:
                later = qa_ref[1, j]
            elif r == 1:
                later = qa_ref[0, j]
            else:
                later = qs[r - 2, j]
            result = 2.0 * now - later + lq
            result = result + inj_ref[NT - 1 + NT - 1 - r, j]
            qs[r, j] = result
            if r < NT - 1:
                pad_q[r + 1, p] = model_ref[j] * result
            return carry

        lax.fori_loop(0, depth, plane, 0)

    def image_plane(j, carry):
        image = jnp.zeros((AX, AY), jnp.float32)
        for r in range(NT):
            image = image + qs[r, j] * lap[NT - 1 - r, j]
        img_ref[j] = IMAGE_SCALE * image
        return carry

    lax.fori_loop(0, depth, image_plane, 0)


def migrate(model, state_fwd, state_adj, wave, source, receivers, resid):
    depth_cells = model.shape[0]
    plane = AX * AY
    block = depth_cells * plane
    offset = lax.axis_index("sub") * depth_cells
    slots = 2 * NT - 1

    def local(cells, slot):
        level = cells // plane - offset
        inside = (level >= 0) & (level < depth_cells)
        target = slot * block + level * plane + cells % plane
        return jnp.where(inside, target, slots * block)

    src_idx = jnp.stack([local(source, n) for n in range(NT - 1)])
    rcv_idx = jnp.concatenate([local(receivers, NT - 1 + n) for n in range(NT)])
    idx = jnp.concatenate([src_idx, rcv_idx])
    vals = jnp.concatenate([wave[: NT - 1], resid.reshape(-1)])
    inj = jnp.zeros((slots * block,), jnp.float32).at[idx].add(vals, mode="drop")
    inj = inj.reshape(slots, depth_cells, AX, AY)
    vmem = pl.BlockSpec(memory_space=pltpu.VMEM)
    padded = (NT, depth_cells + 2 * RADIUS, AX, AY)
    return pl.pallas_call(
        migrate_kernel,
        out_shape=jax.ShapeDtypeStruct(model.shape, jnp.float32),
        in_specs=[vmem] * 4,
        out_specs=vmem,
        scratch_shapes=[
            pltpu.VMEM(padded, jnp.float32),
            pltpu.VMEM(padded, jnp.float32),
            pltpu.VMEM((NT, depth_cells, AX, AY), jnp.float32),
            pltpu.VMEM((NT, depth_cells, AX, AY), jnp.float32),
            pltpu.SemaphoreType.DMA((NT, 2, 2)),
            pltpu.SemaphoreType.DMA((NT, 2, 2)),
        ],
        compiler_params=pltpu.CompilerParams(collective_id=0, has_side_effects=True),
    )(model, state_fwd.astype(jnp.float32), state_adj.astype(jnp.float32), inj)


def body(
    velocity_tiles,
    forward_state,
    adjoint_state,
    wavelet,
    source_cell,
    receiver_cell,
    residual,
    aperture_row,
    aperture_col,
):
    groups = lax.axis_size("shot")
    own_cols = groups // AP_ROWS
    caps = (AP_COLS + own_cols) // own_cols
    myself = lax.axis_index("shot")
    shots_here = forward_state.shape[0]
    gradient = jnp.zeros(velocity_tiles.shape, jnp.float32)
    every_shot = list(range(shots_here))
    sending = outgoing(
        velocity_tiles, aperture_row, aperture_col, every_shot, groups, own_cols, caps
    )
    fetched = lax.all_to_all(sending, "shot", split_axis=0, concat_axis=0, tiled=True)
    images = []
    for k in every_shot:
        slot_base = k * caps
        shot_id = myself * SHOTS_DEV + k
        row_start = aperture_row[shot_id]
        col_start = aperture_col[shot_id]
        model = assemble(fetched, slot_base, row_start, col_start, own_cols)
        image = migrate(
            model,
            forward_state[k],
            adjoint_state[k],
            wavelet[k],
            source_cell[k],
            receiver_cell[k],
            residual[k],
        )
        images.append(disperse(image, row_start, col_start, groups, own_cols, caps))
    returned = lax.all_to_all(images[0], "shot", split_axis=0, concat_axis=0, tiled=True)
    gradient = accumulate(
        gradient, returned, aperture_row, aperture_col, every_shot, groups, own_cols, caps
    )
    return gradient


def solution(mesh):
    placed = (
        P("shot", "sub", None),
        P("shot", None, "sub", None, None),
        P("shot", None, "sub", None, None),
        P("shot", None),
        P("shot"),
        P("shot", None),
        P("shot", None, None),
        P(),
        P(),
    )
    return jax.shard_map(
        body, mesh=mesh, in_specs=placed, out_specs=P("shot", "sub", None), check_vma=False
    )
```

profile of v0, /device:TPU:5, one launch (start us, length us, event | category | flops | bytes accessed | tf_op | source)
XLA Modules:
  0.0 194.4 jit_solution(6300186643990203098)
XLA Ops:
  0.0 1.3 dynamic_slice.9
  3.9 1.4 gather_fusion.1
  5.6 1.4 gather_fusion
  7.1 0.1 add.833
  7.4 0.6 gather_fusion.2
  8.0 0.9 broadcast_select_fusion.1
  9.0 9.4 %all-to-all-start = ((f32[32,2,8,256]{3,2,1,0:T(8,128)}), f32[32,2,8,256]{3,2,1,0:T(8,128)S(1)}, u32[]{:S(2)}, u32[]{:S(2)}) async-start(f32[32,2,8,256]{3,2,1,0:T(8,128)} %broadcast_select_fusion.1), calls=%async_computation | async-start | bytes 1048576 | tf_op jit(solution)/shard_map/all_to_all | solution.py:335
  18.4 0.6 dynamic_slice.10
  19.0 0.7 fusion.6
  19.6 0.7 fusion.8
  21.7 8.6 %scatter_custom_fusion = f32[458752]{0:T(1024)} fusion(s32[1027]{0:T(1024)S(1)} %fusion.2, f32[1027]{0:T(1024)S(1)} %pad_maximum_fusion, f32[]{:T(128)} %constant.279.clone.1), kind=kCustom, calls=%fused_computation.7 | custom fusion | flops 1027 | bytes 1835012 | tf_op jit(solution)/shard_map/scatter-add | solution.py:293
  30.3 1.1 bitcast_convert_fusion
  31.4 3.3 %all-to-all-done = f32[32,2,8,256]{3,2,1,0:T(8,128)S(1)} async-done(((f32[32,2,8,256]{3,2,1,0:T(8,128)}), f32[32,2,8,256]{3,2,1,0:T(8,128)S(1)}, u32[]{:S(2)}, u32[]{:S(2)}) %all-to-all-start) | async-done | bytes 524320 | tf_op jit(solution)/shard_map/all_to_all | solution.py:335
  34.8 0.6 gather_fusion.3
  35.4 0.7 reshape.1314
  36.1 2.5 %copy.18 = f32[8,4,16,9,16]{2,1,4,3,0:T(4,128)} copy(f32[8,4,16,9,16]{4,2,0,3,1:T(8,128)S(1)} %bitcast.57) | data formatting | bytes 589824 | tf_op jit(solution)/shard_map/transpose | solution.py:126
  38.5 2.5 %reshape.1315 = f32[8,64,144]{1,2,0:T(8,128)S(1)} reshape(f32[8,4,16,9,16]{2,1,4,3,0:T(4,128)} %copy.18) | data formatting | bytes 589824 | tf_op jit(solution)/shard_map/reshape | solution.py:126
  41.1 0.9 copy.22.model_ref
  42.0 106.2 %shard_map.109 = f32[8,64,128]{2,1,0:T(8,128)} custom-call(f32[8,64,128]{2,1,0:T(8,128)} %copy.22.model_ref, f32[2,8,64,128]{3,2,1,0:T(8,128)} %get-tuple-element.19.pf_ref, f32[2,8,64,128]{3,2,1,0:T(8,128)} %get-tuple-element.18.qa_ref, f32[7,8,64,128]{3,2,1,0:T(8,128)} %bitcast.59), custom_call_target="tpu_custom_call" | custom-call | tf_op jit(solution)/shard_map/pallas_call | solution.py:297
  148.2 1.1 copy.20
  149.4 1.1 dynamic_update_slice.3
  150.5 1.0 reshape.1317
  151.6 2.5 %copy.21 = f32[4,9,8,16,16]{4,3,2,1,0:T(8,128)} copy(f32[4,9,8,16,16]{3,0,4,1,2:T(4,128)S(1)} %bitcast.58) | data formatting | bytes 589824 | tf_op jit(solution)/shard_map/transpose | solution.py:135
  154.1 2.5 %reshape.1318 = f32[36,8,256]{2,1,0:T(8,128)S(1)} reshape(f32[4,9,8,16,16]{4,3,2,1,0:T(8,128)} %copy.21) | data formatting | bytes 589824 | tf_op jit(solution)/shard_map/reshape | solution.py:135
  156.6 0.6 gather_fusion.4
  157.2 0.9 broadcast_select_fusion
  158.2 11.3 %all-to-all-start.1 = ((f32[32,2,8,256]{3,2,1,0:T(8,128)}), f32[32,2,8,256]{3,2,1,0:T(8,128)S(1)}, u32[]{:S(2)}, u32[]{:S(2)}) async-start(f32[32,2,8,256]{3,2,1,0:T(8,128)} %broadcast_select_fusion), calls=%async_computation.1 | async-start | bytes 1048576 | tf_op jit(solution)/shard_map/all_to_all | solution.py:353
  169.6 0.1 le.32
  169.7 16.2 %all-to-all-done.1 = f32[32,2,8,256]{3,2,1,0:T(8,128)S(1)} async-done(((f32[32,2,8,256]{3,2,1,0:T(8,128)}), f32[32,2,8,256]{3,2,1,0:T(8,128)S(1)}, u32[]{:S(2)}, u32[]{:S(2)}) %all-to-all-start.1) | async-done | bytes 524320 | tf_op jit(solution)/shard_map/all_to_all | solution.py:353
  185.9 0.1 bitcast_select_fusion
  186.1 0.6 broadcast_in_dim.78
  186.7 7.7 %scatter_fusion = f32[12,8,256]{2,1,0:T(8,128)} fusion(f32[12,8,256]{2,1,0:T(8,128)} %broadcast_in_dim.78, s32[64]{0:T(128)S(1)} %fusion.15, f32[64,8,256]{2,1,0:T(8,128)S(1)} %bitcast_select_fusion), kind=kCustom, calls=%fused_computation.6 | custom fusion | flops 131072 | bytes 1573120 | tf_op jit(solution)/shard_map/scatter-add | solution.py:112
  (45 shorter events, 1.4 us)
Async XLA Ops:
  0.0 7.4 %copy-start = (f32[12,8,256]{2,1,0:T(8,128)S(1)}, f32[12,8,256]{2,1,0:T(8,128)}, u32[]{:S(2)}) copy-start(f32[12,8,256]{2,1,0:T(8,128)} %param.11) | copy-start | bytes 294916
  5.5 12.8 %copy-start.1 = (s32[32]{0:T(128)S(1)}, s32[32]{0:T(128)}, u32[]{:S(2)}) copy-start(s32[32]{0:T(128)} %param.18) | copy-start | bytes 388
  5.5 14.8 %copy-start.5 = (s32[1,256]{1,0:T(1,128)S(1)}, s32[1,256]{1,0:T(1,128)}, u32[]{:S(2)}) copy-start(s32[1,256]{1,0:T(1,128)} %param.16) | copy-start | bytes 3076
  5.5 14.9 %copy-start.6 = (f32[1,4]{1,0:T(1,128)S(1)}, f32[1,4]{1,0:T(1,128)}, u32[]{:S(2)}) copy-start(f32[1,4]{1,0:T(1,128)} %param.14) | copy-start | bytes 52
  5.6 15.7 %copy-start.4 = (f32[1,4,256]{2,1,0:T(4,128)S(1)}, f32[1,4,256]{2,1,0:T(4,128)}, u32[]{:S(2)}) copy-start(f32[1,4,256]{2,1,0:T(4,128)} %param.17) | copy-start | bytes 12292
  8.0 22.3 %copy-start.2 = (bf16[1,2,8,64,128]{4,3,2,1,0:T(8,128)(2,1)S(1)}, bf16[1,2,8,64,128]{4,3,2,1,0:T(8,128)(2,1)}, u32[]{:S(2)}) copy-start(bf16[1,2,8,64,128]{4,3,2,1,0:T(8,128)(2,1)} %param.13) | copy-start | bytes 786436
  8.0 22.3 %copy-start.3 = (bf16[1,2,8,64,128]{4,3,2,1,0:T(8,128)(2,1)S(1)}, bf16[1,2,8,64,128]{4,3,2,1,0:T(8,128)(2,1)}, u32[]{:S(2)}) copy-start(bf16[1,2,8,64,128]{4,3,2,1,0:T(8,128)(2,1)} %param.12) | copy-start | bytes 786436
  9.0 25.8 %all-to-all-start = ((f32[32,2,8,256]{3,2,1,0:T(8,128)}), f32[32,2,8,256]{3,2,1,0:T(8,128)S(1)}, u32[]{:S(2)}, u32[]{:S(2)}) async-start(f32[32,2,8,256]{3,2,1,0:T(8,128)} %broadcast_select_fusion.1), calls=%async_computation | async-start | bytes 1048576 | tf_op jit(solution)/shard_map/all_to_all | solution.py:335
  158.2 27.7 %all-to-all-start.1 = ((f32[32,2,8,256]{3,2,1,0:T(8,128)}), f32[32,2,8,256]{3,2,1,0:T(8,128)S(1)}, u32[]{:S(2)}, u32[]{:S(2)}) async-start(f32[32,2,8,256]{3,2,1,0:T(8,128)} %broadcast_select_fusion), calls=%async_computation.1 | async-start | bytes 1048576 | tf_op jit(solution)/shard_map/all_to_all | solution.py:353
where the time goes:
time: 197 us; the launch traced here: 194 us
  Pallas kernels  106 us (54%)
  local copies, waits for them, and re-layouts  23 us (12%)
  other arithmetic  21.2 us (11%)
  starting transfers between devices  20.7 us (11%)
  waiting for transfers between devices  19.6 us (10%)
  between operations  3.65 us (2%)
    pallas_call x1, Pallas kernels, migrate(): pl.pallas_call(migrate_kernel, out_shape=jax.ShapeDtypeStruct(model.shape...  106 us
    all_to_all x1, waiting for transfers between devices, body(): lax.all_to_all(images[0], 'shot', split_axis=0, concat_axis=0, tiled=True)  16.2 us
    all_to_all x1, starting transfers between devices, body(): lax.all_to_all(images[0], 'shot', split_axis=0, concat_axis=0, tiled=True)  11.3 us
    all_to_all x1, starting transfers between devices, body(): lax.all_to_all(sending, 'shot', split_axis=0, concat_axis=0, tiled=True)  9.36 us
    scatter-add x1, other arithmetic, migrate(): jnp.zeros((slots * block,), jnp.float32).at[idx].add(vals, mode='drop')  8.59 us
    scatter-add x1, other arithmetic, accumulate(): return gradient.at[local].add(jnp.where(usable[:, None, None], pieces, 0.0))  7.65 us
  transfers between devices with their start and end apart: 2, of which 2 were waited for; matrix products, arithmetic and copies ran while one was open for 6% of the time, Pallas kernels for 0%

commit v1 on v0

--- a/solution.py
+++ b/solution.py
@@ -84,9 +84,13 @@
     owner_row = myself // own_cols
     owner_col = myself % own_cols
     senders = jnp.arange(groups, dtype=jnp.int32)[:, None]
-    picked = senders * SHOTS_DEV + jnp.asarray(shot_list, dtype=jnp.int32)[None, :]
-    row_start = row_table[picked][..., None]
-    col_start = col_table[picked][..., None]
+    if SHOTS_DEV == 1 and list(shot_list) == [0]:
+        row_start = row_table[:groups].reshape(groups, 1, 1)
+        col_start = col_table[:groups].reshape(groups, 1, 1)
+    else:
+        picked = senders * SHOTS_DEV + jnp.asarray(shot_list, dtype=jnp.int32)[None, :]
+        row_start = row_table[picked][..., None]
+        col_start = col_table[picked][..., None]
     block_row, block_col, usable = slot_layout(
         row_start, col_start, owner_row, owner_col, own_cols, caps
     )
@@ -108,8 +112,12 @@
 
 def accumulate(gradient, returned, row_table, col_table, shot_list, groups, own_cols, caps):
     local, usable = owner_slots(row_table, col_table, shot_list, groups, own_cols, caps)
-    pieces = returned.reshape(-1, gradient.shape[1], gradient.shape[2])
-    return gradient.at[local].add(jnp.where(usable[:, None, None], pieces, 0.0))
+    pieces = returned.reshape(local.shape[0], -1)
+    hot = (local[:, None] == jnp.arange(gradient.shape[0], dtype=jnp.int32)[None, :]) & usable[:, None]
+    summed = jnp.einsum(
+        "st,sf->tf", hot.astype(jnp.float32), pieces, precision=lax.Precision.HIGHEST
+    )
+    return gradient + summed.reshape(gradient.shape)
 
 
 def assemble(received, slot_base, row_start, col_start, own_cols):
@@ -172,7 +180,18 @@
     return summed
 
 
-def migrate_kernel(model_ref, pf_ref, qa_ref, inj_ref, img_ref, pad_p, pad_q, lap, qs, send_sem, recv_sem):
+def split_bf16(values):
+    high = values.astype(jnp.bfloat16)
+    rest = values - high.astype(jnp.float32)
+    middle = rest.astype(jnp.bfloat16)
+    low = (rest - middle.astype(jnp.float32)).astype(jnp.bfloat16)
+    return (high, middle, low)
+
+
+def migrate_kernel(
+    src_ref, wave_ref, rrow_ref, rcol_ref, resid_ref, model_ref, pf_ref, qa_ref,
+    img_ref, pad_p, pad_q, lap, qs, inject, send_sem, recv_sem,
+):
     me = lax.axis_index("sub")
     n_sub = lax.axis_size("sub")
     depth = model_ref.shape[0]
@@ -191,6 +210,26 @@
     pl.semaphore_wait(barrier, 2)
     rows = lax.broadcasted_iota(jnp.int32, (AX, AY), 0)
     lanes = lax.broadcasted_iota(jnp.int32, (AX, AY), 1)
+    n_rec = rcol_ref.shape[0]
+    src_level = src_ref[0]
+    src_spot = (rows == src_ref[1]) & (lanes == src_ref[2])
+
+    def build_injection(step):
+        hit_y = lax.broadcasted_iota(jnp.int32, (n_rec, AY), 1) == rcol_ref[...]
+        spread = jnp.where(hit_y, resid_ref[:, step : step + 1], 0.0)
+        parts = split_bf16(spread)
+        rec_level = rrow_ref[0:1, :]
+        hit_x = lax.broadcasted_iota(jnp.int32, (AX, n_rec), 0) == rrow_ref[1:2, :]
+
+        def plane(j, carry):
+            picks = (hit_x & (rec_level == j)).astype(jnp.bfloat16)
+            total = jnp.dot(picks, parts[0], preferred_element_type=jnp.float32)
+            total = total + jnp.dot(picks, parts[1], preferred_element_type=jnp.float32)
+            total = total + jnp.dot(picks, parts[2], preferred_element_type=jnp.float32)
+            inject[j] = total
+            return carry
+
+        lax.fori_loop(0, depth, plane, 0)
 
     def exchange(r):
         descs = []
@@ -223,6 +262,9 @@
             for down, up in descs:
                 up.start()
 
+        return descs
+
+    def finish(descs):
         @pl.when(me > 0)
         def _():
             for down, up in descs:
@@ -236,7 +278,9 @@
                 down.wait_recv()
 
     for r in range(NT):
-        exchange(r)
+        descs = exchange(r)
+        build_injection(NT - 1 - r)
+        finish(descs)
 
         def plane(j, carry, r=r):
             p = j + RADIUS
@@ -245,7 +289,8 @@
             if r < NT - 1:
                 before = pf_ref[1, j] if r == 0 else pad_p[r - 1, p]
                 following = 2.0 * pad_p[r, p] - before + model_ref[j] * lp
-                pad_p[r + 1, p] = following + inj_ref[r, j]
+                source = jnp.where(src_spot & (src_level == j), wave_ref[r], 0.0)
+                pad_p[r + 1, p] = following + source
             lq = plane_stencil(pad_q, r, p, rows, lanes)
             now = qa_ref[0, j] if r == 0 else qs[r - 1, j]
             if r == 0:
@@ -255,7 +300,7 @@
             else:
                 later = qs[r - 2, j]
             result = 2.0 * now - later + lq
-            result = result + inj_ref[NT - 1 + NT - 1 - r, j]
+            result = result + inject[j]
             qs[r, j] = result
             if r < NT - 1:
                 pad_q[r + 1, p] = model_ref[j] * result
@@ -276,39 +321,45 @@
 def migrate(model, state_fwd, state_adj, wave, source, receivers, resid):
     depth_cells = model.shape[0]
     plane = AX * AY
-    block = depth_cells * plane
     offset = lax.axis_index("sub") * depth_cells
-    slots = 2 * NT - 1
-
-    def local(cells, slot):
+
+    def level_of(cells):
         level = cells // plane - offset
         inside = (level >= 0) & (level < depth_cells)
-        target = slot * block + level * plane + cells % plane
-        return jnp.where(inside, target, slots * block)
-
-    src_idx = jnp.stack([local(source, n) for n in range(NT - 1)])
-    rcv_idx = jnp.concatenate([local(receivers, NT - 1 + n) for n in range(NT)])
-    idx = jnp.concatenate([src_idx, rcv_idx])
-    vals = jnp.concatenate([wave[: NT - 1], resid.reshape(-1)])
-    inj = jnp.zeros((slots * block,), jnp.float32).at[idx].add(vals, mode="drop")
-    inj = inj.reshape(slots, depth_cells, AX, AY)
+        return jnp.where(inside, level, -1)
+
+    src = jnp.stack([level_of(source), source % plane // AY, source % AY]).astype(jnp.int32)
+    rrow = jnp.stack([level_of(receivers), receivers % plane // AY]).astype(jnp.int32)
+    rcol = (receivers % AY).astype(jnp.int32).reshape(-1, 1)
     vmem = pl.BlockSpec(memory_space=pltpu.VMEM)
+    smem = pl.BlockSpec(memory_space=pltpu.SMEM)
     padded = (NT, depth_cells + 2 * RADIUS, AX, AY)
+    field = (NT, depth_cells, AX, AY)
     return pl.pallas_call(
         migrate_kernel,
         out_shape=jax.ShapeDtypeStruct(model.shape, jnp.float32),
-        in_specs=[vmem] * 4,
+        in_specs=[smem, smem] + [vmem] * 6,
         out_specs=vmem,
         scratch_shapes=[
             pltpu.VMEM(padded, jnp.float32),
             pltpu.VMEM(padded, jnp.float32),
-            pltpu.VMEM((NT, depth_cells, AX, AY), jnp.float32),
-            pltpu.VMEM((NT, depth_cells, AX, AY), jnp.float32),
+            pltpu.VMEM(field, jnp.float32),
+            pltpu.VMEM(field, jnp.float32),
+            pltpu.VMEM(model.shape, jnp.float32),
             pltpu.SemaphoreType.DMA((NT, 2, 2)),
             pltpu.SemaphoreType.DMA((NT, 2, 2)),
         ],
         compiler_params=pltpu.CompilerParams(collective_id=0, has_side_effects=True),
-    )(model, state_fwd.astype(jnp.float32), state_adj.astype(jnp.float32), inj)
+    )(
+        src,
+        wave.astype(jnp.float32),
+        rrow,
+        rcol,
+        resid.T,
+        model,
+        state_fwd.astype(jnp.float32),
+        state_adj.astype(jnp.float32),
+    )
 
 
 def body(

time: 197 us -> 186 us (0.944); the launches traced: 194 us -> 186 us
  other arithmetic: 21.2 us -> 7.83 us
  waiting for transfers between devices: 19.6 us -> 25.5 us
    scatter-add x2 -> x0, other arithmetic: 16.2 us -> none  [the longest x1 8.59 us: migrate(): jnp.zeros((slots * block,), jnp.float32).at[idx].add(vals, mode='drop')]
    all_to_all x1, waiting for transfers between devices: 3.34 us -> 9.49 us  [body(): lax.all_to_all(sending, 'shot', split_axis=0, concat_axis=0, tiled=True)]
    gather x2 -> x0, local copies, waits for them, and re-layouts: 2.74 us -> none  [the longest x1 1.38 us: owner_slots(): row_start = row_table[picked][..., None]]
  transfers between devices with their start and end apart: 2 -> 2, of which waited for: 2 -> 2; matrix products, arithmetic and copies ran while one was open for 6% -> 4% of each run, Pallas kernels for 0% -> 0%
where the time goes in v1:
time: 186 us
  Pallas kernels  106 us (57%)
  waiting for transfers between devices  25.5 us (14%)
  local copies, waits for them, and re-layouts  21.4 us (12%)
  starting transfers between devices  20.6 us (11%)
  other arithmetic  7.83 us (4%)
  between operations  3.62 us (2%)
    pallas_call x1, Pallas kernels, migrate(): pl.pallas_call(migrate_kernel, out_shape=jax.ShapeDtypeStruct(model.shape...  106 us
    all_to_all x1, waiting for transfers between devices, body(): lax.all_to_all(images[0], 'shot', split_axis=0, concat_axis=0, tiled=True)  16 us
    all_to_all x1, starting transfers between devices, body(): lax.all_to_all(images[0], 'shot', split_axis=0, concat_axis=0, tiled=True)  11.3 us
    all_to_all x1, waiting for transfers between devices, body(): lax.all_to_all(sending, 'shot', split_axis=0, concat_axis=0, tiled=True)  9.49 us
    all_to_all x1, starting transfers between devices, body(): lax.all_to_all(sending, 'shot', split_axis=0, concat_axis=0, tiled=True)  9.36 us
  transfers between devices with their start and end apart: 2, of which 2 were waited for; matrix products, arithmetic and copies ran while one was open for 4% of the time, Pallas kernels for 0%

profile of v1, /device:TPU:5, one launch (start us, length us, event | category | flops | bytes accessed | tf_op | source)
XLA Modules:
  0.0 185.6 jit_solution(13202041652010799087)
XLA Ops:
  0.0 1.3 dynamic_slice.9
  4.0 0.7 and_select_fusion.13
  4.9 0.7 fusion.22
  6.0 0.6 gather_fusion
  6.6 0.9 broadcast_select_fusion.1
  7.5 9.4 %all-to-all-start = ((f32[32,2,8,256]{3,2,1,0:T(8,128)}), f32[32,2,8,256]{3,2,1,0:T(8,128)S(1)}, u32[]{:S(2)}, u32[]{:S(2)}) async-start(f32[32,2,8,256]{3,2,1,0:T(8,128)} %broadcast_select_fusion.1), calls=%async_computation | async-start | bytes 1048576 | tf_op jit(solution)/shard_map/all_to_all | solution.py:386
  16.9 0.6 dynamic_slice.10
  18.2 0.6 fusion.11
  18.8 0.6 fusion.13
  19.7 0.8 copy.26
  20.7 0.6 pad_add_fusion.rrow_ref
  21.3 0.7 pad_add_fusion.1.src_ref
  22.0 0.7 add_select_fusion.rcol_ref
  22.7 1.1 bitcast_convert_fusion
  23.8 9.5 %all-to-all-done = f32[32,2,8,256]{3,2,1,0:T(8,128)S(1)} async-done(((f32[32,2,8,256]{3,2,1,0:T(8,128)}), f32[32,2,8,256]{3,2,1,0:T(8,128)S(1)}, u32[]{:S(2)}, u32[]{:S(2)}) %all-to-all-start) | async-done | bytes 524320 | tf_op jit(solution)/shard_map/all_to_all | solution.py:386
  33.3 0.6 gather_fusion.1
  33.9 0.7 reshape.662
  34.6 2.5 %copy.28 = f32[8,4,16,9,16]{2,1,4,3,0:T(4,128)} copy(f32[8,4,16,9,16]{4,2,0,3,1:T(8,128)S(1)} %bitcast.73) | data formatting | bytes 589824 | tf_op jit(solution)/shard_map/transpose | solution.py:134
  37.2 2.5 %reshape.663 = f32[8,64,144]{1,2,0:T(8,128)S(1)} reshape(f32[8,4,16,9,16]{2,1,4,3,0:T(4,128)} %copy.28) | data formatting | bytes 589824 | tf_op jit(solution)/shard_map/reshape | solution.py:134
  39.7 0.9 copy.34.model_ref
  40.6 106.3 %shard_map.91 = f32[8,64,128]{2,1,0:T(8,128)} custom-call(s32[3]{0:T(128)} %pad_add_fusion.1.src_ref, f32[4]{0:T(128)} %bitcast.81, s32[2,256]{1,0:T(2,128)} %pad_add_fusion.rrow_ref, s32[256,1]{1,0:T(8,128)} %add_select_fusion.rcol_ref, f32[256,4]{1,0:T(8,128)} %bitcast.79, f32[8,64,128]{2,1,0:T(8,128)} %copy.34.model_ref, ...), custom_call_target="tpu_custom_call" | custom-call | tf_op jit(solution)/shard_map/pallas_call | solution.py:338
  146.9 1.1 copy.30
  148.1 1.1 dynamic_update_slice.3
  149.2 1.0 reshape.664
  150.3 2.5 %copy.31 = f32[4,9,8,16,16]{4,3,2,1,0:T(8,128)} copy(f32[4,9,8,16,16]{3,0,4,1,2:T(4,128)S(1)} %bitcast.74) | data formatting | bytes 589824 | tf_op jit(solution)/shard_map/transpose | solution.py:143
  152.7 2.5 %reshape.665 = f32[36,8,256]{2,1,0:T(8,128)S(1)} reshape(f32[4,9,8,16,16]{4,3,2,1,0:T(8,128)} %copy.31) | data formatting | bytes 589824 | tf_op jit(solution)/shard_map/reshape | solution.py:143
  155.3 0.6 gather_fusion.2
  155.9 0.9 broadcast_select_fusion
  156.8 11.3 %all-to-all-start.1 = ((f32[32,2,8,256]{3,2,1,0:T(8,128)}), f32[32,2,8,256]{3,2,1,0:T(8,128)S(1)}, u32[]{:S(2)}, u32[]{:S(2)}) async-start(f32[32,2,8,256]{3,2,1,0:T(8,128)} %broadcast_select_fusion), calls=%async_computation.1 | async-start | bytes 1048576 | tf_op jit(solution)/shard_map/all_to_all | solution.py:404
  168.5 16.0 %all-to-all-done.1 = f32[32,2,8,256]{3,2,1,0:T(8,128)S(1)} async-done(((f32[32,2,8,256]{3,2,1,0:T(8,128)}), f32[32,2,8,256]{3,2,1,0:T(8,128)S(1)}, u32[]{:S(2)}, u32[]{:S(2)}) %all-to-all-start.1) | async-done | bytes 524320 | tf_op jit(solution)/shard_map/all_to_all | solution.py:404
  184.5 0.4 fusion
  184.9 0.7 copy.33
  (39 shorter events, 1.7 us)
Async XLA Ops:
  0.0 6.0 %copy-start = (f32[12,8,256]{2,1,0:T(8,128)S(1)}, f32[12,8,256]{2,1,0:T(8,128)}, u32[]{:S(2)}) copy-start(f32[12,8,256]{2,1,0:T(8,128)} %param.9) | copy-start | bytes 294916
  0.0 16.9 %copy-start.5 = (s32[32]{0:T(128)S(1)}, s32[32]{0:T(128)}, u32[]{:S(2)}) copy-start(s32[32]{0:T(128)} %param.16) | copy-start | bytes 388
  0.0 19.5 %copy-start.3 = (s32[1,256]{1,0:T(1,128)S(1)}, s32[1,256]{1,0:T(1,128)}, u32[]{:S(2)}) copy-start(s32[1,256]{1,0:T(1,128)} %param.14) | copy-start | bytes 3076
  0.0 19.6 %copy-start.4 = (f32[1,4,256]{2,1,0:T(4,128)S(1)}, f32[1,4,256]{2,1,0:T(4,128)}, u32[]{:S(2)}) copy-start(f32[1,4,256]{2,1,0:T(4,128)} %param.15) | copy-start | bytes 12292
  0.0 22.7 %copy-start.2 = (bf16[1,2,8,64,128]{4,3,2,1,0:T(8,128)(2,1)S(1)}, bf16[1,2,8,64,128]{4,3,2,1,0:T(8,128)(2,1)}, u32[]{:S(2)}) copy-start(bf16[1,2,8,64,128]{4,3,2,1,0:T(8,128)(2,1)} %param.10) | copy-start | bytes 786436
  0.0 22.7 %copy-start.1 = (bf16[1,2,8,64,128]{4,3,2,1,0:T(8,128)(2,1)S(1)}, bf16[1,2,8,64,128]{4,3,2,1,0:T(8,128)(2,1)}, u32[]{:S(2)}) copy-start(bf16[1,2,8,64,128]{4,3,2,1,0:T(8,128)(2,1)} %param.11) | copy-start | bytes 786436
  7.5 25.8 %all-to-all-start = ((f32[32,2,8,256]{3,2,1,0:T(8,128)}), f32[32,2,8,256]{3,2,1,0:T(8,128)S(1)}, u32[]{:S(2)}, u32[]{:S(2)}) async-start(f32[32,2,8,256]{3,2,1,0:T(8,128)} %broadcast_select_fusion.1), calls=%async_computation | async-start | bytes 1048576 | tf_op jit(solution)/shard_map/all_to_all | solution.py:386
  156.8 27.7 %all-to-all-start.1 = ((f32[32,2,8,256]{3,2,1,0:T(8,128)}), f32[32,2,8,256]{3,2,1,0:T(8,128)S(1)}, u32[]{:S(2)}, u32[]{:S(2)}) async-start(f32[32,2,8,256]{3,2,1,0:T(8,128)} %broadcast_select_fusion), calls=%async_computation.1 | async-start | bytes 1048576 | tf_op jit(solution)/shard_map/all_to_all | solution.py:404

commit v2 on v1

--- a/solution.py
+++ b/solution.py
@@ -231,58 +231,50 @@
 
         lax.fori_loop(0, depth, plane, 0)
 
-    def exchange(r):
-        descs = []
-        for f, buf in enumerate((pad_p, pad_q)):
-            down = pltpu.make_async_remote_copy(
-                src_ref=buf.at[r, RADIUS : 2 * RADIUS],
-                dst_ref=buf.at[r, RADIUS + depth : 2 * RADIUS + depth],
-                send_sem=send_sem.at[r, f, 0],
-                recv_sem=recv_sem.at[r, f, 0],
-                device_id={"sub": down_dev},
-                device_id_type=pl.DeviceIdType.MESH,
-            )
-            up = pltpu.make_async_remote_copy(
-                src_ref=buf.at[r, depth : RADIUS + depth],
-                dst_ref=buf.at[r, 0:RADIUS],
-                send_sem=send_sem.at[r, f, 1],
-                recv_sem=recv_sem.at[r, f, 1],
-                device_id={"sub": up_dev},
-                device_id_type=pl.DeviceIdType.MESH,
-            )
-            descs.append((down, up))
+    def exchange(r, f):
+        buf = (pad_p, pad_q)[f]
+        down = pltpu.make_async_remote_copy(
+            src_ref=buf.at[r, RADIUS : 2 * RADIUS],
+            dst_ref=buf.at[r, RADIUS + depth : 2 * RADIUS + depth],
+            send_sem=send_sem.at[r, f, 0],
+            recv_sem=recv_sem.at[r, f, 0],
+            device_id={"sub": down_dev},
+            device_id_type=pl.DeviceIdType.MESH,
+        )
+        up = pltpu.make_async_remote_copy(
+            src_ref=buf.at[r, depth : RADIUS + depth],
+            dst_ref=buf.at[r, 0:RADIUS],
+            send_sem=send_sem.at[r, f, 1],
+            recv_sem=recv_sem.at[r, f, 1],
+            device_id={"sub": up_dev},
+            device_id_type=pl.DeviceIdType.MESH,
+        )
 
         @pl.when(me > 0)
         def _():
-            for down, up in descs:
-                down.start()
+            down.start()
 
         @pl.when(me < n_sub - 1)
         def _():
-            for down, up in descs:
-                up.start()
-
-        return descs
-
-    def finish(descs):
+            up.start()
+
+        return (down, up)
+
+    def finish(pair):
+        down, up = pair
+
         @pl.when(me > 0)
         def _():
-            for down, up in descs:
-                down.wait_send()
-                up.wait_recv()
+            down.wait_send()
+            up.wait_recv()
 
         @pl.when(me < n_sub - 1)
         def _():
-            for down, up in descs:
-                up.wait_send()
-                down.wait_recv()
-
-    for r in range(NT):
-        descs = exchange(r)
-        build_injection(NT - 1 - r)
-        finish(descs)
-
-        def plane(j, carry, r=r):
+            up.wait_send()
+            down.wait_recv()
+
+    def forward_round(r):
+        def plane(j, carry):
             p = j + RADIUS
             lp = plane_stencil(pad_p, r, p, rows, lanes)
             lap[r, j] = lp
@@ -291,6 +283,13 @@
                 following = 2.0 * pad_p[r, p] - before + model_ref[j] * lp
                 source = jnp.where(src_spot & (src_level == j), wave_ref[r], 0.0)
                 pad_p[r + 1, p] = following + source
+            return carry
+
+        lax.fori_loop(0, depth, plane, 0)
+
+    def adjoint_round(r):
+        def plane(j, carry):
+            p = j + RADIUS
             lq = plane_stencil(pad_q, r, p, rows, lanes)
             now = qa_ref[0, j] if r == 0 else qs[r - 1, j]
             if r == 0:
@@ -301,21 +300,32 @@
                 later = qs[r - 2, j]
             result = 2.0 * now - later + lq
             result = result + inject[j]
-            qs[r, j] = result
             if r < NT - 1:
+                qs[r, j] = result
                 pad_q[r + 1, p] = model_ref[j] * result
+            else:
+                image = jnp.zeros((AX, AY), jnp.float32)
+                for s in range(NT - 1):
+                    image = image + qs[s, j] * lap[NT - 1 - s, j]
+                image = image + result * lap[0, j]
+                img_ref[j] = IMAGE_SCALE * image
             return carry
 
         lax.fori_loop(0, depth, plane, 0)
 
-    def image_plane(j, carry):
-        image = jnp.zeros((AX, AY), jnp.float32)
-        for r in range(NT):
-            image = image + qs[r, j] * lap[NT - 1 - r, j]
-        img_ref[j] = IMAGE_SCALE * image
-        return carry
-
-    lax.fori_loop(0, depth, image_plane, 0)
+    fwd = exchange(0, 0)
+    adj = exchange(0, 1)
+    build_injection(NT - 1)
+    for r in range(NT):
+        finish(fwd)
+        forward_round(r)
+        if r < NT - 1:
+            fwd = exchange(r + 1, 0)
+        finish(adj)
+        adjoint_round(r)
+        if r < NT - 1:
+            adj = exchange(r + 1, 1)
+            build_injection(NT - 2 - r)
 
 
 def migrate(model, state_fwd, state_adj, wave, source, receivers, resid):

time: 186 us -> 177 us (0.952)
  Pallas kernels: 106 us -> 89.2 us
  starting transfers between devices: 20.6 us -> 28.3 us
    pallas_call x1, Pallas kernels: 106 us -> 89.2 us  [migrate(): pl.pallas_call(migrate_kernel, out_shape=jax.ShapeDtypeStruct(model.shape...]
    all_to_all x1, starting transfers between devices: 11.3 us -> 19 us  [body(): lax.all_to_all(images[0], 'shot', split_axis=0, concat_axis=0, tiled=True)]
where the time goes in v2:
time: 177 us; the launch traced here: 176 us
  Pallas kernels  89.2 us (50%)
  starting transfers between devices  28.3 us (16%)
  waiting for transfers between devices  25.5 us (14%)
  local copies, waits for them, and re-layouts  21.4 us (12%)
  other arithmetic  7.83 us (4%)
  between operations  3.62 us (2%)
    pallas_call x1, Pallas kernels, migrate(): pl.pallas_call(migrate_kernel, out_shape=jax.ShapeDtypeStruct(model.shape...  89.2 us
    all_to_all x1, starting transfers between devices, body(): lax.all_to_all(images[0], 'shot', split_axis=0, concat_axis=0, tiled=True)  19 us
    all_to_all x1, waiting for transfers between devices, body(): lax.all_to_all(images[0], 'shot', split_axis=0, concat_axis=0, tiled=True)  16 us
    all_to_all x1, waiting for transfers between devices, body(): lax.all_to_all(sending, 'shot', split_axis=0, concat_axis=0, tiled=True)  9.49 us
    all_to_all x1, starting transfers between devices, body(): lax.all_to_all(sending, 'shot', split_axis=0, concat_axis=0, tiled=True)  9.36 us
  transfers between devices with their start and end apart: 2, of which 2 were waited for; matrix products, arithmetic and copies ran while one was open for 4% of the time, Pallas kernels for 0%

profile of v2, /device:TPU:5, one launch (start us, length us, event | category | flops | bytes accessed | tf_op | source)
XLA Modules:
  0.0 176.3 jit_solution(9597261971604012912)
XLA Ops:
  0.0 1.3 dynamic_slice.9
  4.0 0.7 and_select_fusion.13
  4.9 0.7 fusion.22
  6.0 0.6 gather_fusion
  6.6 0.9 broadcast_select_fusion.1
  7.5 9.4 %all-to-all-start = ((f32[32,2,8,256]{3,2,1,0:T(8,128)}), f32[32,2,8,256]{3,2,1,0:T(8,128)S(1)}, u32[]{:S(2)}, u32[]{:S(2)}) async-start(f32[32,2,8,256]{3,2,1,0:T(8,128)} %broadcast_select_fusion.1), calls=%async_computation | async-start | bytes 1048576 | tf_op jit(solution)/shard_map/all_to_all | solution.py:396
  16.9 0.6 dynamic_slice.10
  18.2 0.6 fusion.11
  18.8 0.6 fusion.13
  19.7 0.8 copy.26
  20.7 0.6 pad_add_fusion.rrow_ref
  21.3 0.7 pad_add_fusion.1.src_ref
  22.0 0.7 add_select_fusion.rcol_ref
  22.7 1.1 bitcast_convert_fusion
  23.8 9.5 %all-to-all-done = f32[32,2,8,256]{3,2,1,0:T(8,128)S(1)} async-done(((f32[32,2,8,256]{3,2,1,0:T(8,128)}), f32[32,2,8,256]{3,2,1,0:T(8,128)S(1)}, u32[]{:S(2)}, u32[]{:S(2)}) %all-to-all-start) | async-done | bytes 524320 | tf_op jit(solution)/shard_map/all_to_all | solution.py:396
  33.3 0.6 gather_fusion.1
  33.9 0.7 reshape.662
  34.6 2.5 %copy.28 = f32[8,4,16,9,16]{2,1,4,3,0:T(4,128)} copy(f32[8,4,16,9,16]{4,2,0,3,1:T(8,128)S(1)} %bitcast.73) | data formatting | bytes 589824 | tf_op jit(solution)/shard_map/transpose | solution.py:134
  37.2 2.5 %reshape.663 = f32[8,64,144]{1,2,0:T(8,128)S(1)} reshape(f32[8,4,16,9,16]{2,1,4,3,0:T(4,128)} %copy.28) | data formatting | bytes 589824 | tf_op jit(solution)/shard_map/reshape | solution.py:134
  39.7 0.9 copy.34.model_ref
  40.6 89.2 %shard_map.91 = f32[8,64,128]{2,1,0:T(8,128)} custom-call(s32[3]{0:T(128)} %pad_add_fusion.1.src_ref, f32[4]{0:T(128)} %bitcast.81, s32[2,256]{1,0:T(2,128)} %pad_add_fusion.rrow_ref, s32[256,1]{1,0:T(8,128)} %add_select_fusion.rcol_ref, f32[256,4]{1,0:T(8,128)} %bitcast.79, f32[8,64,128]{2,1,0:T(8,128)} %copy.34.model_ref, ...), custom_call_target="tpu_custom_call" | custom-call | tf_op jit(solution)/shard_map/pallas_call | solution.py:348
  129.8 1.1 copy.30
  131.0 1.1 dynamic_update_slice.3
  132.2 1.0 reshape.664
  133.2 2.5 %copy.31 = f32[4,9,8,16,16]{4,3,2,1,0:T(8,128)} copy(f32[4,9,8,16,16]{3,0,4,1,2:T(4,128)S(1)} %bitcast.74) | data formatting | bytes 589824 | tf_op jit(solution)/shard_map/transpose | solution.py:143
  135.6 2.5 %reshape.665 = f32[36,8,256]{2,1,0:T(8,128)S(1)} reshape(f32[4,9,8,16,16]{4,3,2,1,0:T(8,128)} %copy.31) | data formatting | bytes 589824 | tf_op jit(solution)/shard_map/reshape | solution.py:143
  138.2 0.6 gather_fusion.2
  138.8 0.9 broadcast_select_fusion
  139.7 19.0 %all-to-all-start.1 = ((f32[32,2,8,256]{3,2,1,0:T(8,128)}), f32[32,2,8,256]{3,2,1,0:T(8,128)S(1)}, u32[]{:S(2)}, u32[]{:S(2)}) async-start(f32[32,2,8,256]{3,2,1,0:T(8,128)} %broadcast_select_fusion), calls=%async_computation.1 | async-start | bytes 1048576 | tf_op jit(solution)/shard_map/all_to_all | solution.py:414
  159.2 16.0 %all-to-all-done.1 = f32[32,2,8,256]{3,2,1,0:T(8,128)S(1)} async-done(((f32[32,2,8,256]{3,2,1,0:T(8,128)}), f32[32,2,8,256]{3,2,1,0:T(8,128)S(1)}, u32[]{:S(2)}, u32[]{:S(2)}) %all-to-all-start.1) | async-done | bytes 524320 | tf_op jit(solution)/shard_map/all_to_all | solution.py:414
  175.1 0.4 fusion
  175.6 0.7 copy.33
  (39 shorter events, 1.7 us)
Async XLA Ops:
  0.0 6.0 %copy-start = (f32[12,8,256]{2,1,0:T(8,128)S(1)}, f32[12,8,256]{2,1,0:T(8,128)}, u32[]{:S(2)}) copy-start(f32[12,8,256]{2,1,0:T(8,128)} %param.9) | copy-start | bytes 294916
  0.0 16.9 %copy-start.5 = (s32[32]{0:T(128)S(1)}, s32[32]{0:T(128)}, u32[]{:S(2)}) copy-start(s32[32]{0:T(128)} %param.16) | copy-start | bytes 388
  0.0 19.5 %copy-start.3 = (s32[1,256]{1,0:T(1,128)S(1)}, s32[1,256]{1,0:T(1,128)}, u32[]{:S(2)}) copy-start(s32[1,256]{1,0:T(1,128)} %param.14) | copy-start | bytes 3076
  0.0 19.6 %copy-start.4 = (f32[1,4,256]{2,1,0:T(4,128)S(1)}, f32[1,4,256]{2,1,0:T(4,128)}, u32[]{:S(2)}) copy-start(f32[1,4,256]{2,1,0:T(4,128)} %param.15) | copy-start | bytes 12292
  0.0 22.7 %copy-start.2 = (bf16[1,2,8,64,128]{4,3,2,1,0:T(8,128)(2,1)S(1)}, bf16[1,2,8,64,128]{4,3,2,1,0:T(8,128)(2,1)}, u32[]{:S(2)}) copy-start(bf16[1,2,8,64,128]{4,3,2,1,0:T(8,128)(2,1)} %param.10) | copy-start | bytes 786436
  0.0 22.7 %copy-start.1 = (bf16[1,2,8,64,128]{4,3,2,1,0:T(8,128)(2,1)S(1)}, bf16[1,2,8,64,128]{4,3,2,1,0:T(8,128)(2,1)}, u32[]{:S(2)}) copy-start(bf16[1,2,8,64,128]{4,3,2,1,0:T(8,128)(2,1)} %param.11) | copy-start | bytes 786436
  7.5 25.8 %all-to-all-start = ((f32[32,2,8,256]{3,2,1,0:T(8,128)}), f32[32,2,8,256]{3,2,1,0:T(8,128)S(1)}, u32[]{:S(2)}, u32[]{:S(2)}) async-start(f32[32,2,8,256]{3,2,1,0:T(8,128)} %broadcast_select_fusion.1), calls=%async_computation | async-start | bytes 1048576 | tf_op jit(solution)/shard_map/all_to_all | solution.py:396
  139.7 35.4 %all-to-all-start.1 = ((f32[32,2,8,256]{3,2,1,0:T(8,128)}), f32[32,2,8,256]{3,2,1,0:T(8,128)S(1)}, u32[]{:S(2)}, u32[]{:S(2)}) async-start(f32[32,2,8,256]{3,2,1,0:T(8,128)} %broadcast_select_fusion), calls=%async_computation.1 | async-start | bytes 1048576 | tf_op jit(solution)/shard_map/all_to_all | solution.py:414

commit v3 on v2

--- a/solution.py
+++ b/solution.py
@@ -101,34 +101,51 @@
     return (local.reshape(-1), usable.reshape(-1))
 
 
+def lane_column():
+    return jnp.arange(TILE * TILE, dtype=jnp.int32) % TILE
+
+
+def merge_slots(pair, spare_ok, offset):
+    lower = spare_ok & (lane_column() < offset)
+    return jnp.where(lower, pair[:, 1], pair[:, 0])
+
+
 def outgoing(velocity_tiles, row_table, col_table, shot_list, groups, own_cols, caps):
     local, usable = owner_slots(row_table, col_table, shot_list, groups, own_cols, caps)
     chosen = velocity_tiles[local]
     chosen = jnp.where(usable[:, None, None], chosen, 0.0)
-    return chosen.reshape(
-        groups, len(shot_list) * caps, velocity_tiles.shape[1], velocity_tiles.shape[2]
-    )
+    chosen = chosen.reshape(groups, caps, velocity_tiles.shape[1], velocity_tiles.shape[2])
+    usable = usable.reshape(groups, caps)
+    offset = (col_table[:groups] % TILE).reshape(groups, 1, 1)
+    merged = merge_slots(chosen, usable[:, 1, None, None], offset)
+    return merged.reshape(groups, 1, velocity_tiles.shape[1], velocity_tiles.shape[2])
 
 
 def accumulate(gradient, returned, row_table, col_table, shot_list, groups, own_cols, caps):
     local, usable = owner_slots(row_table, col_table, shot_list, groups, own_cols, caps)
-    pieces = returned.reshape(local.shape[0], -1)
-    hot = (local[:, None] == jnp.arange(gradient.shape[0], dtype=jnp.int32)[None, :]) & usable[:, None]
+    usable = usable.reshape(groups, caps)
+    offset = (col_table[:groups] % TILE).reshape(groups, 1, 1)
+    lower = lane_column() < offset
+    piece = returned.reshape(groups, gradient.shape[1], gradient.shape[2])
+    spare = usable[:, 1, None, None]
+    first = jnp.where(spare & lower, 0.0, piece)
+    second = jnp.where(spare & lower, piece, 0.0)
+    pieces = jnp.stack([first, second], axis=1).reshape(groups * caps, -1)
+    hot = (local[:, None] == jnp.arange(gradient.shape[0], dtype=jnp.int32)[None, :]) & usable.reshape(-1)[:, None]
     summed = jnp.einsum(
         "st,sf->tf", hot.astype(jnp.float32), pieces, precision=lax.Precision.HIGHEST
     )
     return gradient + summed.reshape(gradient.shape)
 
 
-def assemble(received, slot_base, row_start, col_start, own_cols):
+def assemble(received, row_start, col_start, own_cols):
     depth_cells = received.shape[2]
-    slot_count = received.shape[1]
     rel_row = jnp.arange(AP_ROWS, dtype=jnp.int32)[:, None]
     rel_col = jnp.arange(AP_COLS + 1, dtype=jnp.int32)[None, :]
     source_owner = (row_start + rel_row) % AP_ROWS * own_cols + (
         col_start // TILE + rel_col
     ) % own_cols
-    flat_index = (source_owner * slot_count + slot_base + rel_col // own_cols).reshape(-1)
+    flat_index = source_owner.reshape(-1)
     pieces = received.reshape(-1, depth_cells, TILE * TILE)[flat_index]
     block = pieces.reshape(AP_ROWS, AP_COLS + 1, depth_cells, TILE, TILE)
     block = block.transpose(2, 0, 3, 1, 4).reshape(depth_cells, AX, (AP_COLS + 1) * TILE)
@@ -148,7 +165,9 @@
         row_start, col_start, owners // own_cols, owners % own_cols, own_cols, caps
     )
     position = jnp.clip(block_row * (AP_COLS + 1) + block_col, 0, AP_ROWS * (AP_COLS + 1) - 1)
-    return jnp.where(usable[..., None, None], pieces[position], 0.0)
+    chosen = jnp.where(usable[..., None, None], pieces[position], 0.0)
+    merged = merge_slots(chosen, usable[:, 1, None, None], col_start % TILE)
+    return merged.reshape(groups, 1, depth_cells, TILE * TILE)
 
 
 def shift_rows(c, k, rows):
@@ -386,6 +405,7 @@
     groups = lax.axis_size("shot")
     own_cols = groups // AP_ROWS
     caps = (AP_COLS + own_cols) // own_cols
+    assert own_cols == AP_COLS and caps == 2 and forward_state.shape[0] == 1
     myself = lax.axis_index("shot")
     shots_here = forward_state.shape[0]
     gradient = jnp.zeros(velocity_tiles.shape, jnp.float32)
@@ -396,11 +416,10 @@
     fetched = lax.all_to_all(sending, "shot", split_axis=0, concat_axis=0, tiled=True)
     images = []
     for k in every_shot:
-        slot_base = k * caps
         shot_id = myself * SHOTS_DEV + k
         row_start = aperture_row[shot_id]
         col_start = aperture_col[shot_id]
-        model = assemble(fetched, slot_base, row_start, col_start, own_cols)
+        model = assemble(fetched, row_start, col_start, own_cols)
         image = migrate(
             model,
             forward_state[k],

time: 177 us -> 166 us (0.938)
  starting transfers between devices: 28.3 us -> 15.7 us
  Pallas kernels: 89.2 us -> 101 us
  waiting for transfers between devices: 25.5 us -> 14.4 us
    all_to_all x1, starting transfers between devices: 19 us -> 6.3 us  [body(): lax.all_to_all(images[0], 'shot', split_axis=0, concat_axis=0, tiled=True)]
    pallas_call x1, Pallas kernels: 89.2 us -> 101 us  [migrate(): pl.pallas_call(migrate_kernel, out_shape=jax.ShapeDtypeStruct(model.shape...]
    all_to_all x1, waiting for transfers between devices: 9.49 us -> 3.69 us  [body(): lax.all_to_all(sending, 'shot', split_axis=0, concat_axis=0, tiled=True)]
    all_to_all x1, waiting for transfers between devices: 16 us -> 10.7 us  [body(): lax.all_to_all(images[0], 'shot', split_axis=0, concat_axis=0, tiled=True)]
where the time goes in v3:
time: 166 us; the launch traced here: 165 us
  Pallas kernels  101 us (61%)
  local copies, waits for them, and re-layouts  21.5 us (13%)
  starting transfers between devices  15.7 us (9%)
  waiting for transfers between devices  14.4 us (9%)
  other arithmetic  8.21 us (5%)
  between operations  3.75 us (2%)
    pallas_call x1, Pallas kernels, migrate(): pl.pallas_call(migrate_kernel, out_shape=jax.ShapeDtypeStruct(model.shape...  101 us
    all_to_all x1, waiting for transfers between devices, body(): lax.all_to_all(images[0], 'shot', split_axis=0, concat_axis=0, tiled=True)  10.7 us
    all_to_all x1, starting transfers between devices, body(): lax.all_to_all(sending, 'shot', split_axis=0, concat_axis=0, tiled=True)  9.36 us
    all_to_all x1, starting transfers between devices, body(): lax.all_to_all(images[0], 'shot', split_axis=0, concat_axis=0, tiled=True)  6.3 us
    all_to_all x1, waiting for transfers between devices, body(): lax.all_to_all(sending, 'shot', split_axis=0, concat_axis=0, tiled=True)  3.69 us
  transfers between devices with their start and end apart: 2, of which 2 were waited for; matrix products, arithmetic and copies ran while one was open for 4% of the time, Pallas kernels for 0%

profile of v3, /device:TPU:5, one launch (start us, length us, event | category | flops | bytes accessed | tf_op | source)
XLA Modules:
  0.0 165.3 jit_solution(597093611502335313)
XLA Ops:
  0.1 1.3 dynamic_slice.9
  3.4 0.7 and_select_fusion.14
  4.3 0.7 fusion.22
  6.0 0.6 gather_fusion
  6.9 0.7 slice_select_fusion.1
  7.6 9.4 %all-to-all-start = ((f32[32,1,8,256]{3,2,1,0:T(8,128)}), f32[32,1,8,256]{3,2,1,0:T(8,128)S(1)}, u32[]{:S(2)}, u32[]{:S(2)}) async-start(f32[32,1,8,256]{3,2,1,0:T(8,128)} %slice_select_fusion.1), calls=%async_computation | async-start | bytes 524288 | tf_op jit(solution)/shard_map/all_to_all | solution.py:416
  17.0 0.7 dynamic_slice.10
  18.4 0.7 fusion.11
  19.1 0.7 fusion.13
  20.3 0.6 pad_add_fusion.rrow_ref
  21.0 0.6 pad_add_fusion.1.src_ref
  21.8 0.8 copy.18
  22.6 0.7 add_select_fusion.rcol_ref
  23.3 1.1 bitcast_convert_fusion
  24.4 3.7 %all-to-all-done = f32[32,1,8,256]{3,2,1,0:T(8,128)S(1)} async-done(((f32[32,1,8,256]{3,2,1,0:T(8,128)}), f32[32,1,8,256]{3,2,1,0:T(8,128)S(1)}, u32[]{:S(2)}, u32[]{:S(2)}) %all-to-all-start) | async-done | bytes 262176 | tf_op jit(solution)/shard_map/all_to_all | solution.py:416
  28.1 0.6 gather_fusion.1
  28.7 0.7 reshape.707
  29.4 2.5 %copy.20 = f32[8,4,16,9,16]{2,1,4,3,0:T(4,128)} copy(f32[8,4,16,9,16]{4,2,0,3,1:T(8,128)S(1)} %bitcast.77) | data formatting | bytes 589824 | tf_op jit(solution)/shard_map/transpose | solution.py:151
  31.9 2.5 %reshape.708 = f32[8,64,144]{1,2,0:T(8,128)S(1)} reshape(f32[8,4,16,9,16]{2,1,4,3,0:T(4,128)} %copy.20) | data formatting | bytes 589824 | tf_op jit(solution)/shard_map/reshape | solution.py:151
  34.5 0.9 copy.26.model_ref
  35.4 101.4 %shard_map.91 = f32[8,64,128]{2,1,0:T(8,128)} custom-call(s32[3]{0:T(128)} %pad_add_fusion.1.src_ref, f32[4]{0:T(128)} %bitcast.85, s32[2,256]{1,0:T(2,128)} %pad_add_fusion.rrow_ref, s32[256,1]{1,0:T(8,128)} %add_select_fusion.rcol_ref, f32[256,4]{1,0:T(8,128)} %bitcast.83, f32[8,64,128]{2,1,0:T(8,128)} %copy.26.model_ref, ...), custom_call_target="tpu_custom_call" | custom-call | tf_op jit(solution)/shard_map/pallas_call | solution.py:367
  136.8 1.1 copy.22
  138.0 1.1 dynamic_update_slice.3
  139.1 1.0 reshape.709
  140.1 2.5 %copy.23 = f32[4,9,8,16,16]{4,3,2,1,0:T(8,128)} copy(f32[4,9,8,16,16]{3,0,4,1,2:T(4,128)S(1)} %bitcast.78) | data formatting | bytes 589824 | tf_op jit(solution)/shard_map/transpose | solution.py:160
  142.6 2.5 %reshape.710 = f32[36,8,256]{2,1,0:T(8,128)S(1)} reshape(f32[4,9,8,16,16]{4,3,2,1,0:T(8,128)} %copy.23) | data formatting | bytes 589824 | tf_op jit(solution)/shard_map/reshape | solution.py:160
  145.1 0.6 gather_fusion.2
  145.9 0.7 slice_select_fusion
  146.6 6.3 %all-to-all-start.1 = ((f32[32,1,8,256]{3,2,1,0:T(8,128)}), f32[32,1,8,256]{3,2,1,0:T(8,128)S(1)}, u32[]{:S(2)}, u32[]{:S(2)}) async-start(f32[32,1,8,256]{3,2,1,0:T(8,128)} %slice_select_fusion), calls=%async_computation.1 | async-start | bytes 524288 | tf_op jit(solution)/shard_map/all_to_all | solution.py:433
  153.4 10.7 %all-to-all-done.1 = f32[32,1,8,256]{3,2,1,0:T(8,128)S(1)} async-done(((f32[32,1,8,256]{3,2,1,0:T(8,128)}), f32[32,1,8,256]{3,2,1,0:T(8,128)S(1)}, u32[]{:S(2)}, u32[]{:S(2)}) %all-to-all-start.1) | async-done | bytes 262176 | tf_op jit(solution)/shard_map/all_to_all | solution.py:433
  164.1 0.4 fusion
  164.6 0.7 copy.25
  (49 shorter events, 2.3 us)
Async XLA Ops:
  0.0 6.0 %copy-start = (f32[12,8,256]{2,1,0:T(8,128)S(1)}, f32[12,8,256]{2,1,0:T(8,128)}, u32[]{:S(2)}) copy-start(f32[12,8,256]{2,1,0:T(8,128)} %param.9) | copy-start | bytes 294916
  0.0 17.0 %copy-start.5 = (s32[32]{0:T(128)S(1)}, s32[32]{0:T(128)}, u32[]{:S(2)}) copy-start(s32[32]{0:T(128)} %param.16) | copy-start | bytes 388
  0.0 20.0 %copy-start.3 = (s32[1,256]{1,0:T(1,128)S(1)}, s32[1,256]{1,0:T(1,128)}, u32[]{:S(2)}) copy-start(s32[1,256]{1,0:T(1,128)} %param.14) | copy-start | bytes 3076
  0.0 21.8 %copy-start.4 = (f32[1,4,256]{2,1,0:T(4,128)S(1)}, f32[1,4,256]{2,1,0:T(4,128)}, u32[]{:S(2)}) copy-start(f32[1,4,256]{2,1,0:T(4,128)} %param.15) | copy-start | bytes 12292
  0.0 23.3 %copy-start.2 = (bf16[1,2,8,64,128]{4,3,2,1,0:T(8,128)(2,1)S(1)}, bf16[1,2,8,64,128]{4,3,2,1,0:T(8,128)(2,1)}, u32[]{:S(2)}) copy-start(bf16[1,2,8,64,128]{4,3,2,1,0:T(8,128)(2,1)} %param.10) | copy-start | bytes 786436
  0.0 23.3 %copy-start.1 = (bf16[1,2,8,64,128]{4,3,2,1,0:T(8,128)(2,1)S(1)}, bf16[1,2,8,64,128]{4,3,2,1,0:T(8,128)(2,1)}, u32[]{:S(2)}) copy-start(bf16[1,2,8,64,128]{4,3,2,1,0:T(8,128)(2,1)} %param.11) | copy-start | bytes 786436
  7.6 20.5 %all-to-all-start = ((f32[32,1,8,256]{3,2,1,0:T(8,128)}), f32[32,1,8,256]{3,2,1,0:T(8,128)S(1)}, u32[]{:S(2)}, u32[]{:S(2)}) async-start(f32[32,1,8,256]{3,2,1,0:T(8,128)} %slice_select_fusion.1), calls=%async_computation | async-start | bytes 524288 | tf_op jit(solution)/shard_map/all_to_all | solution.py:416
  146.6 17.4 %all-to-all-start.1 = ((f32[32,1,8,256]{3,2,1,0:T(8,128)}), f32[32,1,8,256]{3,2,1,0:T(8,128)S(1)}, u32[]{:S(2)}, u32[]{:S(2)}) async-start(f32[32,1,8,256]{3,2,1,0:T(8,128)} %slice_select_fusion), calls=%async_computation.1 | async-start | bytes 524288 | tf_op jit(solution)/shard_map/all_to_all | solution.py:433

commit v4 on v3

--- a/solution.py
+++ b/solution.py
@@ -170,6 +170,30 @@
     return merged.reshape(groups, 1, depth_cells, TILE * TILE)
 
 
+X_CHIPS = 4
+GROUP_ROW = 8
+
+
+def crossing(group):
+    return (group // GROUP_ROW * 2 + group % 2) % X_CHIPS
+
+
+def block_of(group, sub):
+    cross = crossing(group)
+    x, half = sub // 2, sub % 2
+    low = (x - cross + 2 * X_CHIPS - 1) % X_CHIPS
+    high = X_CHIPS + (cross - x + X_CHIPS) % X_CHIPS
+    return (1 - half) * low + half * high
+
+
+def device_of(group, block):
+    cross = crossing(group)
+    half = block // X_CHIPS
+    low = (cross + 1 + block) % X_CHIPS
+    high = (cross - block + 2 * X_CHIPS) % X_CHIPS
+    return ((1 - half) * low + half * high) * 2 + half
+
+
 def shift_rows(c, k, rows):
     if k > 0:
         moved = pltpu.roll(c, AX - k, 0)
@@ -211,7 +235,8 @@
     src_ref, wave_ref, rrow_ref, rcol_ref, resid_ref, model_ref, pf_ref, qa_ref,
     img_ref, pad_p, pad_q, lap, qs, inject, send_sem, recv_sem,
 ):
-    me = lax.axis_index("sub")
+    group = lax.axis_index("shot")
+    me = block_of(group, lax.axis_index("sub"))
     n_sub = lax.axis_size("sub")
     depth = model_ref.shape[0]
     halo = jnp.zeros((RADIUS, AX, AY), jnp.float32)
@@ -221,8 +246,8 @@
             buf[r, RADIUS + depth : 2 * RADIUS + depth] = halo
     pad_p[0, RADIUS : RADIUS + depth] = pf_ref[0]
     pad_q[0, RADIUS : RADIUS + depth] = model_ref[...] * qa_ref[0]
-    up_dev = lax.rem(me + 1, n_sub)
-    down_dev = lax.rem(me + n_sub - 1, n_sub)
+    up_dev = device_of(group, (me + 1) % n_sub)
+    down_dev = device_of(group, (me + n_sub - 1) % n_sub)
     barrier = pltpu.get_barrier_semaphore()
     pl.semaphore_signal(barrier, 1, device_id={"sub": up_dev}, device_id_type=pl.DeviceIdType.MESH)
     pl.semaphore_signal(barrier, 1, device_id={"sub": down_dev}, device_id_type=pl.DeviceIdType.MESH)
@@ -350,7 +375,7 @@
 def migrate(model, state_fwd, state_adj, wave, source, receivers, resid):
     depth_cells = model.shape[0]
     plane = AX * AY
-    offset = lax.axis_index("sub") * depth_cells
+    offset = block_of(lax.axis_index("shot"), lax.axis_index("sub")) * depth_cells
 
     def level_of(cells):
         level = cells // plane - offset
@@ -406,6 +431,11 @@
     own_cols = groups // AP_ROWS
     caps = (AP_COLS + own_cols) // own_cols
     assert own_cols == AP_COLS and caps == 2 and forward_state.shape[0] == 1
+    n_sub = lax.axis_size("sub")
+    assert n_sub == 2 * X_CHIPS and groups % GROUP_ROW == 0
+    outbound = [
+        (g * n_sub + b, g * n_sub + device_of(g, b)) for g in range(groups) for b in range(n_sub)
+    ]
     myself = lax.axis_index("shot")
     shots_here = forward_state.shape[0]
     gradient = jnp.zeros(velocity_tiles.shape, jnp.float32)
@@ -420,15 +450,24 @@
         row_start = aperture_row[shot_id]
         col_start = aperture_col[shot_id]
         model = assemble(fetched, row_start, col_start, own_cols)
+        moving = jnp.concatenate(
+            [
+                model[None],
+                forward_state[k].astype(jnp.float32),
+                adjoint_state[k].astype(jnp.float32),
+            ]
+        )
+        moving = lax.ppermute(moving, ("shot", "sub"), outbound)
         image = migrate(
-            model,
-            forward_state[k],
-            adjoint_state[k],
+            moving[0],
+            moving[1:3],
+            moving[3:5],
             wavelet[k],
             source_cell[k],
             receiver_cell[k],
             residual[k],
         )
+        image = lax.ppermute(image, ("shot", "sub"), [(b, a) for a, b in outbound])
         images.append(disperse(image, row_start, col_start, groups, own_cols, caps))
     returned = lax.all_to_all(images[0], "shot", split_axis=0, concat_axis=0, tiled=True)
     gradient = accumulate(

time: 166 us -> 190 us (1.14)
  Pallas kernels: 101 us -> 29.3 us
  waiting for transfers between devices: 14.4 us -> 70.7 us
  starting transfers between devices: 15.7 us -> 52.9 us
  local copies, waits for them, and re-layouts: 21.5 us -> 24.2 us
    pallas_call x1, Pallas kernels: 101 us -> 29.3 us  [migrate(): pl.pallas_call(migrate_kernel, out_shape=jax.ShapeDtypeStruct(model.shape...]
    ppermute x0 -> x2, waiting for transfers between devices: none -> 50.5 us  [the longest x1 36.7 us: body(): moving = lax.ppermute(moving, ('shot', 'sub'), outbound)]
    all_to_all x1, starting transfers between devices: 6.3 us -> 30.8 us  [body(): lax.all_to_all(images[0], 'shot', split_axis=0, concat_axis=0, tiled=True)]
    ppermute x0 -> x2, starting transfers between devices: none -> 12.7 us  [the longest x1 6.64 us: body(): image = lax.ppermute(image, ('shot', 'sub'), [(b, a) for a, b in outbound])]
    all_to_all x1, waiting for transfers between devices: 3.69 us -> 9.59 us  [body(): lax.all_to_all(sending, 'shot', split_axis=0, concat_axis=0, tiled=True)]
  transfers between devices with their start and end apart: 2 -> 4, of which waited for: 2 -> 4; matrix products, arithmetic and copies ran while one was open for 4% -> 3% of each run, Pallas kernels for 0% -> 0%
where the time goes in v4:
time: 190 us
  waiting for transfers between devices  70.7 us (37%)
  starting transfers between devices  52.9 us (28%)
  Pallas kernels  29.3 us (15%)
  local copies, waits for them, and re-layouts  24.2 us (13%)
  other arithmetic  8.19 us (4%)
  between operations  3.84 us (2%)
    ppermute x1, waiting for transfers between devices, body(): moving = lax.ppermute(moving, ('shot', 'sub'), outbound)  36.7 us
    all_to_all x1, starting transfers between devices, body(): lax.all_to_all(images[0], 'shot', split_axis=0, concat_axis=0, tiled=True)  30.8 us
    pallas_call x1, Pallas kernels, migrate(): pl.pallas_call(migrate_kernel, out_shape=jax.ShapeDtypeStruct(model.shape...  29.3 us
    ppermute x1, waiting for transfers between devices, body(): image = lax.ppermute(image, ('shot', 'sub'), [(b, a) for a, b in outbound])  13.8 us
    all_to_all x1, waiting for transfers between devices, body(): lax.all_to_all(images[0], 'shot', split_axis=0, concat_axis=0, tiled=True)  10.7 us
    all_to_all x1, waiting for transfers between devices, body(): lax.all_to_all(sending, 'shot', split_axis=0, concat_axis=0, tiled=True)  9.59 us
    all_to_all x1, starting transfers between devices, body(): lax.all_to_all(sending, 'shot', split_axis=0, concat_axis=0, tiled=True)  9.36 us
    ppermute x1, starting transfers between devices, body(): image = lax.ppermute(image, ('shot', 'sub'), [(b, a) for a, b in outbound])  6.64 us
  transfers between devices with their start and end apart: 4, of which 4 were waited for; matrix products, arithmetic and copies ran while one was open for 3% of the time, Pallas kernels for 0%

profile of v4, /device:TPU:5, one launch (start us, length us, event | category | flops | bytes accessed | tf_op | source)
XLA Modules:
  0.0 189.6 jit_solution(2702839370491183651)
XLA Ops:
  0.0 1.3 dynamic_slice.9
  3.2 0.7 and_select_fusion.14
  4.1 0.7 fusion.22
  6.9 0.6 gather_fusion
  7.8 0.7 slice_select_fusion.1
  8.5 9.4 %all-to-all-start = ((f32[32,1,8,256]{3,2,1,0:T(8,128)}), f32[32,1,8,256]{3,2,1,0:T(8,128)S(1)}, u32[]{:S(2)}, u32[]{:S(2)}) async-start(f32[32,1,8,256]{3,2,1,0:T(8,128)} %slice_select_fusion.1), calls=%async_computation | async-start | bytes 524288 | tf_op jit(solution)/shard_map/all_to_all | solution.py:446
  17.9 0.6 dynamic_slice.10
  19.4 9.6 %all-to-all-done = f32[32,1,8,256]{3,2,1,0:T(8,128)S(1)} async-done(((f32[32,1,8,256]{3,2,1,0:T(8,128)}), f32[32,1,8,256]{3,2,1,0:T(8,128)S(1)}, u32[]{:S(2)}, u32[]{:S(2)}) %all-to-all-start) | async-done | bytes 262176 | tf_op jit(solution)/shard_map/all_to_all | solution.py:446
  29.0 1.3 gather_fusion.1
  30.3 1.7 reshape.707
  32.0 2.5 %copy.32 = f32[8,4,16,9,16]{2,1,4,3,0:T(4,128)} copy(f32[8,4,16,9,16]{4,2,0,3,1:T(8,128)S(1)} %bitcast.80) | data formatting | bytes 589824 | tf_op jit(solution)/shard_map/transpose | solution.py:151
  34.5 2.5 %reshape.708 = f32[8,64,144]{1,2,0:T(8,128)S(1)} reshape(f32[8,4,16,9,16]{2,1,4,3,0:T(4,128)} %copy.32) | data formatting | bytes 589824 | tf_op jit(solution)/shard_map/reshape | solution.py:151
  37.3 1.2 pad_maximum_fusion
  38.5 6.1 %collective-permute-start = (f32[5,8,64,128]{3,2,1,0:T(8,128)}, f32[5,8,64,128]{3,2,1,0:T(8,128)S(1)}, u32[]{:S(2)}, u32[]{:S(2)}) collective-permute-start(f32[5,8,64,128]{3,2,1,0:T(8,128)} %pad_maximum_fusion), channel_id=1, source_target_pairs={{0,2},{1,4},{2,6},{3,0},{4,1},{5,7},{6,5},{7,3},{8,12},{9,14},{10,... | collective-permute-start | bytes 3932168 | tf_op jit(solution)/shard_map/ppermute | solution.py:460
  45.5 0.8 copy.30
  47.1 0.7 pad_add_fusion.1.src_ref
  48.4 0.7 add_select_fusion.rcol_ref
  49.1 36.7 %collective-permute-done = f32[5,8,64,128]{3,2,1,0:T(8,128)S(1)} collective-permute-done((f32[5,8,64,128]{3,2,1,0:T(8,128)}, f32[5,8,64,128]{3,2,1,0:T(8,128)S(1)}, u32[]{:S(2)}, u32[]{:S(2)}) %collective-permute-start) | collective-permute-done | bytes 1310752 | tf_op jit(solution)/shard_map/ppermute | solution.py:460
  85.8 1.1 fusion.23
  86.8 0.7 slice_bitcast_fusion.model_ref
  87.5 29.3 %shard_map.91 = f32[8,64,128]{2,1,0:T(8,128)} custom-call(s32[3]{0:T(128)} %pad_add_fusion.1.src_ref, f32[4]{0:T(128)} %bitcast.89, s32[2,256]{1,0:T(2,128)} %pad_add_fusion.rrow_ref, s32[256,1]{1,0:T(8,128)} %add_select_fusion.rcol_ref, f32[256,4]{1,0:T(8,128)} %bitcast.87, f32[8,64,128]{2,1,0:T(8,128)} %slice_bitcast_fusion.model_ref, ...), custom_call_target="tpu_custom_call" | custom-call | tf_op jit(solution)/shard_map/pallas_call | solution.py:392
  116.9 6.6 %collective-permute-start.1 = (f32[8,64,128]{2,1,0:T(8,128)}, f32[8,64,128]{2,1,0:T(8,128)S(1)}, u32[]{:S(2)}, u32[]{:S(2)}) collective-permute-start(f32[8,64,128]{2,1,0:T(8,128)} %shard_map.91), channel_id=1, source_target_pairs={{2,0},{4,1},{6,2},{0,3},{1,4},{7,5},{5,6},{3,7},{12,8},{14,9},{8,1... | collective-permute-start | bytes 786440 | tf_op jit(solution)/shard_map/ppermute | solution.py:470
  123.7 13.8 %collective-permute-done.1 = f32[8,64,128]{2,1,0:T(8,128)S(1)} collective-permute-done((f32[8,64,128]{2,1,0:T(8,128)}, f32[8,64,128]{2,1,0:T(8,128)S(1)}, u32[]{:S(2)}, u32[]{:S(2)}) %collective-permute-start.1) | collective-permute-done | bytes 262176 | tf_op jit(solution)/shard_map/ppermute | solution.py:470
  137.7 1.1 dynamic_update_slice.3
  138.9 1.0 reshape.709
  139.9 2.5 %copy.35 = f32[4,9,8,16,16]{4,3,2,1,0:T(8,128)} copy(f32[4,9,8,16,16]{3,0,4,1,2:T(4,128)S(1)} %bitcast.81) | data formatting | bytes 589824 | tf_op jit(solution)/shard_map/transpose | solution.py:160
  142.4 2.5 %reshape.710 = f32[36,8,256]{2,1,0:T(8,128)S(1)} reshape(f32[4,9,8,16,16]{4,3,2,1,0:T(8,128)} %copy.35) | data formatting | bytes 589824 | tf_op jit(solution)/shard_map/reshape | solution.py:160
  144.9 0.6 gather_fusion.2
  145.7 0.7 slice_select_fusion
  146.4 30.8 %all-to-all-start.1 = ((f32[32,1,8,256]{3,2,1,0:T(8,128)}), f32[32,1,8,256]{3,2,1,0:T(8,128)S(1)}, u32[]{:S(2)}, u32[]{:S(2)}) async-start(f32[32,1,8,256]{3,2,1,0:T(8,128)} %slice_select_fusion), calls=%async_computation.1 | async-start | bytes 524288 | tf_op jit(solution)/shard_map/all_to_all | solution.py:472
  177.7 10.7 %all-to-all-done.1 = f32[32,1,8,256]{3,2,1,0:T(8,128)S(1)} async-done(((f32[32,1,8,256]{3,2,1,0:T(8,128)}), f32[32,1,8,256]{3,2,1,0:T(8,128)S(1)}, u32[]{:S(2)}, u32[]{:S(2)}) %all-to-all-start.1) | async-done | bytes 262176 | tf_op jit(solution)/shard_map/all_to_all | solution.py:472
  188.9 0.7 copy.37
  (66 shorter events, 5.9 us)
Async XLA Ops:
  0.0 6.9 %copy-start = (f32[12,8,256]{2,1,0:T(8,128)S(1)}, f32[12,8,256]{2,1,0:T(8,128)}, u32[]{:S(2)}) copy-start(f32[12,8,256]{2,1,0:T(8,128)} %param.9) | copy-start | bytes 294916
  5.7 0.6 copy-start.7
  5.8 1.9 %copy-start.3 = (pred[32,2]{0,1:T(4,128)(4,1)}, pred[32,2]{0,1:T(4,128)(4,1)S(1)}, u32[]{:S(2)}) copy-start(pred[32,2]{0,1:T(4,128)(4,1)S(1)} %get-tuple-element.13) | copy-start | bytes 196
  7.5 10.4 %copy-start.10 = (s32[32]{0:T(128)S(1)}, s32[32]{0:T(128)}, u32[]{:S(2)}) copy-start(s32[32]{0:T(128)} %param.16) | copy-start | bytes 388
  7.5 11.7 %copy-start.1 = (bf16[1,2,8,64,128]{4,3,2,1,0:T(8,128)(2,1)S(1)}, bf16[1,2,8,64,128]{4,3,2,1,0:T(8,128)(2,1)}, u32[]{:S(2)}) copy-start(bf16[1,2,8,64,128]{4,3,2,1,0:T(8,128)(2,1)} %param.11) | copy-start | bytes 786436
  7.5 11.7 %copy-start.2 = (bf16[1,2,8,64,128]{4,3,2,1,0:T(8,128)(2,1)S(1)}, bf16[1,2,8,64,128]{4,3,2,1,0:T(8,128)(2,1)}, u32[]{:S(2)}) copy-start(bf16[1,2,8,64,128]{4,3,2,1,0:T(8,128)(2,1)} %param.10) | copy-start | bytes 786436
  8.5 20.5 %all-to-all-start = ((f32[32,1,8,256]{3,2,1,0:T(8,128)}), f32[32,1,8,256]{3,2,1,0:T(8,128)S(1)}, u32[]{:S(2)}, u32[]{:S(2)}) async-start(f32[32,1,8,256]{3,2,1,0:T(8,128)} %slice_select_fusion.1), calls=%async_computation | async-start | bytes 524288 | tf_op jit(solution)/shard_map/all_to_all | solution.py:446
  37.3 8.1 %copy-start.5 = (s32[1,256]{1,0:T(1,128)S(1)}, s32[1,256]{1,0:T(1,128)}, u32[]{:S(2)}) copy-start(s32[1,256]{1,0:T(1,128)} %param.14) | copy-start | bytes 3076
  37.3 8.2 %copy-start.6 = (f32[1,4,256]{2,1,0:T(4,128)S(1)}, f32[1,4,256]{2,1,0:T(4,128)}, u32[]{:S(2)}) copy-start(f32[1,4,256]{2,1,0:T(4,128)} %param.15) | copy-start | bytes 12292
  37.3 9.6 %copy-start.8 = (s32[32]{0:T(128)S(1)}, s32[32]{0:T(128)}, u32[]{:S(2)}) copy-start(s32[32]{0:T(128)} %copy-done.7) | copy-start | bytes 388
  38.5 47.3 %collective-permute-start = (f32[5,8,64,128]{3,2,1,0:T(8,128)}, f32[5,8,64,128]{3,2,1,0:T(8,128)S(1)}, u32[]{:S(2)}, u32[]{:S(2)}) collective-permute-start(f32[5,8,64,128]{3,2,1,0:T(8,128)} %pad_maximum_fusion), channel_id=1, source_target_pairs={{0,2},{1,4},{2,6},{3,0},{4,1},{5,7},{6,5},{7,3},{8,12},{9,14},{10,... | collective-permute-start | bytes 3932168 | tf_op jit(solution)/shard_map/ppermute | solution.py:460
  86.8 36.7 %copy-start.4 = (pred[32,2]{0,1:T(4,128)(4,1)S(1)}, pred[32,2]{0,1:T(4,128)(4,1)}, u32[]{:S(2)}) copy-start(pred[32,2]{0,1:T(4,128)(4,1)} %copy-done.3) | copy-start | bytes 196
  86.8 36.8 %copy-start.9 = (pred[32]{0:T(512)(128)(4,1)S(1)}, pred[32]{0:T(512)(128)(4,1)}, u32[]{:S(2)}) copy-start(pred[32]{0:T(512)(128)(4,1)} %get-tuple-element.16) | copy-start | bytes 100
  116.9 20.6 %collective-permute-start.1 = (f32[8,64,128]{2,1,0:T(8,128)}, f32[8,64,128]{2,1,0:T(8,128)S(1)}, u32[]{:S(2)}, u32[]{:S(2)}) collective-permute-start(f32[8,64,128]{2,1,0:T(8,128)} %shard_map.91), channel_id=1, source_target_pairs={{2,0},{4,1},{6,2},{0,3},{1,4},{7,5},{5,6},{3,7},{12,8},{14,9},{8,1... | collective-permute-start | bytes 786440 | tf_op jit(solution)/shard_map/ppermute | solution.py:470
  146.4 41.9 %all-to-all-start.1 = ((f32[32,1,8,256]{3,2,1,0:T(8,128)}), f32[32,1,8,256]{3,2,1,0:T(8,128)S(1)}, u32[]{:S(2)}, u32[]{:S(2)}) async-start(f32[32,1,8,256]{3,2,1,0:T(8,128)} %slice_select_fusion), calls=%async_computation.1 | async-start | bytes 524288 | tf_op jit(solution)/shard_map/all_to_all | solution.py:472

commit v5 on v4

--- a/solution.py
+++ b/solution.py
@@ -440,6 +440,12 @@
     shots_here = forward_state.shape[0]
     gradient = jnp.zeros(velocity_tiles.shape, jnp.float32)
     every_shot = list(range(shots_here))
+    states_moved = []
+    for k in range(shots_here):
+        states = jnp.concatenate(
+            [forward_state[k].astype(jnp.float32), adjoint_state[k].astype(jnp.float32)]
+        )
+        states_moved.append(lax.ppermute(states, ("shot", "sub"), outbound))
     sending = outgoing(
         velocity_tiles, aperture_row, aperture_col, every_shot, groups, own_cols, caps
     )
@@ -450,18 +456,12 @@
         row_start = aperture_row[shot_id]
         col_start = aperture_col[shot_id]
         model = assemble(fetched, row_start, col_start, own_cols)
-        moving = jnp.concatenate(
-            [
-                model[None],
-                forward_state[k].astype(jnp.float32),
-                adjoint_state[k].astype(jnp.float32),
-            ]
-        )
-        moving = lax.ppermute(moving, ("shot", "sub"), outbound)
+        model = lax.ppermute(model, ("shot", "sub"), outbound)
+        states = states_moved[k]
         image = migrate(
-            moving[0],
-            moving[1:3],
-            moving[3:5],
+            model,
+            states[0:2],
+            states[2:4],
             wavelet[k],
             source_cell[k],
             receiver_cell[k],

time: 190 us -> 172 us (0.905)
  waiting for transfers between devices: 70.7 us -> 43.3 us
  starting transfers between devices: 52.9 us -> 63.7 us
    ppermute x1 -> x2, waiting for transfers between devices: 36.7 us -> 22.3 us  [the longest x1 19.9 us: body(): states_moved.append(lax.ppermute(states, ('shot', 'sub'), outbound))]
    all_to_all x1, waiting for transfers between devices: 9.59 us -> 0.01 us  [body(): lax.all_to_all(sending, 'shot', split_axis=0, concat_axis=0, tiled=True)]
    all_to_all x1, starting transfers between devices: 30.8 us -> 37.5 us  [body(): lax.all_to_all(images[0], 'shot', split_axis=0, concat_axis=0, tiled=True)]
    ppermute x1 -> x2, starting transfers between devices: 6.08 us -> 10.2 us  [the longest x1 6.08 us: body(): states_moved.append(lax.ppermute(states, ('shot', 'sub'), outbound))]
    ppermute x1, waiting for transfers between devices: 13.8 us -> 10.3 us  [body(): image = lax.ppermute(image, ('shot', 'sub'), [(b, a) for a, b in outbound])]
  transfers between devices with their start and end apart: 4 -> 5, of which waited for: 4 -> 4; matrix products, arithmetic and copies ran while one was open for 3% -> 9% of each run, Pallas kernels for 0% -> 0%
where the time goes in v5:
time: 172 us; the launch traced here: 171 us
  starting transfers between devices  63.7 us (37%)
  waiting for transfers between devices  43.3 us (25%)
  Pallas kernels  29.3 us (17%)
  local copies, waits for them, and re-layouts  22.8 us (13%)
  other arithmetic  8.11 us (5%)
  between operations  3.75 us (2%)
    all_to_all x1, starting transfers between devices, body(): lax.all_to_all(images[0], 'shot', split_axis=0, concat_axis=0, tiled=True)  37.5 us
    pallas_call x1, Pallas kernels, migrate(): pl.pallas_call(migrate_kernel, out_shape=jax.ShapeDtypeStruct(model.shape...  29.3 us
    ppermute x1, waiting for transfers between devices, body(): states_moved.append(lax.ppermute(states, ('shot', 'sub'), outbound))  19.9 us
    all_to_all x1, waiting for transfers between devices, body(): lax.all_to_all(images[0], 'shot', split_axis=0, concat_axis=0, tiled=True)  10.7 us
    ppermute x1, waiting for transfers between devices, body(): image = lax.ppermute(image, ('shot', 'sub'), [(b, a) for a, b in outbound])  10.3 us
    all_to_all x1, starting transfers between devices, body(): lax.all_to_all(sending, 'shot', split_axis=0, concat_axis=0, tiled=True)  9.36 us
    ppermute x1, starting transfers between devices, body(): image = lax.ppermute(image, ('shot', 'sub'), [(b, a) for a, b in outbound])  6.67 us
    ppermute x1, starting transfers between devices, body(): states_moved.append(lax.ppermute(states, ('shot', 'sub'), outbound))  6.08 us
  transfers between devices with their start and end apart: 5, of which 4 were waited for; matrix products, arithmetic and copies ran while one was open for 9% of the time, Pallas kernels for 0%

profile of v5, /device:TPU:5, one launch (start us, length us, event | category | flops | bytes accessed | tf_op | source)
XLA Modules:
  0.0 171.3 jit_solution(1617299645523082062)
XLA Ops:
  0.0 1.3 dynamic_slice.9
  3.3 0.7 and_select_fusion.14
  4.2 0.7 fusion.22
  6.0 0.6 gather_fusion
  6.9 0.7 slice_select_fusion.1
  7.6 9.4 %all-to-all-start = ((f32[32,1,8,256]{3,2,1,0:T(8,128)}), f32[32,1,8,256]{3,2,1,0:T(8,128)S(1)}, u32[]{:S(2)}, u32[]{:S(2)}) async-start(f32[32,1,8,256]{3,2,1,0:T(8,128)} %slice_select_fusion.1), calls=%async_computation | async-start | bytes 524288 | tf_op jit(solution)/shard_map/all_to_all | solution.py:452
  17.0 1.0 maximum_convert_fusion
  18.0 6.1 %collective-permute-start.1 = (f32[4,8,64,128]{3,2,1,0:T(8,128)}, f32[4,8,64,128]{3,2,1,0:T(8,128)}, u32[]{:S(2)}, u32[]{:S(2)}) collective-permute-start(f32[4,8,64,128]{3,2,1,0:T(8,128)} %maximum_convert_fusion), channel_id=1, source_target_pairs={{0,2},{1,4},{2,6},{3,0},{4,1},{5,7},{6,5},{7,3},{8,12},{9,14},{10,... | collective-permute-start | bytes 3145736 | tf_op jit(solution)/shard_map/ppermute | solution.py:448
  24.7 0.7 fusion.11
  25.6 0.7 fusion.13
  27.6 0.7 pad_add_fusion.1.src_ref
  28.4 0.8 copy.18
  29.4 0.7 add_select_fusion.rcol_ref
  30.7 0.7 reshape.707
  31.4 2.5 %copy.20 = f32[8,4,16,9,16]{2,1,4,3,0:T(4,128)} copy(f32[8,4,16,9,16]{4,2,0,3,1:T(8,128)S(1)} %bitcast.73) | data formatting | bytes 589824 | tf_op jit(solution)/shard_map/transpose | solution.py:151
  33.9 2.5 %reshape.708 = f32[8,64,144]{1,2,0:T(8,128)S(1)} reshape(f32[8,4,16,9,16]{2,1,4,3,0:T(4,128)} %copy.20) | data formatting | bytes 589824 | tf_op jit(solution)/shard_map/reshape | solution.py:151
  36.7 4.1 %collective-permute-start = (f32[8,64,128]{2,1,0:T(8,128)S(1)}, f32[8,64,128]{2,1,0:T(8,128)S(1)}, u32[]{:S(2)}, u32[]{:S(2)}) collective-permute-start(f32[8,64,128]{2,1,0:T(8,128)S(1)} %copy.26), channel_id=1, source_target_pairs={{0,2},{1,4},{2,6},{3,0},{4,1},{5,7},{6,5},{7,3},{8,12},{9,14},{10,... | collective-permute-start | bytes 786440 | tf_op jit(solution)/shard_map/ppermute | solution.py:459
  40.8 19.9 %collective-permute-done.1 = f32[4,8,64,128]{3,2,1,0:T(8,128)} collective-permute-done((f32[4,8,64,128]{3,2,1,0:T(8,128)}, f32[4,8,64,128]{3,2,1,0:T(8,128)}, u32[]{:S(2)}, u32[]{:S(2)}) %collective-permute-start.1) | collective-permute-done | bytes 1048608 | tf_op jit(solution)/shard_map/ppermute | solution.py:448
  60.6 2.3 %fusion.23 = (f32[2,8,64,128]{3,2,1,0:T(8,128)}, f32[2,8,64,128]{3,2,1,0:T(8,128)}) fusion(f32[4,8,64,128]{3,2,1,0:T(8,128)} %collective-permute-done.1), kind=kLoop, calls=%fused_computation.109 | loop fusion | bytes 2097152 | tf_op jit(solution)/shard_map/slice | solution.py:464
  62.9 2.4 %collective-permute-done.model_ref = f32[8,64,128]{2,1,0:T(8,128)S(1)} collective-permute-done((f32[8,64,128]{2,1,0:T(8,128)S(1)}, f32[8,64,128]{2,1,0:T(8,128)S(1)}, u32[]{:S(2)}, u32[]{:S(2)}) %collective-permute-start) | collective-permute-done | bytes 262176 | tf_op jit(solution)/shard_map/ppermute | solution.py:459
  65.3 0.7 copy-done.3
  66.1 29.3 %shard_map.91 = f32[8,64,128]{2,1,0:T(8,128)} custom-call(s32[3]{0:T(128)} %pad_add_fusion.1.src_ref, f32[4]{0:T(128)} %bitcast.83, s32[2,256]{1,0:T(2,128)} %pad_add_fusion.rrow_ref, s32[256,1]{1,0:T(8,128)} %add_select_fusion.rcol_ref, f32[256,4]{1,0:T(8,128)} %bitcast.79, f32[8,64,128]{2,1,0:T(8,128)} %copy-done.3, ...), custom_call_target="tpu_custom_call" | custom-call | tf_op jit(solution)/shard_map/pallas_call | solution.py:392
  95.4 6.7 %collective-permute-start.2 = (f32[8,64,128]{2,1,0:T(8,128)}, f32[8,64,128]{2,1,0:T(8,128)S(1)}, u32[]{:S(2)}, u32[]{:S(2)}) collective-permute-start(f32[8,64,128]{2,1,0:T(8,128)} %shard_map.91), channel_id=1, source_target_pairs={{2,0},{4,1},{6,2},{0,3},{1,4},{7,5},{5,6},{3,7},{12,8},{14,9},{8,1... | collective-permute-start | bytes 786440 | tf_op jit(solution)/shard_map/ppermute | solution.py:470
  102.2 10.3 %collective-permute-done.2 = f32[8,64,128]{2,1,0:T(8,128)S(1)} collective-permute-done((f32[8,64,128]{2,1,0:T(8,128)}, f32[8,64,128]{2,1,0:T(8,128)S(1)}, u32[]{:S(2)}, u32[]{:S(2)}) %collective-permute-start.2) | collective-permute-done | bytes 262176 | tf_op jit(solution)/shard_map/ppermute | solution.py:470
  112.8 1.1 dynamic_update_slice.3
  113.9 1.0 reshape.709
  114.9 2.5 %copy.23 = f32[4,9,8,16,16]{4,3,2,1,0:T(8,128)} copy(f32[4,9,8,16,16]{3,0,4,1,2:T(4,128)S(1)} %bitcast.74) | data formatting | bytes 589824 | tf_op jit(solution)/shard_map/transpose | solution.py:160
  117.4 2.5 %reshape.710 = f32[36,8,256]{2,1,0:T(8,128)S(1)} reshape(f32[4,9,8,16,16]{4,3,2,1,0:T(8,128)} %copy.23) | data formatting | bytes 589824 | tf_op jit(solution)/shard_map/reshape | solution.py:160
  120.7 0.7 slice_select_fusion
  121.5 37.5 %all-to-all-start.1 = ((f32[32,1,8,256]{3,2,1,0:T(8,128)}), f32[32,1,8,256]{3,2,1,0:T(8,128)S(1)}, u32[]{:S(2)}, u32[]{:S(2)}) async-start(f32[32,1,8,256]{3,2,1,0:T(8,128)} %slice_select_fusion), calls=%async_computation.1 | async-start | bytes 524288 | tf_op jit(solution)/shard_map/all_to_all | solution.py:472
  159.4 10.7 %all-to-all-done.1 = f32[32,1,8,256]{3,2,1,0:T(8,128)S(1)} async-done(((f32[32,1,8,256]{3,2,1,0:T(8,128)}), f32[32,1,8,256]{3,2,1,0:T(8,128)S(1)}, u32[]{:S(2)}, u32[]{:S(2)}) %all-to-all-start.1) | async-done | bytes 262176 | tf_op jit(solution)/shard_map/all_to_all | solution.py:472
  170.6 0.7 copy.25
  (58 shorter events, 5.4 us)
Async XLA Ops:
  0.0 6.0 %copy-start = (f32[12,8,256]{2,1,0:T(8,128)S(1)}, f32[12,8,256]{2,1,0:T(8,128)}, u32[]{:S(2)}) copy-start(f32[12,8,256]{2,1,0:T(8,128)} %param.9) | copy-start | bytes 294916
  0.0 17.0 %copy-start.2 = (bf16[1,2,8,64,128]{4,3,2,1,0:T(8,128)(2,1)S(1)}, bf16[1,2,8,64,128]{4,3,2,1,0:T(8,128)(2,1)}, u32[]{:S(2)}) copy-start(bf16[1,2,8,64,128]{4,3,2,1,0:T(8,128)(2,1)} %param.10) | copy-start | bytes 786436
  0.0 17.0 %copy-start.1 = (bf16[1,2,8,64,128]{4,3,2,1,0:T(8,128)(2,1)S(1)}, bf16[1,2,8,64,128]{4,3,2,1,0:T(8,128)(2,1)}, u32[]{:S(2)}) copy-start(bf16[1,2,8,64,128]{4,3,2,1,0:T(8,128)(2,1)} %param.11) | copy-start | bytes 786436
  6.0 18.2 %copy-start.6 = (s32[32]{0:T(128)S(1)}, s32[32]{0:T(128)}, u32[]{:S(2)}) copy-start(s32[32]{0:T(128)} %param.16) | copy-start | bytes 388
  6.0 19.6 %copy-start.4 = (s32[1,256]{1,0:T(1,128)S(1)}, s32[1,256]{1,0:T(1,128)}, u32[]{:S(2)}) copy-start(s32[1,256]{1,0:T(1,128)} %param.14) | copy-start | bytes 3076
  6.6 21.8 %copy-start.5 = (f32[1,4,256]{2,1,0:T(4,128)S(1)}, f32[1,4,256]{2,1,0:T(4,128)}, u32[]{:S(2)}) copy-start(f32[1,4,256]{2,1,0:T(4,128)} %param.15) | copy-start | bytes 12292
  7.6 22.5 %all-to-all-start = ((f32[32,1,8,256]{3,2,1,0:T(8,128)}), f32[32,1,8,256]{3,2,1,0:T(8,128)S(1)}, u32[]{:S(2)}, u32[]{:S(2)}) async-start(f32[32,1,8,256]{3,2,1,0:T(8,128)} %slice_select_fusion.1), calls=%async_computation | async-start | bytes 524288 | tf_op jit(solution)/shard_map/all_to_all | solution.py:452
  18.0 42.6 %collective-permute-start.1 = (f32[4,8,64,128]{3,2,1,0:T(8,128)}, f32[4,8,64,128]{3,2,1,0:T(8,128)}, u32[]{:S(2)}, u32[]{:S(2)}) collective-permute-start(f32[4,8,64,128]{3,2,1,0:T(8,128)} %maximum_convert_fusion), channel_id=1, source_target_pairs={{0,2},{1,4},{2,6},{3,0},{4,1},{5,7},{6,5},{7,3},{8,12},{9,14},{10,... | collective-permute-start | bytes 3145736 | tf_op jit(solution)/shard_map/ppermute | solution.py:448
  36.7 28.7 %collective-permute-start = (f32[8,64,128]{2,1,0:T(8,128)S(1)}, f32[8,64,128]{2,1,0:T(8,128)S(1)}, u32[]{:S(2)}, u32[]{:S(2)}) collective-permute-start(f32[8,64,128]{2,1,0:T(8,128)S(1)} %copy.26), channel_id=1, source_target_pairs={{0,2},{1,4},{2,6},{3,0},{4,1},{5,7},{6,5},{7,3},{8,12},{9,14},{10,... | collective-permute-start | bytes 786440 | tf_op jit(solution)/shard_map/ppermute | solution.py:459
  65.3 0.7 copy-start.3
  95.4 17.2 %collective-permute-start.2 = (f32[8,64,128]{2,1,0:T(8,128)}, f32[8,64,128]{2,1,0:T(8,128)S(1)}, u32[]{:S(2)}, u32[]{:S(2)}) collective-permute-start(f32[8,64,128]{2,1,0:T(8,128)} %shard_map.91), channel_id=1, source_target_pairs={{2,0},{4,1},{6,2},{0,3},{1,4},{7,5},{5,6},{3,7},{12,8},{14,9},{8,1... | collective-permute-start | bytes 786440 | tf_op jit(solution)/shard_map/ppermute | solution.py:470
  121.5 48.6 %all-to-all-start.1 = ((f32[32,1,8,256]{3,2,1,0:T(8,128)}), f32[32,1,8,256]{3,2,1,0:T(8,128)S(1)}, u32[]{:S(2)}, u32[]{:S(2)}) async-start(f32[32,1,8,256]{3,2,1,0:T(8,128)} %slice_select_fusion), calls=%async_computation.1 | async-start | bytes 524288 | tf_op jit(solution)/shard_map/all_to_all | solution.py:472

commit v6 on v5

--- a/solution.py
+++ b/solution.py
@@ -1,3 +1,5 @@
+import functools
+
 import jax
 import jax.numpy as jnp
 from jax import lax
@@ -231,94 +233,77 @@
     return (high, middle, low)
 
 
-def migrate_kernel(
-    src_ref, wave_ref, rrow_ref, rcol_ref, resid_ref, model_ref, pf_ref, qa_ref,
-    img_ref, pad_p, pad_q, lap, qs, inject, send_sem, recv_sem,
-):
+def halo_exchange(buf, r, f, me, n_sub, up_dev, down_dev, send_sem, recv_sem):
+    depth = buf.shape[1] - 2 * RADIUS
+    down = pltpu.make_async_remote_copy(
+        src_ref=buf.at[r, RADIUS : 2 * RADIUS],
+        dst_ref=buf.at[r, RADIUS + depth : 2 * RADIUS + depth],
+        send_sem=send_sem.at[r, f, 0],
+        recv_sem=recv_sem.at[r, f, 0],
+        device_id={"sub": down_dev},
+        device_id_type=pl.DeviceIdType.MESH,
+    )
+    up = pltpu.make_async_remote_copy(
+        src_ref=buf.at[r, depth : RADIUS + depth],
+        dst_ref=buf.at[r, 0:RADIUS],
+        send_sem=send_sem.at[r, f, 1],
+        recv_sem=recv_sem.at[r, f, 1],
+        device_id={"sub": up_dev},
+        device_id_type=pl.DeviceIdType.MESH,
+    )
+
+    @pl.when(me > 0)
+    def _():
+        down.start()
+
+    @pl.when(me < n_sub - 1)
+    def _():
+        up.start()
+
+    def finish():
+        @pl.when(me > 0)
+        def _():
+            down.wait_send()
+            up.wait_recv()
+
+        @pl.when(me < n_sub - 1)
+        def _():
+            up.wait_send()
+            down.wait_recv()
+
+    return finish
+
+
+def chain_setup(pad, first, depth):
     group = lax.axis_index("shot")
     me = block_of(group, lax.axis_index("sub"))
     n_sub = lax.axis_size("sub")
-    depth = model_ref.shape[0]
     halo = jnp.zeros((RADIUS, AX, AY), jnp.float32)
     for r in range(NT):
-        for buf in (pad_p, pad_q):
-            buf[r, 0:RADIUS] = halo
-            buf[r, RADIUS + depth : 2 * RADIUS + depth] = halo
-    pad_p[0, RADIUS : RADIUS + depth] = pf_ref[0]
-    pad_q[0, RADIUS : RADIUS + depth] = model_ref[...] * qa_ref[0]
+        pad[r, 0:RADIUS] = halo
+        pad[r, RADIUS + depth : 2 * RADIUS + depth] = halo
+    pad[0, RADIUS : RADIUS + depth] = first
     up_dev = device_of(group, (me + 1) % n_sub)
     down_dev = device_of(group, (me + n_sub - 1) % n_sub)
     barrier = pltpu.get_barrier_semaphore()
     pl.semaphore_signal(barrier, 1, device_id={"sub": up_dev}, device_id_type=pl.DeviceIdType.MESH)
     pl.semaphore_signal(barrier, 1, device_id={"sub": down_dev}, device_id_type=pl.DeviceIdType.MESH)
     pl.semaphore_wait(barrier, 2)
+    return me, n_sub, up_dev, down_dev
+
+
+def forward_kernel(src_ref, wave_ref, model_ref, pf_ref, lap, pad_p, send_sem, recv_sem):
+    depth = model_ref.shape[0]
+    me, n_sub, up_dev, down_dev = chain_setup(pad_p, pf_ref[0], depth)
     rows = lax.broadcasted_iota(jnp.int32, (AX, AY), 0)
     lanes = lax.broadcasted_iota(jnp.int32, (AX, AY), 1)
-    n_rec = rcol_ref.shape[0]
     src_level = src_ref[0]
     src_spot = (rows == src_ref[1]) & (lanes == src_ref[2])
-
-    def build_injection(step):
-        hit_y = lax.broadcasted_iota(jnp.int32, (n_rec, AY), 1) == rcol_ref[...]
-        spread = jnp.where(hit_y, resid_ref[:, step : step + 1], 0.0)
-        parts = split_bf16(spread)
-        rec_level = rrow_ref[0:1, :]
-        hit_x = lax.broadcasted_iota(jnp.int32, (AX, n_rec), 0) == rrow_ref[1:2, :]
-
-        def plane(j, carry):
-            picks = (hit_x & (rec_level == j)).astype(jnp.bfloat16)
-            total = jnp.dot(picks, parts[0], preferred_element_type=jnp.float32)
-            total = total + jnp.dot(picks, parts[1], preferred_element_type=jnp.float32)
-            total = total + jnp.dot(picks, parts[2], preferred_element_type=jnp.float32)
-            inject[j] = total
-            return carry
-
-        lax.fori_loop(0, depth, plane, 0)
-
-    def exchange(r, f):
-        buf = (pad_p, pad_q)[f]
-        down = pltpu.make_async_remote_copy(
-            src_ref=buf.at[r, RADIUS : 2 * RADIUS],
-            dst_ref=buf.at[r, RADIUS + depth : 2 * RADIUS + depth],
-            send_sem=send_sem.at[r, f, 0],
-            recv_sem=recv_sem.at[r, f, 0],
-            device_id={"sub": down_dev},
-            device_id_type=pl.DeviceIdType.MESH,
-        )
-        up = pltpu.make_async_remote_copy(
-            src_ref=buf.at[r, depth : RADIUS + depth],
-            dst_ref=buf.at[r, 0:RADIUS],
-            send_sem=send_sem.at[r, f, 1],
-            recv_sem=recv_sem.at[r, f, 1],
-            device_id={"sub": up_dev},
-            device_id_type=pl.DeviceIdType.MESH,
-        )
-
-        @pl.when(me > 0)
-        def _():
-            down.start()
-
-        @pl.when(me < n_sub - 1)
-        def _():
-            up.start()
-
-        return (down, up)
-
-    def finish(pair):
-        down, up = pair
-
-        @pl.when(me > 0)
-        def _():
-            down.wait_send()
-            up.wait_recv()
-
-        @pl.when(me < n_sub - 1)
-        def _():
-            up.wait_send()
-            down.wait_recv()
-
-    def forward_round(r):
-        def plane(j, carry):
+    for r in range(NT):
+        finish = halo_exchange(pad_p, r, 0, me, n_sub, up_dev, down_dev, send_sem, recv_sem)
+        finish()
+
+        def plane(j, carry, r=r):
             p = j + RADIUS
             lp = plane_stencil(pad_p, r, p, rows, lanes)
             lap[r, j] = lp
@@ -331,8 +316,40 @@
 
         lax.fori_loop(0, depth, plane, 0)
 
-    def adjoint_round(r):
+
+def adjoint_kernel(
+    rrow_ref, rcol_ref, resid_ref, model_ref, qa_ref, lap, img_ref,
+    pad_q, qs, inject, send_sem, recv_sem,
+):
+    depth = model_ref.shape[0]
+    me, n_sub, up_dev, down_dev = chain_setup(pad_q, model_ref[...] * qa_ref[0], depth)
+    n_rec = rcol_ref.shape[0]
+
+    def build_injection(step):
+        hit_y = lax.broadcasted_iota(jnp.int32, (n_rec, AY), 1) == rcol_ref[...]
+        spread = jnp.where(hit_y, resid_ref[:, step : step + 1], 0.0)
+        parts = split_bf16(spread)
+        rec_level = rrow_ref[0:1, :]
+        hit_x = lax.broadcasted_iota(jnp.int32, (AX, n_rec), 0) == rrow_ref[1:2, :]
+
         def plane(j, carry):
+            picks = (hit_x & (rec_level == j)).astype(jnp.bfloat16)
+            total = jnp.dot(picks, parts[0], preferred_element_type=jnp.float32)
+            total = total + jnp.dot(picks, parts[1], preferred_element_type=jnp.float32)
+            total = total + jnp.dot(picks, parts[2], preferred_element_type=jnp.float32)
+            inject[j] = total
+            return carry
+
+        lax.fori_loop(0, depth, plane, 0)
+
+    rows = lax.broadcasted_iota(jnp.int32, (AX, AY), 0)
+    lanes = lax.broadcasted_iota(jnp.int32, (AX, AY), 1)
+    for r in range(NT):
+        finish = halo_exchange(pad_q, r, 0, me, n_sub, up_dev, down_dev, send_sem, recv_sem)
+        build_injection(NT - 1 - r)
+        finish()
+
+        def plane(j, carry, r=r):
             p = j + RADIUS
             lq = plane_stencil(pad_q, r, p, rows, lanes)
             now = qa_ref[0, j] if r == 0 else qs[r - 1, j]
@@ -357,20 +374,6 @@
 
         lax.fori_loop(0, depth, plane, 0)
 
-    fwd = exchange(0, 0)
-    adj = exchange(0, 1)
-    build_injection(NT - 1)
-    for r in range(NT):
-        finish(fwd)
-        forward_round(r)
-        if r < NT - 1:
-            fwd = exchange(r + 1, 0)
-        finish(adj)
-        adjoint_round(r)
-        if r < NT - 1:
-            adj = exchange(r + 1, 1)
-            build_injection(NT - 2 - r)
-
 
 def migrate(model, state_fwd, state_adj, wave, source, receivers, resid):
     depth_cells = model.shape[0]
@@ -389,31 +392,33 @@
     smem = pl.BlockSpec(memory_space=pltpu.SMEM)
     padded = (NT, depth_cells + 2 * RADIUS, AX, AY)
     field = (NT, depth_cells, AX, AY)
-    return pl.pallas_call(
-        migrate_kernel,
-        out_shape=jax.ShapeDtypeStruct(model.shape, jnp.float32),
-        in_specs=[smem, smem] + [vmem] * 6,
+    lap = pl.pallas_call(
+        forward_kernel,
+        out_shape=jax.ShapeDtypeStruct(field, jnp.float32),
+        in_specs=[smem, smem, vmem, vmem],
         out_specs=vmem,
         scratch_shapes=[
             pltpu.VMEM(padded, jnp.float32),
-            pltpu.VMEM(padded, jnp.float32),
-            pltpu.VMEM(field, jnp.float32),
-            pltpu.VMEM(field, jnp.float32),
-            pltpu.VMEM(model.shape, jnp.float32),
-            pltpu.SemaphoreType.DMA((NT, 2, 2)),
-            pltpu.SemaphoreType.DMA((NT, 2, 2)),
+            pltpu.SemaphoreType.DMA((NT, 1, 2)),
+            pltpu.SemaphoreType.DMA((NT, 1, 2)),
         ],
         compiler_params=pltpu.CompilerParams(collective_id=0, has_side_effects=True),
-    )(
-        src,
-        wave.astype(jnp.float32),
-        rrow,
-        rcol,
-        resid.T,
-        model,
-        state_fwd.astype(jnp.float32),
-        state_adj.astype(jnp.float32),
-    )
+    )(src, wave.astype(jnp.float32), model, state_fwd.astype(jnp.float32))
+    state_adj = state_adj()
+    return pl.pallas_call(
+        adjoint_kernel,
+        out_shape=jax.ShapeDtypeStruct(model.shape, jnp.float32),
+        in_specs=[vmem] * 6,
+        out_specs=vmem,
+        scratch_shapes=[
+            pltpu.VMEM(padded, jnp.float32),
+            pltpu.VMEM((NT - 1, depth_cells, AX, AY), jnp.float32),
+            pltpu.VMEM(model.shape, jnp.float32),
+            pltpu.SemaphoreType.DMA((NT, 1, 2)),
+            pltpu.SemaphoreType.DMA((NT, 1, 2)),
+        ],
+        compiler_params=pltpu.CompilerParams(collective_id=1, has_side_effects=True),
+    )(rrow, rcol, resid.T, model, state_adj.astype(jnp.float32), lap)
 
 
 def body(
@@ -440,12 +445,10 @@
     shots_here = forward_state.shape[0]
     gradient = jnp.zeros(velocity_tiles.shape, jnp.float32)
     every_shot = list(range(shots_here))
-    states_moved = []
+    forward_moved = []
     for k in range(shots_here):
-        states = jnp.concatenate(
-            [forward_state[k].astype(jnp.float32), adjoint_state[k].astype(jnp.float32)]
-        )
-        states_moved.append(lax.ppermute(states, ("shot", "sub"), outbound))
+        states = forward_state[k].astype(jnp.float32)
+        forward_moved.append(lax.ppermute(states, ("shot", "sub"), outbound))
     sending = outgoing(
         velocity_tiles, aperture_row, aperture_col, every_shot, groups, own_cols, caps
     )
@@ -457,11 +460,13 @@
         col_start = aperture_col[shot_id]
         model = assemble(fetched, row_start, col_start, own_cols)
         model = lax.ppermute(model, ("shot", "sub"), outbound)
-        states = states_moved[k]
+        adjoint_moved = functools.partial(
+            lax.ppermute, adjoint_state[k].astype(jnp.float32), ("shot", "sub"), outbound
+        )
         image = migrate(
             model,
-            states[0:2],
-            states[2:4],
+            forward_moved[k],
+            adjoint_moved,
             wavelet[k],
             source_cell[k],
             receiver_cell[k],

time: 172 us -> 196 us (1.14)
  Pallas kernels: 29.3 us -> 61.6 us
  starting transfers between devices: 63.7 us -> 58.5 us
  waiting for transfers between devices: 43.3 us -> 40.1 us
    pallas_call x1 -> x2, Pallas kernels: 29.3 us -> 61.6 us  [the longest x1 36.9 us: migrate(): pl.pallas_call(adjoint_kernel, out_shape=jax.ShapeDtypeStruct(model.shape...]
    ppermute x1 -> x2, waiting for transfers between devices: 19.9 us -> 0.01 us  [the longest x1 0.01 us: body(): forward_moved.append(lax.ppermute(states, ('shot', 'sub'), outbound))]
    ppermute x1, waiting for transfers between devices: 2.41 us -> 22 us  [body(): model = lax.ppermute(model, ('shot', 'sub'), outbound)]
    all_to_all x1, starting transfers between devices: 37.5 us -> 32.9 us  [body(): lax.all_to_all(images[0], 'shot', split_axis=0, concat_axis=0, tiled=True)]
    ppermute x1 -> x2, starting transfers between devices: 6.08 us -> 9.14 us  [the longest x1 6.08 us: body(): forward_moved.append(lax.ppermute(states, ('shot', 'sub'), outbound))]
    ppermute x1, waiting for transfers between devices: 10.3 us -> 7.47 us  [body(): image = lax.ppermute(image, ('shot', 'sub'), [(b, a) for a, b in outbound])]
    slice x1 -> x0, local copies, waits for them, and re-layouts: 2.29 us -> none  [body(): states[2:4]]
  transfers between devices with their start and end apart: 5 -> 6, of which waited for: 4 -> 3; matrix products, arithmetic and copies ran while one was open for 9% -> 7% of each run, Pallas kernels for 0% -> 13%
where the time goes in v6:
time: 196 us; the launch traced here: 195 us
  Pallas kernels  61.6 us (31%)
  starting transfers between devices  58.5 us (30%)
  waiting for transfers between devices  40.1 us (20%)
  local copies, waits for them, and re-layouts  21.2 us (11%)
  other arithmetic  9.21 us (5%)
  between operations  3.85 us (2%)
    pallas_call x1, Pallas kernels, migrate(): pl.pallas_call(adjoint_kernel, out_shape=jax.ShapeDtypeStruct(model.shape...  36.9 us
    all_to_all x1, starting transfers between devices, body(): lax.all_to_all(images[0], 'shot', split_axis=0, concat_axis=0, tiled=True)  32.9 us
    pallas_call x1, Pallas kernels, migrate(): pl.pallas_call(forward_kernel, out_shape=jax.ShapeDtypeStruct(field, jnp....  24.8 us
    ppermute x1, waiting for transfers between devices, body(): model = lax.ppermute(model, ('shot', 'sub'), outbound)  22 us
    all_to_all x1, waiting for transfers between devices, body(): lax.all_to_all(images[0], 'shot', split_axis=0, concat_axis=0, tiled=True)  10.7 us
    all_to_all x1, starting transfers between devices, body(): lax.all_to_all(sending, 'shot', split_axis=0, concat_axis=0, tiled=True)  9.36 us
    ppermute x1, waiting for transfers between devices, body(): image = lax.ppermute(image, ('shot', 'sub'), [(b, a) for a, b in outbound])  7.47 us
    ppermute x1, starting transfers between devices, body(): forward_moved.append(lax.ppermute(states, ('shot', 'sub'), outbound))  6.08 us
  transfers between devices with their start and end apart: 6, of which 3 were waited for; matrix products, arithmetic and copies ran while one was open for 7% of the time, Pallas kernels for 13%

profile of v6, /device:TPU:5, one launch (start us, length us, event | category | flops | bytes accessed | tf_op | source)
XLA Modules:
  0.0 194.9 jit_solution(13798003135267349075)
XLA Ops:
  0.0 1.4 dynamic_slice.9
  3.4 0.7 and_select_fusion.14
  4.2 0.7 fusion.22
  7.5 0.7 slice_select_fusion.1
  8.2 9.4 %all-to-all-start = ((f32[32,1,8,256]{3,2,1,0:T(8,128)}), f32[32,1,8,256]{3,2,1,0:T(8,128)S(1)}, u32[]{:S(2)}, u32[]{:S(2)}) async-start(f32[32,1,8,256]{3,2,1,0:T(8,128)} %slice_select_fusion.1), calls=%async_computation | async-start | bytes 524288 | tf_op jit(solution)/shard_map/all_to_all | solution.py:455
  17.6 0.9 bitcast_convert_fusion
  18.5 6.1 %collective-permute-start.2 = (f32[2,8,64,128]{3,2,1,0:T(8,128)}, f32[2,8,64,128]{3,2,1,0:T(8,128)S(1)}, u32[]{:S(2)}, u32[]{:S(2)}) collective-permute-start(f32[2,8,64,128]{3,2,1,0:T(8,128)} %bitcast_convert_fusion), channel_id=1, source_target_pairs={{0,2},{1,4},{2,6},{3,0},{4,1},{5,7},{6,5},{7,3},{8,12},{9,14},{10,... | collective-permute-start | bytes 1572872 | tf_op jit(solution)/shard_map/ppermute | solution.py:451
  24.6 0.8 bitcast_convert_fusion.1
  25.4 3.1 %collective-permute-start.1 = (f32[2,8,64,128]{3,2,1,0:T(8,128)}, f32[2,8,64,128]{3,2,1,0:T(8,128)}, u32[]{:S(2)}, u32[]{:S(2)}) collective-permute-start(f32[2,8,64,128]{3,2,1,0:T(8,128)} %bitcast_convert_fusion.1), channel_id=1, source_target_pairs={{0,2},{1,4},{2,6},{3,0},{4,1},{5,7},{6,5},{7,3},{8,12},{9,14},{10,... | collective-permute-start | bytes 1572872 | tf_op jit(solution)/shard_map/ppermute | solution.py:407
  29.1 0.6 fusion.11
  29.7 0.6 fusion.13
  33.3 0.7 reshape.707
  34.0 2.5 %copy.20 = f32[8,4,16,9,16]{2,1,4,3,0:T(4,128)} copy(f32[8,4,16,9,16]{4,2,0,3,1:T(8,128)S(1)} %bitcast.77) | data formatting | bytes 589824 | tf_op jit(solution)/shard_map/transpose | solution.py:153
  36.5 2.5 %reshape.708 = f32[8,64,144]{1,2,0:T(8,128)S(1)} reshape(f32[8,4,16,9,16]{2,1,4,3,0:T(4,128)} %copy.20) | data formatting | bytes 589824 | tf_op jit(solution)/shard_map/reshape | solution.py:153
  39.3 2.2 %collective-permute-start = (f32[8,64,128]{2,1,0:T(8,128)S(1)}, f32[8,64,128]{2,1,0:T(8,128)S(1)}, u32[]{:S(2)}, u32[]{:S(2)}) collective-permute-start(f32[8,64,128]{2,1,0:T(8,128)S(1)} %copy.26), channel_id=1, source_target_pairs={{0,2},{1,4},{2,6},{3,0},{4,1},{5,7},{6,5},{7,3},{8,12},{9,14},{10,... | collective-permute-start | bytes 786440 | tf_op jit(solution)/shard_map/ppermute | solution.py:462
  42.2 0.8 copy.18
  43.1 0.7 add_select_fusion.rcol_ref
  43.8 22.0 %collective-permute-done.model_ref = f32[8,64,128]{2,1,0:T(8,128)S(1)} collective-permute-done((f32[8,64,128]{2,1,0:T(8,128)S(1)}, f32[8,64,128]{2,1,0:T(8,128)S(1)}, u32[]{:S(2)}, u32[]{:S(2)}) %collective-permute-start) | collective-permute-done | bytes 262176 | tf_op jit(solution)/shard_map/ppermute | solution.py:462
  65.8 0.7 copy-done.1
  66.5 24.8 %shard_map.91.lap = f32[4,8,64,128]{3,2,1,0:T(8,128)} custom-call(s32[3]{0:T(128)} %pad_add_fusion.1.src_ref, f32[4]{0:T(128)} %bitcast.85, f32[8,64,128]{2,1,0:T(8,128)} %copy-done.1, f32[2,8,64,128]{3,2,1,0:T(8,128)} %copy-done.2), custom_call_target="tpu_custom_call" | custom-call | tf_op jit(solution)/shard_map/pallas_call | solution.py:395
  91.3 36.9 %shard_map.92 = f32[8,64,128]{2,1,0:T(8,128)} custom-call(s32[2,256]{1,0:T(2,128)} %pad_add_fusion.rrow_ref, s32[256,1]{1,0:T(8,128)} %add_select_fusion.rcol_ref, f32[256,4]{1,0:T(8,128)} %bitcast.83, f32[8,64,128]{2,1,0:T(8,128)} %copy-done.1, f32[2,8,64,128]{3,2,1,0:T(8,128)} %collective-permute-done.1.qa_ref, f32[4,8,64,128]{3,2,1,0:T(8,128)} %shard_map.91.lap), custom_call_target="tpu_custom_call" | custom-call | tf_op jit(solution)/shard_map/pallas_call | solution.py:408
  128.2 4.9 %collective-permute-start.3 = (f32[8,64,128]{2,1,0:T(8,128)}, f32[8,64,128]{2,1,0:T(8,128)S(1)}, u32[]{:S(2)}, u32[]{:S(2)}) collective-permute-start(f32[8,64,128]{2,1,0:T(8,128)} %shard_map.92), channel_id=1, source_target_pairs={{2,0},{4,1},{6,2},{0,3},{1,4},{7,5},{5,6},{3,7},{12,8},{14,9},{8,1... | collective-permute-start | bytes 786440 | tf_op jit(solution)/shard_map/ppermute | solution.py:475
  133.3 7.5 %collective-permute-done.3 = f32[8,64,128]{2,1,0:T(8,128)S(1)} collective-permute-done((f32[8,64,128]{2,1,0:T(8,128)}, f32[8,64,128]{2,1,0:T(8,128)S(1)}, u32[]{:S(2)}, u32[]{:S(2)}) %collective-permute-start.3) | collective-permute-done | bytes 262176 | tf_op jit(solution)/shard_map/ppermute | solution.py:475
  141.0 1.1 dynamic_update_slice.3
  142.1 1.0 reshape.709
  143.1 2.4 %copy.23 = f32[4,9,8,16,16]{4,3,2,1,0:T(8,128)} copy(f32[4,9,8,16,16]{3,0,4,1,2:T(4,128)S(1)} %bitcast.78) | data formatting | bytes 589824 | tf_op jit(solution)/shard_map/transpose | solution.py:162
  145.6 2.5 %reshape.710 = f32[36,8,256]{2,1,0:T(8,128)S(1)} reshape(f32[4,9,8,16,16]{4,3,2,1,0:T(8,128)} %copy.23) | data formatting | bytes 589824 | tf_op jit(solution)/shard_map/reshape | solution.py:162
  148.1 0.6 gather_fusion.2
  148.9 0.7 slice_select_fusion
  149.7 32.9 %all-to-all-start.1 = ((f32[32,1,8,256]{3,2,1,0:T(8,128)}), f32[32,1,8,256]{3,2,1,0:T(8,128)S(1)}, u32[]{:S(2)}, u32[]{:S(2)}) async-start(f32[32,1,8,256]{3,2,1,0:T(8,128)} %slice_select_fusion), calls=%async_computation.1 | async-start | bytes 524288 | tf_op jit(solution)/shard_map/all_to_all | solution.py:477
  183.0 10.7 %all-to-all-done.1 = f32[32,1,8,256]{3,2,1,0:T(8,128)S(1)} async-done(((f32[32,1,8,256]{3,2,1,0:T(8,128)}), f32[32,1,8,256]{3,2,1,0:T(8,128)S(1)}, u32[]{:S(2)}, u32[]{:S(2)}) %all-to-all-start.1) | async-done | bytes 262176 | tf_op jit(solution)/shard_map/all_to_all | solution.py:477
  194.2 0.7 copy.25
  (89 shorter events, 7.3 us)
Async XLA Ops:
  0.0 6.6 %copy-start = (f32[12,8,256]{2,1,0:T(8,128)S(1)}, f32[12,8,256]{2,1,0:T(8,128)}, u32[]{:S(2)}) copy-start(f32[12,8,256]{2,1,0:T(8,128)} %param.9) | copy-start | bytes 294916
  0.0 17.6 %copy-start.3 = (bf16[1,2,8,64,128]{4,3,2,1,0:T(8,128)(2,1)S(1)}, bf16[1,2,8,64,128]{4,3,2,1,0:T(8,128)(2,1)}, u32[]{:S(2)}) copy-start(bf16[1,2,8,64,128]{4,3,2,1,0:T(8,128)(2,1)} %param.10) | copy-start | bytes 786436
  0.0 24.5 %copy-start.4 = (bf16[1,2,8,64,128]{4,3,2,1,0:T(8,128)(2,1)S(1)}, bf16[1,2,8,64,128]{4,3,2,1,0:T(8,128)(2,1)}, u32[]{:S(2)}) copy-start(bf16[1,2,8,64,128]{4,3,2,1,0:T(8,128)(2,1)} %param.11) | copy-start | bytes 786436
  0.0 30.5 %copy-start.10 = (s32[2]{0:T(128)}, s32[2]{0:T(128)S(1)}, u32[]{:S(2)}) copy-start(s32[2]{0:T(128)S(1)} %iota_multiply_fusion) | copy-start | bytes 28
  4.0 3.2 %copy-start.12 = (s32[32]{0:T(128)}, s32[32]{0:T(128)S(1)}, u32[]{:S(2)}) copy-start(s32[32]{0:T(128)S(1)} %get-tuple-element.5) | copy-start | bytes 388
  5.0 2.3 %copy-start.5 = (s32[32,1,1,2]{3,0,2,1:T(8,128)}, s32[32,1,1,2]{3,0,2,1:T(8,128)S(1)}, u32[]{:S(2)}) copy-start(s32[32,1,1,2]{3,0,2,1:T(8,128)S(1)} %add.447) | copy-start | bytes 772
  5.9 1.4 copy-start.14
  6.6 21.9 %copy-start.20 = (s32[32]{0:T(128)S(1)}, s32[32]{0:T(128)}, u32[]{:S(2)}) copy-start(s32[32]{0:T(128)} %param.16) | copy-start | bytes 388
  6.6 24.7 %copy-start.16 = (s32[1,256]{1,0:T(1,128)S(1)}, s32[1,256]{1,0:T(1,128)}, u32[]{:S(2)}) copy-start(s32[1,256]{1,0:T(1,128)} %param.14) | copy-start | bytes 3076
  7.5 25.2 %copy-start.8 = (pred[32,256]{1,0:T(8,128)(4,1)}, pred[32,256]{1,0:T(8,128)(4,1)S(1)}, u32[]{:S(2)}) copy-start(pred[32,256]{1,0:T(8,128)(4,1)S(1)} %compare_and_fusion) | copy-start | bytes 24580
  8.2 24.5 %all-to-all-start = ((f32[32,1,8,256]{3,2,1,0:T(8,128)}), f32[32,1,8,256]{3,2,1,0:T(8,128)S(1)}, u32[]{:S(2)}, u32[]{:S(2)}) async-start(f32[32,1,8,256]{3,2,1,0:T(8,128)} %slice_select_fusion.1), calls=%async_computation | async-start | bytes 524288 | tf_op jit(solution)/shard_map/all_to_all | solution.py:455
  18.5 25.3 %collective-permute-start.2 = (f32[2,8,64,128]{3,2,1,0:T(8,128)}, f32[2,8,64,128]{3,2,1,0:T(8,128)S(1)}, u32[]{:S(2)}, u32[]{:S(2)}) collective-permute-start(f32[2,8,64,128]{3,2,1,0:T(8,128)} %bitcast_convert_fusion), channel_id=1, source_target_pairs={{0,2},{1,4},{2,6},{3,0},{4,1},{5,7},{6,5},{7,3},{8,12},{9,14},{10,... | collective-permute-start | bytes 1572872 | tf_op jit(solution)/shard_map/ppermute | solution.py:451
  25.4 65.9 %collective-permute-start.1 = (f32[2,8,64,128]{3,2,1,0:T(8,128)}, f32[2,8,64,128]{3,2,1,0:T(8,128)}, u32[]{:S(2)}, u32[]{:S(2)}) collective-permute-start(f32[2,8,64,128]{3,2,1,0:T(8,128)} %bitcast_convert_fusion.1), channel_id=1, source_target_pairs={{0,2},{1,4},{2,6},{3,0},{4,1},{5,7},{6,5},{7,3},{8,12},{9,14},{10,... | collective-permute-start | bytes 1572872 | tf_op jit(solution)/shard_map/ppermute | solution.py:407
  36.5 5.6 %copy-start.17 = (s32[1,256]{1,0:T(1,128)S(1)}, s32[1,256]{1,0:T(1,128)}, u32[]{:S(2)}) copy-start(s32[1,256]{1,0:T(1,128)} %param.14) | copy-start | bytes 3076
  36.5 5.7 %copy-start.18 = (f32[1,4,256]{2,1,0:T(4,128)S(1)}, f32[1,4,256]{2,1,0:T(4,128)}, u32[]{:S(2)}) copy-start(f32[1,4,256]{2,1,0:T(4,128)} %param.15) | copy-start | bytes 12292
  39.3 26.4 %collective-permute-start = (f32[8,64,128]{2,1,0:T(8,128)S(1)}, f32[8,64,128]{2,1,0:T(8,128)S(1)}, u32[]{:S(2)}, u32[]{:S(2)}) collective-permute-start(f32[8,64,128]{2,1,0:T(8,128)S(1)} %copy.26), channel_id=1, source_target_pairs={{0,2},{1,4},{2,6},{3,0},{4,1},{5,7},{6,5},{7,3},{8,12},{9,14},{10,... | collective-permute-start | bytes 786440 | tf_op jit(solution)/shard_map/ppermute | solution.py:462
  42.1 91.0 %copy-start.15 = (pred[32,2]{0,1:T(4,128)(4,1)S(1)}, pred[32,2]{0,1:T(4,128)(4,1)}, u32[]{:S(2)}) copy-start(pred[32,2]{0,1:T(4,128)(4,1)} %copy-done.14) | copy-start | bytes 196
  42.1 91.1 %copy-start.19 = (pred[32]{0:T(512)(128)(4,1)S(1)}, pred[32]{0:T(512)(128)(4,1)}, u32[]{:S(2)}) copy-start(pred[32]{0:T(512)(128)(4,1)} %get-tuple-element.14) | copy-start | bytes 100
  43.8 22.0 %copy-start.2 = (f32[2,8,64,128]{3,2,1,0:T(8,128)}, f32[2,8,64,128]{3,2,1,0:T(8,128)S(1)}, u32[]{:S(2)}) copy-start(f32[2,8,64,128]{3,2,1,0:T(8,128)S(1)} %collective-permute-done.2.pf_ref) | copy-start | bytes 1572868
  65.8 0.7 copy-start.1
  128.2 12.6 %collective-permute-start.3 = (f32[8,64,128]{2,1,0:T(8,128)}, f32[8,64,128]{2,1,0:T(8,128)S(1)}, u32[]{:S(2)}, u32[]{:S(2)}) collective-permute-start(f32[8,64,128]{2,1,0:T(8,128)} %shard_map.92), channel_id=1, source_target_pairs={{2,0},{4,1},{6,2},{0,3},{1,4},{7,5},{5,6},{3,7},{12,8},{14,9},{8,1... | collective-permute-start | bytes 786440 | tf_op jit(solution)/shard_map/ppermute | solution.py:475
  145.6 2.5 %copy-start.7 = (s32[1024]{0:T(1024)S(1)}, s32[1024]{0:T(1024)}, u32[]{:S(2)}) copy-start(s32[1024]{0:T(1024)} %pad_clamp_fusion) | copy-start | bytes 12292
  148.1 34.6 %copy-start.6 = (s32[32,1,1,2]{3,0,2,1:T(8,128)S(1)}, s32[32,1,1,2]{3,0,2,1:T(8,128)}, u32[]{:S(2)}) copy-start(s32[32,1,1,2]{3,0,2,1:T(8,128)} %copy-done.5) | copy-start | bytes 772
  148.1 34.7 %copy-start.11 = (s32[2]{0:T(128)S(1)}, s32[2]{0:T(128)}, u32[]{:S(2)}) copy-start(s32[2]{0:T(128)} %copy-done.10) | copy-start | bytes 28
  148.1 34.7 %copy-start.13 = (s32[32]{0:T(128)S(1)}, s32[32]{0:T(128)}, u32[]{:S(2)}) copy-start(s32[32]{0:T(128)} %copy-done.12) | copy-start | bytes 388
  148.1 45.6 %copy-start.9 = (pred[32,256]{1,0:T(8,128)(4,1)S(1)}, pred[32,256]{1,0:T(8,128)(4,1)}, u32[]{:S(2)}) copy-start(pred[32,256]{1,0:T(8,128)(4,1)} %copy-done.8) | copy-start | bytes 24580
  149.7 44.0 %all-to-all-start.1 = ((f32[32,1,8,256]{3,2,1,0:T(8,128)}), f32[32,1,8,256]{3,2,1,0:T(8,128)S(1)}, u32[]{:S(2)}, u32[]{:S(2)}) async-start(f32[32,1,8,256]{3,2,1,0:T(8,128)} %slice_select_fusion), calls=%async_computation.1 | async-start | bytes 524288 | tf_op jit(solution)/shard_map/all_to_all | solution.py:477

commit v7 on v5

--- a/solution.py
+++ b/solution.py
@@ -178,9 +178,15 @@
     return (group // GROUP_ROW * 2 + group % 2) % X_CHIPS
 
 
+def mirror(group):
+    return group % 2
+
+
 def block_of(group, sub):
     cross = crossing(group)
-    x, half = sub // 2, sub % 2
+    x, side = sub // 2, sub % 2
+    flip = mirror(group)
+    half = side + flip - 2 * side * flip
     low = (x - cross + 2 * X_CHIPS - 1) % X_CHIPS
     high = X_CHIPS + (cross - x + X_CHIPS) % X_CHIPS
     return (1 - half) * low + half * high
@@ -191,7 +197,9 @@
     half = block // X_CHIPS
     low = (cross + 1 + block) % X_CHIPS
     high = (cross - block + 2 * X_CHIPS) % X_CHIPS
-    return ((1 - half) * low + half * high) * 2 + half
+    flip = mirror(group)
+    side = half + flip - 2 * half * flip
+    return ((1 - half) * low + half * high) * 2 + side
 
 
 def shift_rows(c, k, rows):

time: 172 us -> 150 us (0.87)
  starting transfers between devices: 63.7 us -> 42 us
  waiting for transfers between devices: 43.3 us -> 40.3 us
  Pallas kernels: 29.3 us -> 31.5 us
    ppermute x1, waiting for transfers between devices: 2.41 us -> 24 us  [body(): model = lax.ppermute(model, ('shot', 'sub'), outbound)]
    ppermute x1, waiting for transfers between devices: 19.9 us -> 0.29 us  [body(): states_moved.append(lax.ppermute(states, ('shot', 'sub'), outbound))]
    all_to_all x1, starting transfers between devices: 37.5 us -> 22.1 us  [body(): lax.all_to_all(images[0], 'shot', split_axis=0, concat_axis=0, tiled=True)]
    ppermute x1, waiting for transfers between devices: 10.3 us -> 3.42 us  [body(): image = lax.ppermute(image, ('shot', 'sub'), [(b, a) for a, b in outbound])]
    ppermute x1, starting transfers between devices: 6.08 us -> 2.15 us  [body(): states_moved.append(lax.ppermute(states, ('shot', 'sub'), outbound))]
    ppermute x1, starting transfers between devices: 6.67 us -> 4.25 us  [body(): image = lax.ppermute(image, ('shot', 'sub'), [(b, a) for a, b in outbound])]
    pallas_call x1, Pallas kernels: 29.3 us -> 31.5 us  [migrate(): pl.pallas_call(migrate_kernel, out_shape=jax.ShapeDtypeStruct(model.shape...]
    all_to_all x1, waiting for transfers between devices: 0.01 us -> 1.92 us  [body(): lax.all_to_all(sending, 'shot', split_axis=0, concat_axis=0, tiled=True)]
  transfers between devices with their start and end apart: 5 -> 5, of which waited for: 4 -> 5; matrix products, arithmetic and copies ran while one was open for 9% -> 11% of each run, Pallas kernels for 0% -> 0%
where the time goes in v7:
time: 150 us; the launch traced here: 149 us
  starting transfers between devices  42 us (28%)
  waiting for transfers between devices  40.3 us (27%)
  Pallas kernels  31.5 us (21%)
  local copies, waits for them, and re-layouts  22.7 us (15%)
  other arithmetic  8.11 us (5%)
  between operations  3.75 us (2%)
    pallas_call x1, Pallas kernels, migrate(): pl.pallas_call(migrate_kernel, out_shape=jax.ShapeDtypeStruct(model.shape...  31.5 us
    ppermute x1, waiting for transfers between devices, body(): model = lax.ppermute(model, ('shot', 'sub'), outbound)  24 us
    all_to_all x1, starting transfers between devices, body(): lax.all_to_all(images[0], 'shot', split_axis=0, concat_axis=0, tiled=True)  22.1 us
    all_to_all x1, waiting for transfers between devices, body(): lax.all_to_all(images[0], 'shot', split_axis=0, concat_axis=0, tiled=True)  10.7 us
    all_to_all x1, starting transfers between devices, body(): lax.all_to_all(sending, 'shot', split_axis=0, concat_axis=0, tiled=True)  9.36 us
    ppermute x1, starting transfers between devices, body(): image = lax.ppermute(image, ('shot', 'sub'), [(b, a) for a, b in outbound])  4.25 us
    ppermute x1, starting transfers between devices, body(): model = lax.ppermute(model, ('shot', 'sub'), outbound)  4.17 us
    ppermute x1, waiting for transfers between devices, body(): image = lax.ppermute(image, ('shot', 'sub'), [(b, a) for a, b in outbound])  3.42 us
  transfers between devices with their start and end apart: 5, of which 5 were waited for; matrix products, arithmetic and copies ran while one was open for 11% of the time, Pallas kernels for 0%

profile of v7, /device:TPU:5, one launch (start us, length us, event | category | flops | bytes accessed | tf_op | source)
XLA Modules:
  0.0 148.8 jit_solution(7786951529074303392)
XLA Ops:
  0.0 1.3 dynamic_slice.9
  3.3 0.7 and_select_fusion.14
  4.2 0.7 fusion.22
  6.0 0.6 gather_fusion
  6.9 0.7 slice_select_fusion.1
  7.6 9.4 %all-to-all-start = ((f32[32,1,8,256]{3,2,1,0:T(8,128)}), f32[32,1,8,256]{3,2,1,0:T(8,128)S(1)}, u32[]{:S(2)}, u32[]{:S(2)}) async-start(f32[32,1,8,256]{3,2,1,0:T(8,128)} %slice_select_fusion.1), calls=%async_computation | async-start | bytes 524288 | tf_op jit(solution)/shard_map/all_to_all | solution.py:460
  17.0 1.0 maximum_convert_fusion
  18.0 2.2 %collective-permute-start.1 = (f32[4,8,64,128]{3,2,1,0:T(8,128)}, f32[4,8,64,128]{3,2,1,0:T(8,128)}, u32[]{:S(2)}, u32[]{:S(2)}) collective-permute-start(f32[4,8,64,128]{3,2,1,0:T(8,128)} %maximum_convert_fusion), channel_id=1, source_target_pairs={{0,2},{1,4},{2,6},{3,0},{4,1},{5,7},{6,5},{7,3},{8,13},{9,15},{10,... | collective-permute-start | bytes 3145736 | tf_op jit(solution)/shard_map/ppermute | solution.py:456
  20.8 0.7 fusion.11
  21.7 0.7 fusion.13
  23.7 0.7 pad_add_fusion.1.src_ref
  24.5 0.8 copy.18
  25.4 0.7 add_select_fusion.rcol_ref
  26.1 1.9 %all-to-all-done = f32[32,1,8,256]{3,2,1,0:T(8,128)S(1)} async-done(((f32[32,1,8,256]{3,2,1,0:T(8,128)}), f32[32,1,8,256]{3,2,1,0:T(8,128)S(1)}, u32[]{:S(2)}, u32[]{:S(2)}) %all-to-all-start) | async-done | bytes 262176 | tf_op jit(solution)/shard_map/all_to_all | solution.py:460
  28.7 0.7 reshape.707
  29.4 2.5 %copy.20 = f32[8,4,16,9,16]{2,1,4,3,0:T(4,128)} copy(f32[8,4,16,9,16]{4,2,0,3,1:T(8,128)S(1)} %bitcast.73) | data formatting | bytes 589824 | tf_op jit(solution)/shard_map/transpose | solution.py:151
  31.9 2.5 %reshape.708 = f32[8,64,144]{1,2,0:T(8,128)S(1)} reshape(f32[8,4,16,9,16]{2,1,4,3,0:T(4,128)} %copy.20) | data formatting | bytes 589824 | tf_op jit(solution)/shard_map/reshape | solution.py:151
  34.7 4.2 %collective-permute-start = (f32[8,64,128]{2,1,0:T(8,128)S(1)}, f32[8,64,128]{2,1,0:T(8,128)S(1)}, u32[]{:S(2)}, u32[]{:S(2)}) collective-permute-start(f32[8,64,128]{2,1,0:T(8,128)S(1)} %copy.26), channel_id=1, source_target_pairs={{0,2},{1,4},{2,6},{3,0},{4,1},{5,7},{6,5},{7,3},{8,13},{9,15},{10,... | collective-permute-start | bytes 786440 | tf_op jit(solution)/shard_map/ppermute | solution.py:467
  39.1 2.3 %fusion.23 = (f32[2,8,64,128]{3,2,1,0:T(8,128)}, f32[2,8,64,128]{3,2,1,0:T(8,128)}) fusion(f32[4,8,64,128]{3,2,1,0:T(8,128)} %collective-permute-done.1), kind=kLoop, calls=%fused_computation.109 | loop fusion | bytes 2097152 | tf_op jit(solution)/shard_map/slice | solution.py:472
  41.4 24.0 %collective-permute-done.model_ref = f32[8,64,128]{2,1,0:T(8,128)S(1)} collective-permute-done((f32[8,64,128]{2,1,0:T(8,128)S(1)}, f32[8,64,128]{2,1,0:T(8,128)S(1)}, u32[]{:S(2)}, u32[]{:S(2)}) %collective-permute-start) | collective-permute-done | bytes 262176 | tf_op jit(solution)/shard_map/ppermute | solution.py:467
  65.4 0.7 copy-done.3
  66.1 31.5 %shard_map.91 = f32[8,64,128]{2,1,0:T(8,128)} custom-call(s32[3]{0:T(128)} %pad_add_fusion.1.src_ref, f32[4]{0:T(128)} %bitcast.83, s32[2,256]{1,0:T(2,128)} %pad_add_fusion.rrow_ref, s32[256,1]{1,0:T(8,128)} %add_select_fusion.rcol_ref, f32[256,4]{1,0:T(8,128)} %bitcast.79, f32[8,64,128]{2,1,0:T(8,128)} %copy-done.3, ...), custom_call_target="tpu_custom_call" | custom-call | tf_op jit(solution)/shard_map/pallas_call | solution.py:400
  97.7 4.2 %collective-permute-start.2 = (f32[8,64,128]{2,1,0:T(8,128)}, f32[8,64,128]{2,1,0:T(8,128)S(1)}, u32[]{:S(2)}, u32[]{:S(2)}) collective-permute-start(f32[8,64,128]{2,1,0:T(8,128)} %shard_map.91), channel_id=1, source_target_pairs={{2,0},{4,1},{6,2},{0,3},{1,4},{7,5},{5,6},{3,7},{13,8},{15,9},{9,1... | collective-permute-start | bytes 786440 | tf_op jit(solution)/shard_map/ppermute | solution.py:478
  102.1 3.4 %collective-permute-done.2 = f32[8,64,128]{2,1,0:T(8,128)S(1)} collective-permute-done((f32[8,64,128]{2,1,0:T(8,128)}, f32[8,64,128]{2,1,0:T(8,128)S(1)}, u32[]{:S(2)}, u32[]{:S(2)}) %collective-permute-start.2) | collective-permute-done | bytes 262176 | tf_op jit(solution)/shard_map/ppermute | solution.py:478
  105.8 1.1 dynamic_update_slice.3
  106.9 1.0 reshape.709
  107.9 2.5 %copy.23 = f32[4,9,8,16,16]{4,3,2,1,0:T(8,128)} copy(f32[4,9,8,16,16]{3,0,4,1,2:T(4,128)S(1)} %bitcast.74) | data formatting | bytes 589824 | tf_op jit(solution)/shard_map/transpose | solution.py:160
  110.4 2.5 %reshape.710 = f32[36,8,256]{2,1,0:T(8,128)S(1)} reshape(f32[4,9,8,16,16]{4,3,2,1,0:T(8,128)} %copy.23) | data formatting | bytes 589824 | tf_op jit(solution)/shard_map/reshape | solution.py:160
  113.7 0.7 slice_select_fusion
  114.4 22.1 %all-to-all-start.1 = ((f32[32,1,8,256]{3,2,1,0:T(8,128)}), f32[32,1,8,256]{3,2,1,0:T(8,128)S(1)}, u32[]{:S(2)}, u32[]{:S(2)}) async-start(f32[32,1,8,256]{3,2,1,0:T(8,128)} %slice_select_fusion), calls=%async_computation.1 | async-start | bytes 524288 | tf_op jit(solution)/shard_map/all_to_all | solution.py:480
  136.9 10.7 %all-to-all-done.1 = f32[32,1,8,256]{3,2,1,0:T(8,128)S(1)} async-done(((f32[32,1,8,256]{3,2,1,0:T(8,128)}), f32[32,1,8,256]{3,2,1,0:T(8,128)S(1)}, u32[]{:S(2)}, u32[]{:S(2)}) %all-to-all-start.1) | async-done | bytes 262176 | tf_op jit(solution)/shard_map/all_to_all | solution.py:480
  148.1 0.7 copy.25
  (58 shorter events, 5.7 us)
Async XLA Ops:
  0.0 6.0 %copy-start = (f32[12,8,256]{2,1,0:T(8,128)S(1)}, f32[12,8,256]{2,1,0:T(8,128)}, u32[]{:S(2)}) copy-start(f32[12,8,256]{2,1,0:T(8,128)} %param.9) | copy-start | bytes 294916
  0.0 17.0 %copy-start.2 = (bf16[1,2,8,64,128]{4,3,2,1,0:T(8,128)(2,1)S(1)}, bf16[1,2,8,64,128]{4,3,2,1,0:T(8,128)(2,1)}, u32[]{:S(2)}) copy-start(bf16[1,2,8,64,128]{4,3,2,1,0:T(8,128)(2,1)} %param.10) | copy-start | bytes 786436
  0.0 17.0 %copy-start.1 = (bf16[1,2,8,64,128]{4,3,2,1,0:T(8,128)(2,1)S(1)}, bf16[1,2,8,64,128]{4,3,2,1,0:T(8,128)(2,1)}, u32[]{:S(2)}) copy-start(bf16[1,2,8,64,128]{4,3,2,1,0:T(8,128)(2,1)} %param.11) | copy-start | bytes 786436
  6.0 14.2 %copy-start.6 = (s32[32]{0:T(128)S(1)}, s32[32]{0:T(128)}, u32[]{:S(2)}) copy-start(s32[32]{0:T(128)} %param.16) | copy-start | bytes 388
  6.0 15.7 %copy-start.4 = (s32[1,256]{1,0:T(1,128)S(1)}, s32[1,256]{1,0:T(1,128)}, u32[]{:S(2)}) copy-start(s32[1,256]{1,0:T(1,128)} %param.14) | copy-start | bytes 3076
  6.6 17.9 %copy-start.5 = (f32[1,4,256]{2,1,0:T(4,128)S(1)}, f32[1,4,256]{2,1,0:T(4,128)}, u32[]{:S(2)}) copy-start(f32[1,4,256]{2,1,0:T(4,128)} %param.15) | copy-start | bytes 12292
  7.6 20.5 %all-to-all-start = ((f32[32,1,8,256]{3,2,1,0:T(8,128)}), f32[32,1,8,256]{3,2,1,0:T(8,128)S(1)}, u32[]{:S(2)}, u32[]{:S(2)}) async-start(f32[32,1,8,256]{3,2,1,0:T(8,128)} %slice_select_fusion.1), calls=%async_computation | async-start | bytes 524288 | tf_op jit(solution)/shard_map/all_to_all | solution.py:460
  18.0 21.1 %collective-permute-start.1 = (f32[4,8,64,128]{3,2,1,0:T(8,128)}, f32[4,8,64,128]{3,2,1,0:T(8,128)}, u32[]{:S(2)}, u32[]{:S(2)}) collective-permute-start(f32[4,8,64,128]{3,2,1,0:T(8,128)} %maximum_convert_fusion), channel_id=1, source_target_pairs={{0,2},{1,4},{2,6},{3,0},{4,1},{5,7},{6,5},{7,3},{8,13},{9,15},{10,... | collective-permute-start | bytes 3145736 | tf_op jit(solution)/shard_map/ppermute | solution.py:456
  34.7 30.8 %collective-permute-start = (f32[8,64,128]{2,1,0:T(8,128)S(1)}, f32[8,64,128]{2,1,0:T(8,128)S(1)}, u32[]{:S(2)}, u32[]{:S(2)}) collective-permute-start(f32[8,64,128]{2,1,0:T(8,128)S(1)} %copy.26), channel_id=1, source_target_pairs={{0,2},{1,4},{2,6},{3,0},{4,1},{5,7},{6,5},{7,3},{8,13},{9,15},{10,... | collective-permute-start | bytes 786440 | tf_op jit(solution)/shard_map/ppermute | solution.py:467
  65.4 0.7 copy-start.3
  97.7 7.9 %collective-permute-start.2 = (f32[8,64,128]{2,1,0:T(8,128)}, f32[8,64,128]{2,1,0:T(8,128)S(1)}, u32[]{:S(2)}, u32[]{:S(2)}) collective-permute-start(f32[8,64,128]{2,1,0:T(8,128)} %shard_map.91), channel_id=1, source_target_pairs={{2,0},{4,1},{6,2},{0,3},{1,4},{7,5},{5,6},{3,7},{13,8},{15,9},{9,1... | collective-permute-start | bytes 786440 | tf_op jit(solution)/shard_map/ppermute | solution.py:478
  114.4 33.2 %all-to-all-start.1 = ((f32[32,1,8,256]{3,2,1,0:T(8,128)}), f32[32,1,8,256]{3,2,1,0:T(8,128)S(1)}, u32[]{:S(2)}, u32[]{:S(2)}) async-start(f32[32,1,8,256]{3,2,1,0:T(8,128)} %slice_select_fusion), calls=%async_computation.1 | async-start | bytes 524288 | tf_op jit(solution)/shard_map/all_to_all | solution.py:480

commit v8 on v7

--- a/solution.py
+++ b/solution.py
@@ -241,10 +241,11 @@
 
 def migrate_kernel(
     src_ref, wave_ref, rrow_ref, rcol_ref, resid_ref, model_ref, pf_ref, qa_ref,
-    img_ref, pad_p, pad_q, lap, qs, inject, send_sem, recv_sem,
+    img_ref, pad_p, pad_q, lap, qs, inject, model_scr, send_sem, recv_sem, model_sem,
 ):
     group = lax.axis_index("shot")
-    me = block_of(group, lax.axis_index("sub"))
+    sub = lax.axis_index("sub")
+    me = block_of(group, sub)
     n_sub = lax.axis_size("sub")
     depth = model_ref.shape[0]
     halo = jnp.zeros((RADIUS, AX, AY), jnp.float32)
@@ -253,13 +254,42 @@
             buf[r, 0:RADIUS] = halo
             buf[r, RADIUS + depth : 2 * RADIUS + depth] = halo
     pad_p[0, RADIUS : RADIUS + depth] = pf_ref[0]
-    pad_q[0, RADIUS : RADIUS + depth] = model_ref[...] * qa_ref[0]
     up_dev = device_of(group, (me + 1) % n_sub)
     down_dev = device_of(group, (me + n_sub - 1) % n_sub)
+    target = device_of(group, sub)
+    moved = target != sub
+    mesh_id = pl.DeviceIdType.MESH
     barrier = pltpu.get_barrier_semaphore()
-    pl.semaphore_signal(barrier, 1, device_id={"sub": up_dev}, device_id_type=pl.DeviceIdType.MESH)
-    pl.semaphore_signal(barrier, 1, device_id={"sub": down_dev}, device_id_type=pl.DeviceIdType.MESH)
-    pl.semaphore_wait(barrier, 2)
+    pl.semaphore_signal(barrier, 1, device_id={"sub": up_dev}, device_id_type=mesh_id)
+    pl.semaphore_signal(barrier, 1, device_id={"sub": down_dev}, device_id_type=mesh_id)
+
+    @pl.when(moved)
+    def _():
+        pl.semaphore_signal(barrier, 1, device_id={"sub": target}, device_id_type=mesh_id)
+        pl.semaphore_signal(barrier, 1, device_id={"sub": me}, device_id_type=mesh_id)
+        pl.semaphore_wait(barrier, 4)
+
+    @pl.when(jnp.logical_not(moved))
+    def _():
+        pl.semaphore_wait(barrier, 2)
+
+    model_copy = pltpu.make_async_remote_copy(
+        src_ref=model_ref,
+        dst_ref=model_scr,
+        send_sem=model_sem.at[0],
+        recv_sem=model_sem.at[1],
+        device_id={"sub": target},
+        device_id_type=mesh_id,
+    )
+    model_local = pltpu.make_async_copy(model_ref, model_scr, model_sem.at[2])
+
+    @pl.when(moved)
+    def _():
+        model_copy.start()
+
+    @pl.when(jnp.logical_not(moved))
+    def _():
+        model_local.start()
     rows = lax.broadcasted_iota(jnp.int32, (AX, AY), 0)
     lanes = lax.broadcasted_iota(jnp.int32, (AX, AY), 1)
     n_rec = rcol_ref.shape[0]
@@ -332,7 +362,7 @@
             lap[r, j] = lp
             if r < NT - 1:
                 before = pf_ref[1, j] if r == 0 else pad_p[r - 1, p]
-                following = 2.0 * pad_p[r, p] - before + model_ref[j] * lp
+                following = 2.0 * pad_p[r, p] - before + model_scr[j] * lp
                 source = jnp.where(src_spot & (src_level == j), wave_ref[r], 0.0)
                 pad_p[r + 1, p] = following + source
             return carry
@@ -354,7 +384,7 @@
             result = result + inject[j]
             if r < NT - 1:
                 qs[r, j] = result
-                pad_q[r + 1, p] = model_ref[j] * result
+                pad_q[r + 1, p] = model_scr[j] * result
             else:
                 image = jnp.zeros((AX, AY), jnp.float32)
                 for s in range(NT - 1):
@@ -366,6 +396,17 @@
         lax.fori_loop(0, depth, plane, 0)
 
     fwd = exchange(0, 0)
+
+    @pl.when(moved)
+    def _():
+        model_copy.wait_send()
+        model_copy.wait_recv()
+
+    @pl.when(jnp.logical_not(moved))
+    def _():
+        model_local.wait()
+
+    pad_q[0, RADIUS : RADIUS + depth] = model_scr[...] * qa_ref[0]
     adj = exchange(0, 1)
     build_injection(NT - 1)
     for r in range(NT):
@@ -408,8 +449,10 @@
             pltpu.VMEM(field, jnp.float32),
             pltpu.VMEM(field, jnp.float32),
             pltpu.VMEM(model.shape, jnp.float32),
+            pltpu.VMEM(model.shape, jnp.float32),
             pltpu.SemaphoreType.DMA((NT, 2, 2)),
             pltpu.SemaphoreType.DMA((NT, 2, 2)),
+            pltpu.SemaphoreType.DMA((3,)),
         ],
         compiler_params=pltpu.CompilerParams(collective_id=0, has_side_effects=True),
     )(
@@ -464,7 +507,6 @@
         row_start = aperture_row[shot_id]
         col_start = aperture_col[shot_id]
         model = assemble(fetched, row_start, col_start, own_cols)
-        model = lax.ppermute(model, ("shot", "sub"), outbound)
         states = states_moved[k]
         image = migrate(
             model,

time: 150 us -> 156 us (1.040); the launches traced: 149 us -> 153 us
  Pallas kernels: 31.5 us -> 49.3 us
  waiting for transfers between devices: 40.3 us -> 22.6 us
  starting transfers between devices: 42 us -> 46.4 us
    ppermute x1 -> x0, waiting for transfers between devices: 24 us -> none  [body(): model = lax.ppermute(model, ('shot', 'sub'), outbound)]
    pallas_call x1, Pallas kernels: 31.5 us -> 49.3 us  [migrate(): pl.pallas_call(migrate_kernel, out_shape=jax.ShapeDtypeStruct(model.shape...]
    ppermute x1, starting transfers between devices: 4.25 us -> 11.4 us  [body(): image = lax.ppermute(image, ('shot', 'sub'), [(b, a) for a, b in outbound])]
    ppermute x1 -> x0, starting transfers between devices: 4.17 us -> none  [body(): model = lax.ppermute(model, ('shot', 'sub'), outbound)]
    ppermute x1, waiting for transfers between devices: 0.29 us -> 3.75 us  [body(): states_moved.append(lax.ppermute(states, ('shot', 'sub'), outbound))]
    ppermute x1, waiting for transfers between devices: 3.42 us -> 6.13 us  [body(): image = lax.ppermute(image, ('shot', 'sub'), [(b, a) for a, b in outbound])]
  transfers between devices with their start and end apart: 5 -> 4, of which waited for: 5 -> 4; matrix products, arithmetic and copies ran while one was open for 11% -> 9% of each run, Pallas kernels for 0% -> 0%
where the time goes in v8:
time: 156 us; the launch traced here: 153 us
  Pallas kernels  49.3 us (32%)
  starting transfers between devices  46.4 us (30%)
  local copies, waits for them, and re-layouts  22.7 us (15%)
  waiting for transfers between devices  22.6 us (14%)
  other arithmetic  8.03 us (5%)
  between operations  3.74 us (2%)
    pallas_call x1, Pallas kernels, migrate(): pl.pallas_call(migrate_kernel, out_shape=jax.ShapeDtypeStruct(model.shape...  49.3 us
    all_to_all x1, starting transfers between devices, body(): lax.all_to_all(images[0], 'shot', split_axis=0, concat_axis=0, tiled=True)  23.4 us
    ppermute x1, starting transfers between devices, body(): image = lax.ppermute(image, ('shot', 'sub'), [(b, a) for a, b in outbound])  11.4 us
    all_to_all x1, waiting for transfers between devices, body(): lax.all_to_all(images[0], 'shot', split_axis=0, concat_axis=0, tiled=True)  10.7 us
    all_to_all x1, starting transfers between devices, body(): lax.all_to_all(sending, 'shot', split_axis=0, concat_axis=0, tiled=True)  9.36 us
    ppermute x1, waiting for transfers between devices, body(): image = lax.ppermute(image, ('shot', 'sub'), [(b, a) for a, b in outbound])  6.13 us
    ppermute x1, waiting for transfers between devices, body(): states_moved.append(lax.ppermute(states, ('shot', 'sub'), outbound))  3.75 us
  transfers between devices with their start and end apart: 4, of which 4 were waited for; matrix products, arithmetic and copies ran while one was open for 9% of the time, Pallas kernels for 0%

profile of v8, /device:TPU:5, one launch (start us, length us, event | category | flops | bytes accessed | tf_op | source)
XLA Modules:
  0.0 153.1 jit_solution(7299088366938316850)
XLA Ops:
  0.0 1.3 dynamic_slice.9
  3.3 0.7 and_select_fusion.14
  4.2 0.7 fusion.22
  6.0 0.6 gather_fusion
  6.9 0.7 slice_select_fusion.1
  7.6 9.4 %all-to-all-start = ((f32[32,1,8,256]{3,2,1,0:T(8,128)}), f32[32,1,8,256]{3,2,1,0:T(8,128)S(1)}, u32[]{:S(2)}, u32[]{:S(2)}) async-start(f32[32,1,8,256]{3,2,1,0:T(8,128)} %slice_select_fusion.1), calls=%async_computation | async-start | bytes 524288 | tf_op jit(solution)/shard_map/all_to_all | solution.py:503
  17.0 1.0 maximum_convert_fusion
  18.0 2.2 %collective-permute-start = (f32[4,8,64,128]{3,2,1,0:T(8,128)}, f32[4,8,64,128]{3,2,1,0:T(8,128)}, u32[]{:S(2)}, u32[]{:S(2)}) collective-permute-start(f32[4,8,64,128]{3,2,1,0:T(8,128)} %maximum_convert_fusion), channel_id=1, source_target_pairs={{0,2},{1,4},{2,6},{3,0},{4,1},{5,7},{6,5},{7,3},{8,13},{9,15},{10,... | collective-permute-start | bytes 3145736 | tf_op jit(solution)/shard_map/ppermute | solution.py:499
  20.8 0.7 fusion.11
  21.6 0.7 fusion.13
  24.4 0.8 copy.18
  25.4 0.7 add_select_fusion.rcol_ref
  26.1 2.0 %all-to-all-done = f32[32,1,8,256]{3,2,1,0:T(8,128)S(1)} async-done(((f32[32,1,8,256]{3,2,1,0:T(8,128)}), f32[32,1,8,256]{3,2,1,0:T(8,128)S(1)}, u32[]{:S(2)}, u32[]{:S(2)}) %all-to-all-start) | async-done | bytes 262176 | tf_op jit(solution)/shard_map/all_to_all | solution.py:503
  28.1 0.6 gather_fusion.1
  28.7 0.7 reshape.707
  29.4 2.5 %copy.20 = f32[8,4,16,9,16]{2,1,4,3,0:T(4,128)} copy(f32[8,4,16,9,16]{4,2,0,3,1:T(8,128)S(1)} %bitcast.73) | data formatting | bytes 589824 | tf_op jit(solution)/shard_map/transpose | solution.py:151
  31.9 2.5 %reshape.708 = f32[8,64,144]{1,2,0:T(8,128)S(1)} reshape(f32[8,4,16,9,16]{2,1,4,3,0:T(4,128)} %copy.20) | data formatting | bytes 589824 | tf_op jit(solution)/shard_map/reshape | solution.py:151
  34.5 0.9 copy.26.model_ref
  35.4 3.8 %collective-permute-done = f32[4,8,64,128]{3,2,1,0:T(8,128)} collective-permute-done((f32[4,8,64,128]{3,2,1,0:T(8,128)}, f32[4,8,64,128]{3,2,1,0:T(8,128)}, u32[]{:S(2)}, u32[]{:S(2)}) %collective-permute-start) | collective-permute-done | bytes 1048608 | tf_op jit(solution)/shard_map/ppermute | solution.py:499
  39.1 2.3 %fusion.23 = (f32[2,8,64,128]{3,2,1,0:T(8,128)}, f32[2,8,64,128]{3,2,1,0:T(8,128)}) fusion(f32[4,8,64,128]{3,2,1,0:T(8,128)} %collective-permute-done), kind=kLoop, calls=%fused_computation.109 | loop fusion | bytes 2097152 | tf_op jit(solution)/shard_map/slice | solution.py:514
  41.4 49.3 %shard_map.91 = f32[8,64,128]{2,1,0:T(8,128)} custom-call(s32[3]{0:T(128)} %pad_add_fusion.1.src_ref, f32[4]{0:T(128)} %bitcast.83, s32[2,256]{1,0:T(2,128)} %pad_add_fusion.rrow_ref, s32[256,1]{1,0:T(8,128)} %add_select_fusion.rcol_ref, f32[256,4]{1,0:T(8,128)} %bitcast.79, f32[8,64,128]{2,1,0:T(8,128)} %copy.26.model_ref, ...), custom_call_target="tpu_custom_call" | custom-call | tf_op jit(solution)/shard_map/pallas_call | solution.py:441
  90.7 11.4 %collective-permute-start.1 = (f32[8,64,128]{2,1,0:T(8,128)}, f32[8,64,128]{2,1,0:T(8,128)S(1)}, u32[]{:S(2)}, u32[]{:S(2)}) collective-permute-start(f32[8,64,128]{2,1,0:T(8,128)} %shard_map.91), channel_id=1, source_target_pairs={{2,0},{4,1},{6,2},{0,3},{1,4},{7,5},{5,6},{3,7},{13,8},{15,9},{9,1... | collective-permute-start | bytes 786440 | tf_op jit(solution)/shard_map/ppermute | solution.py:520
  102.4 6.1 %collective-permute-done.1 = f32[8,64,128]{2,1,0:T(8,128)S(1)} collective-permute-done((f32[8,64,128]{2,1,0:T(8,128)}, f32[8,64,128]{2,1,0:T(8,128)S(1)}, u32[]{:S(2)}, u32[]{:S(2)}) %collective-permute-start.1) | collective-permute-done | bytes 262176 | tf_op jit(solution)/shard_map/ppermute | solution.py:520
  108.7 1.1 dynamic_update_slice.3
  109.9 1.0 reshape.709
  110.9 2.5 %copy.23 = f32[4,9,8,16,16]{4,3,2,1,0:T(8,128)} copy(f32[4,9,8,16,16]{3,0,4,1,2:T(4,128)S(1)} %bitcast.74) | data formatting | bytes 589824 | tf_op jit(solution)/shard_map/transpose | solution.py:160
  113.3 2.5 %reshape.710 = f32[36,8,256]{2,1,0:T(8,128)S(1)} reshape(f32[4,9,8,16,16]{4,3,2,1,0:T(8,128)} %copy.23) | data formatting | bytes 589824 | tf_op jit(solution)/shard_map/reshape | solution.py:160
  115.9 0.6 gather_fusion.2
  116.7 0.7 slice_select_fusion
  117.4 23.4 %all-to-all-start.1 = ((f32[32,1,8,256]{3,2,1,0:T(8,128)}), f32[32,1,8,256]{3,2,1,0:T(8,128)S(1)}, u32[]{:S(2)}, u32[]{:S(2)}) async-start(f32[32,1,8,256]{3,2,1,0:T(8,128)} %slice_select_fusion), calls=%async_computation.1 | async-start | bytes 524288 | tf_op jit(solution)/shard_map/all_to_all | solution.py:522
  141.2 10.7 %all-to-all-done.1 = f32[32,1,8,256]{3,2,1,0:T(8,128)S(1)} async-done(((f32[32,1,8,256]{3,2,1,0:T(8,128)}), f32[32,1,8,256]{3,2,1,0:T(8,128)S(1)}, u32[]{:S(2)}, u32[]{:S(2)}) %all-to-all-start.1) | async-done | bytes 262176 | tf_op jit(solution)/shard_map/all_to_all | solution.py:522
  152.4 0.7 copy.25
  (54 shorter events, 4.6 us)
Async XLA Ops:
  0.0 6.0 %copy-start = (f32[12,8,256]{2,1,0:T(8,128)S(1)}, f32[12,8,256]{2,1,0:T(8,128)}, u32[]{:S(2)}) copy-start(f32[12,8,256]{2,1,0:T(8,128)} %param.9) | copy-start | bytes 294916
  0.0 17.0 %copy-start.2 = (bf16[1,2,8,64,128]{4,3,2,1,0:T(8,128)(2,1)S(1)}, bf16[1,2,8,64,128]{4,3,2,1,0:T(8,128)(2,1)}, u32[]{:S(2)}) copy-start(bf16[1,2,8,64,128]{4,3,2,1,0:T(8,128)(2,1)} %param.10) | copy-start | bytes 786436
  0.0 17.0 %copy-start.1 = (bf16[1,2,8,64,128]{4,3,2,1,0:T(8,128)(2,1)S(1)}, bf16[1,2,8,64,128]{4,3,2,1,0:T(8,128)(2,1)}, u32[]{:S(2)}) copy-start(bf16[1,2,8,64,128]{4,3,2,1,0:T(8,128)(2,1)} %param.11) | copy-start | bytes 786436
  6.0 14.2 %copy-start.5 = (s32[32]{0:T(128)S(1)}, s32[32]{0:T(128)}, u32[]{:S(2)}) copy-start(s32[32]{0:T(128)} %param.16) | copy-start | bytes 388
  6.0 15.6 %copy-start.3 = (s32[1,256]{1,0:T(1,128)S(1)}, s32[1,256]{1,0:T(1,128)}, u32[]{:S(2)}) copy-start(s32[1,256]{1,0:T(1,128)} %param.14) | copy-start | bytes 3076
  6.6 17.8 %copy-start.4 = (f32[1,4,256]{2,1,0:T(4,128)S(1)}, f32[1,4,256]{2,1,0:T(4,128)}, u32[]{:S(2)}) copy-start(f32[1,4,256]{2,1,0:T(4,128)} %param.15) | copy-start | bytes 12292
  7.6 20.5 %all-to-all-start = ((f32[32,1,8,256]{3,2,1,0:T(8,128)}), f32[32,1,8,256]{3,2,1,0:T(8,128)S(1)}, u32[]{:S(2)}, u32[]{:S(2)}) async-start(f32[32,1,8,256]{3,2,1,0:T(8,128)} %slice_select_fusion.1), calls=%async_computation | async-start | bytes 524288 | tf_op jit(solution)/shard_map/all_to_all | solution.py:503
  18.0 21.1 %collective-permute-start = (f32[4,8,64,128]{3,2,1,0:T(8,128)}, f32[4,8,64,128]{3,2,1,0:T(8,128)}, u32[]{:S(2)}, u32[]{:S(2)}) collective-permute-start(f32[4,8,64,128]{3,2,1,0:T(8,128)} %maximum_convert_fusion), channel_id=1, source_target_pairs={{0,2},{1,4},{2,6},{3,0},{4,1},{5,7},{6,5},{7,3},{8,13},{9,15},{10,... | collective-permute-start | bytes 3145736 | tf_op jit(solution)/shard_map/ppermute | solution.py:499
  90.7 17.8 %collective-permute-start.1 = (f32[8,64,128]{2,1,0:T(8,128)}, f32[8,64,128]{2,1,0:T(8,128)S(1)}, u32[]{:S(2)}, u32[]{:S(2)}) collective-permute-start(f32[8,64,128]{2,1,0:T(8,128)} %shard_map.91), channel_id=1, source_target_pairs={{2,0},{4,1},{6,2},{0,3},{1,4},{7,5},{5,6},{3,7},{13,8},{15,9},{9,1... | collective-permute-start | bytes 786440 | tf_op jit(solution)/shard_map/ppermute | solution.py:520
  117.4 34.5 %all-to-all-start.1 = ((f32[32,1,8,256]{3,2,1,0:T(8,128)}), f32[32,1,8,256]{3,2,1,0:T(8,128)S(1)}, u32[]{:S(2)}, u32[]{:S(2)}) async-start(f32[32,1,8,256]{3,2,1,0:T(8,128)} %slice_select_fusion), calls=%async_computation.1 | async-start | bytes 524288 | tf_op jit(solution)/shard_map/all_to_all | solution.py:522

commit v9 on v7

--- a/solution.py
+++ b/solution.py
@@ -448,12 +448,14 @@
     shots_here = forward_state.shape[0]
     gradient = jnp.zeros(velocity_tiles.shape, jnp.float32)
     every_shot = list(range(shots_here))
-    states_moved = []
-    for k in range(shots_here):
-        states = jnp.concatenate(
+    states = [
+        jnp.concatenate(
             [forward_state[k].astype(jnp.float32), adjoint_state[k].astype(jnp.float32)]
         )
-        states_moved.append(lax.ppermute(states, ("shot", "sub"), outbound))
+        for k in range(shots_here)
+    ]
+    velocity_tiles, states = lax.optimization_barrier((velocity_tiles, states))
+    states_moved = [lax.ppermute(s, ("shot", "sub"), outbound) for s in states]
     sending = outgoing(
         velocity_tiles, aperture_row, aperture_col, every_shot, groups, own_cols, caps
     )

time: 150 us -> 159 us (1.060)
  waiting for transfers between devices: 40.3 us -> 47.7 us
  starting transfers between devices: 42 us -> 40.3 us
    ppermute x1, waiting for transfers between devices: 24 us -> 28.7 us  [body(): model = lax.ppermute(model, ('shot', 'sub'), outbound)]
    all_to_all x1, starting transfers between devices: 22.1 us -> 18.2 us  [body(): lax.all_to_all(images[0], 'shot', split_axis=0, concat_axis=0, tiled=True)]
    ppermute x1, starting transfers between devices: 4.25 us -> 7.48 us  [body(): image = lax.ppermute(image, ('shot', 'sub'), [(b, a) for a, b in outbound])]
  transfers between devices with their start and end apart: 5 -> 5, of which waited for: 5 -> 5; matrix products, arithmetic and copies ran while one was open for 11% -> 9% of each run, Pallas kernels for 0% -> 0%
where the time goes in v9:
time: 159 us; the launch traced here: 156 us
  waiting for transfers between devices  47.7 us (30%)
  starting transfers between devices  40.3 us (25%)
  Pallas kernels  32.4 us (20%)
  local copies, waits for them, and re-layouts  22.7 us (14%)
  other arithmetic  9.07 us (6%)
  between operations  3.71 us (2%)
    pallas_call x1, Pallas kernels, migrate(): pl.pallas_call(migrate_kernel, out_shape=jax.ShapeDtypeStruct(model.shape...  32.4 us
    ppermute x1, waiting for transfers between devices, body(): model = lax.ppermute(model, ('shot', 'sub'), outbound)  28.7 us
    all_to_all x1, starting transfers between devices, body(): lax.all_to_all(images[0], 'shot', split_axis=0, concat_axis=0, tiled=True)  18.2 us
    all_to_all x1, waiting for transfers between devices, body(): lax.all_to_all(images[0], 'shot', split_axis=0, concat_axis=0, tiled=True)  10.8 us
    all_to_all x1, starting transfers between devices, body(): lax.all_to_all(sending, 'shot', split_axis=0, concat_axis=0, tiled=True)  9.36 us
    ppermute x1, starting transfers between devices, body(): image = lax.ppermute(image, ('shot', 'sub'), [(b, a) for a, b in outbound])  7.48 us
    ppermute x1, waiting for transfers between devices, body(): image = lax.ppermute(image, ('shot', 'sub'), [(b, a) for a, b in outbound])  3.42 us
  transfers between devices with their start and end apart: 5, of which 5 were waited for; matrix products, arithmetic and copies ran while one was open for 9% of the time, Pallas kernels for 0%

profile of v9, /device:TPU:5, one launch (start us, length us, event | category | flops | bytes accessed | tf_op | source)
XLA Modules:
  0.0 156.3 jit_solution(4205009052789597222)
XLA Ops:
  0.0 1.3 dynamic_slice.9
  3.2 0.7 and_select_fusion.14
  4.1 0.7 fusion.22
  5.0 2.1 %maximum_convert_fusion = f32[4,8,64,128]{3,2,1,0:T(8,128)} fusion(bf16[2,8,64,128]{3,2,1,0:T(8,128)(2,1)} %bitcast.80, bf16[2,8,64,128]{3,2,1,0:T(8,128)(2,1)} %bitcast.81), kind=kLoop, calls=%fused_computation.6 | loop fusion | flops 524288 | bytes 1572864 | tf_op jit(solution)/shard_map/concatenate | solution.py:452
  8.0 0.6 gather_fusion
  8.9 0.7 slice_select_fusion.1
  9.6 9.4 %all-to-all-start = ((f32[32,1,8,256]{3,2,1,0:T(8,128)}), f32[32,1,8,256]{3,2,1,0:T(8,128)S(1)}, u32[]{:S(2)}, u32[]{:S(2)}) async-start(f32[32,1,8,256]{3,2,1,0:T(8,128)} %slice_select_fusion.1), calls=%async_computation | async-start | bytes 524288 | tf_op jit(solution)/shard_map/all_to_all | solution.py:462
  19.0 2.2 %collective-permute-start.1 = (f32[4,8,64,128]{3,2,1,0:T(8,128)}, f32[4,8,64,128]{3,2,1,0:T(8,128)}, u32[]{:S(2)}, u32[]{:S(2)}) collective-permute-start(f32[4,8,64,128]{3,2,1,0:T(8,128)} %maximum_convert_fusion), channel_id=1, source_target_pairs={{0,2},{1,4},{2,6},{3,0},{4,1},{5,7},{6,5},{7,3},{8,13},{9,15},{10,... | collective-permute-start | bytes 3145736 | tf_op jit(solution)/shard_map/ppermute | solution.py:458
  21.8 0.7 fusion.11
  22.6 0.7 fusion.13
  25.4 0.8 copy.18
  26.3 0.7 add_select_fusion.rcol_ref
  27.0 3.0 %all-to-all-done = f32[32,1,8,256]{3,2,1,0:T(8,128)S(1)} async-done(((f32[32,1,8,256]{3,2,1,0:T(8,128)}), f32[32,1,8,256]{3,2,1,0:T(8,128)S(1)}, u32[]{:S(2)}, u32[]{:S(2)}) %all-to-all-start) | async-done | bytes 262176 | tf_op jit(solution)/shard_map/all_to_all | solution.py:462
  30.7 0.7 reshape.707
  31.4 2.5 %copy.20 = f32[8,4,16,9,16]{2,1,4,3,0:T(4,128)} copy(f32[8,4,16,9,16]{4,2,0,3,1:T(8,128)S(1)} %bitcast.73) | data formatting | bytes 589824 | tf_op jit(solution)/shard_map/transpose | solution.py:151
  33.9 2.5 %reshape.708 = f32[8,64,144]{1,2,0:T(8,128)S(1)} reshape(f32[8,4,16,9,16]{2,1,4,3,0:T(4,128)} %copy.20) | data formatting | bytes 589824 | tf_op jit(solution)/shard_map/reshape | solution.py:151
  36.7 3.0 %collective-permute-start = (f32[8,64,128]{2,1,0:T(8,128)S(1)}, f32[8,64,128]{2,1,0:T(8,128)S(1)}, u32[]{:S(2)}, u32[]{:S(2)}) collective-permute-start(f32[8,64,128]{2,1,0:T(8,128)S(1)} %copy.26), channel_id=1, source_target_pairs={{0,2},{1,4},{2,6},{3,0},{4,1},{5,7},{6,5},{7,3},{8,13},{9,15},{10,... | collective-permute-start | bytes 786440 | tf_op jit(solution)/shard_map/ppermute | solution.py:469
  39.7 1.8 %collective-permute-done.1 = f32[4,8,64,128]{3,2,1,0:T(8,128)} collective-permute-done((f32[4,8,64,128]{3,2,1,0:T(8,128)}, f32[4,8,64,128]{3,2,1,0:T(8,128)}, u32[]{:S(2)}, u32[]{:S(2)}) %collective-permute-start.1) | collective-permute-done | bytes 1048608 | tf_op jit(solution)/shard_map/ppermute | solution.py:458
  41.5 2.3 %fusion.23 = (f32[2,8,64,128]{3,2,1,0:T(8,128)}, f32[2,8,64,128]{3,2,1,0:T(8,128)}) fusion(f32[4,8,64,128]{3,2,1,0:T(8,128)} %collective-permute-done.1), kind=kLoop, calls=%fused_computation.109 | loop fusion | bytes 2097152 | tf_op jit(solution)/shard_map/slice | solution.py:474
  43.8 28.7 %collective-permute-done.model_ref = f32[8,64,128]{2,1,0:T(8,128)S(1)} collective-permute-done((f32[8,64,128]{2,1,0:T(8,128)S(1)}, f32[8,64,128]{2,1,0:T(8,128)S(1)}, u32[]{:S(2)}, u32[]{:S(2)}) %collective-permute-start) | collective-permute-done | bytes 262176 | tf_op jit(solution)/shard_map/ppermute | solution.py:469
  72.5 0.7 copy-done.1
  73.2 32.4 %shard_map.91 = f32[8,64,128]{2,1,0:T(8,128)} custom-call(s32[3]{0:T(128)} %pad_add_fusion.1.src_ref, f32[4]{0:T(128)} %bitcast.83, s32[2,256]{1,0:T(2,128)} %pad_add_fusion.rrow_ref, s32[256,1]{1,0:T(8,128)} %add_select_fusion.rcol_ref, f32[256,4]{1,0:T(8,128)} %bitcast.79, f32[8,64,128]{2,1,0:T(8,128)} %copy-done.1, ...), custom_call_target="tpu_custom_call" | custom-call | tf_op jit(solution)/shard_map/pallas_call | solution.py:400
  105.6 7.5 %collective-permute-start.2 = (f32[8,64,128]{2,1,0:T(8,128)}, f32[8,64,128]{2,1,0:T(8,128)S(1)}, u32[]{:S(2)}, u32[]{:S(2)}) collective-permute-start(f32[8,64,128]{2,1,0:T(8,128)} %shard_map.91), channel_id=1, source_target_pairs={{2,0},{4,1},{6,2},{0,3},{1,4},{7,5},{5,6},{3,7},{13,8},{15,9},{9,1... | collective-permute-start | bytes 786440 | tf_op jit(solution)/shard_map/ppermute | solution.py:480
  113.2 3.4 %collective-permute-done.2 = f32[8,64,128]{2,1,0:T(8,128)S(1)} collective-permute-done((f32[8,64,128]{2,1,0:T(8,128)}, f32[8,64,128]{2,1,0:T(8,128)S(1)}, u32[]{:S(2)}, u32[]{:S(2)}) %collective-permute-start.2) | collective-permute-done | bytes 262176 | tf_op jit(solution)/shard_map/ppermute | solution.py:480
  116.9 1.1 dynamic_update_slice.3
  118.1 1.0 reshape.709
  119.1 2.5 %copy.23 = f32[4,9,8,16,16]{4,3,2,1,0:T(8,128)} copy(f32[4,9,8,16,16]{3,0,4,1,2:T(4,128)S(1)} %bitcast.74) | data formatting | bytes 589824 | tf_op jit(solution)/shard_map/transpose | solution.py:160
  121.5 2.5 %reshape.710 = f32[36,8,256]{2,1,0:T(8,128)S(1)} reshape(f32[4,9,8,16,16]{4,3,2,1,0:T(8,128)} %copy.23) | data formatting | bytes 589824 | tf_op jit(solution)/shard_map/reshape | solution.py:160
  124.9 0.7 slice_select_fusion
  125.6 18.2 %all-to-all-start.1 = ((f32[32,1,8,256]{3,2,1,0:T(8,128)}), f32[32,1,8,256]{3,2,1,0:T(8,128)S(1)}, u32[]{:S(2)}, u32[]{:S(2)}) async-start(f32[32,1,8,256]{3,2,1,0:T(8,128)} %slice_select_fusion), calls=%async_computation.1 | async-start | bytes 524288 | tf_op jit(solution)/shard_map/all_to_all | solution.py:482
  144.2 10.8 %all-to-all-done.1 = f32[32,1,8,256]{3,2,1,0:T(8,128)S(1)} async-done(((f32[32,1,8,256]{3,2,1,0:T(8,128)}), f32[32,1,8,256]{3,2,1,0:T(8,128)S(1)}, u32[]{:S(2)}, u32[]{:S(2)}) %all-to-all-start.1) | async-done | bytes 262176 | tf_op jit(solution)/shard_map/all_to_all | solution.py:482
  155.6 0.7 copy.25
  (54 shorter events, 6.0 us)
Async XLA Ops:
  0.0 8.0 %copy-start = (f32[12,8,256]{2,1,0:T(8,128)S(1)}, f32[12,8,256]{2,1,0:T(8,128)}, u32[]{:S(2)}) copy-start(f32[12,8,256]{2,1,0:T(8,128)} %param.9) | copy-start | bytes 294916
  5.0 16.2 %copy-start.4 = (s32[32]{0:T(128)S(1)}, s32[32]{0:T(128)}, u32[]{:S(2)}) copy-start(s32[32]{0:T(128)} %param.16) | copy-start | bytes 388
  5.0 17.6 %copy-start.2 = (s32[1,256]{1,0:T(1,128)S(1)}, s32[1,256]{1,0:T(1,128)}, u32[]{:S(2)}) copy-start(s32[1,256]{1,0:T(1,128)} %param.14) | copy-start | bytes 3076
  5.0 20.4 %copy-start.3 = (f32[1,4,256]{2,1,0:T(4,128)S(1)}, f32[1,4,256]{2,1,0:T(4,128)}, u32[]{:S(2)}) copy-start(f32[1,4,256]{2,1,0:T(4,128)} %param.15) | copy-start | bytes 12292
  9.6 20.5 %all-to-all-start = ((f32[32,1,8,256]{3,2,1,0:T(8,128)}), f32[32,1,8,256]{3,2,1,0:T(8,128)S(1)}, u32[]{:S(2)}, u32[]{:S(2)}) async-start(f32[32,1,8,256]{3,2,1,0:T(8,128)} %slice_select_fusion.1), calls=%async_computation | async-start | bytes 524288 | tf_op jit(solution)/shard_map/all_to_all | solution.py:462
  19.0 22.5 %collective-permute-start.1 = (f32[4,8,64,128]{3,2,1,0:T(8,128)}, f32[4,8,64,128]{3,2,1,0:T(8,128)}, u32[]{:S(2)}, u32[]{:S(2)}) collective-permute-start(f32[4,8,64,128]{3,2,1,0:T(8,128)} %maximum_convert_fusion), channel_id=1, source_target_pairs={{0,2},{1,4},{2,6},{3,0},{4,1},{5,7},{6,5},{7,3},{8,13},{9,15},{10,... | collective-permute-start | bytes 3145736 | tf_op jit(solution)/shard_map/ppermute | solution.py:458
  36.7 35.8 %collective-permute-start = (f32[8,64,128]{2,1,0:T(8,128)S(1)}, f32[8,64,128]{2,1,0:T(8,128)S(1)}, u32[]{:S(2)}, u32[]{:S(2)}) collective-permute-start(f32[8,64,128]{2,1,0:T(8,128)S(1)} %copy.26), channel_id=1, source_target_pairs={{0,2},{1,4},{2,6},{3,0},{4,1},{5,7},{6,5},{7,3},{8,13},{9,15},{10,... | collective-permute-start | bytes 786440 | tf_op jit(solution)/shard_map/ppermute | solution.py:469
  72.5 0.7 copy-start.1
  105.6 11.1 %collective-permute-start.2 = (f32[8,64,128]{2,1,0:T(8,128)}, f32[8,64,128]{2,1,0:T(8,128)S(1)}, u32[]{:S(2)}, u32[]{:S(2)}) collective-permute-start(f32[8,64,128]{2,1,0:T(8,128)} %shard_map.91), channel_id=1, source_target_pairs={{2,0},{4,1},{6,2},{0,3},{1,4},{7,5},{5,6},{3,7},{13,8},{15,9},{9,1... | collective-permute-start | bytes 786440 | tf_op jit(solution)/shard_map/ppermute | solution.py:480
  125.6 29.4 %all-to-all-start.1 = ((f32[32,1,8,256]{3,2,1,0:T(8,128)}), f32[32,1,8,256]{3,2,1,0:T(8,128)S(1)}, u32[]{:S(2)}, u32[]{:S(2)}) async-start(f32[32,1,8,256]{3,2,1,0:T(8,128)} %slice_select_fusion), calls=%async_computation.1 | async-start | bytes 524288 | tf_op jit(solution)/shard_map/all_to_all | solution.py:482

commit v10 on v7

--- a/solution.py
+++ b/solution.py
@@ -241,10 +241,11 @@
 
 def migrate_kernel(
     src_ref, wave_ref, rrow_ref, rcol_ref, resid_ref, model_ref, pf_ref, qa_ref,
-    img_ref, pad_p, pad_q, lap, qs, inject, send_sem, recv_sem,
+    img_ref, pad_p, pad_q, lap, qs, inject, img_loc, img_scr, send_sem, recv_sem, image_sem,
 ):
     group = lax.axis_index("shot")
-    me = block_of(group, lax.axis_index("sub"))
+    sub = lax.axis_index("sub")
+    me = block_of(group, sub)
     n_sub = lax.axis_size("sub")
     depth = model_ref.shape[0]
     halo = jnp.zeros((RADIUS, AX, AY), jnp.float32)
@@ -256,10 +257,22 @@
     pad_q[0, RADIUS : RADIUS + depth] = model_ref[...] * qa_ref[0]
     up_dev = device_of(group, (me + 1) % n_sub)
     down_dev = device_of(group, (me + n_sub - 1) % n_sub)
+    target = device_of(group, sub)
+    moved = target != sub
+    mesh_id = pl.DeviceIdType.MESH
     barrier = pltpu.get_barrier_semaphore()
-    pl.semaphore_signal(barrier, 1, device_id={"sub": up_dev}, device_id_type=pl.DeviceIdType.MESH)
-    pl.semaphore_signal(barrier, 1, device_id={"sub": down_dev}, device_id_type=pl.DeviceIdType.MESH)
-    pl.semaphore_wait(barrier, 2)
+    pl.semaphore_signal(barrier, 1, device_id={"sub": up_dev}, device_id_type=mesh_id)
+    pl.semaphore_signal(barrier, 1, device_id={"sub": down_dev}, device_id_type=mesh_id)
+
+    @pl.when(moved)
+    def _():
+        pl.semaphore_signal(barrier, 1, device_id={"sub": target}, device_id_type=mesh_id)
+        pl.semaphore_signal(barrier, 1, device_id={"sub": me}, device_id_type=mesh_id)
+        pl.semaphore_wait(barrier, 4)
+
+    @pl.when(jnp.logical_not(moved))
+    def _():
+        pl.semaphore_wait(barrier, 2)
     rows = lax.broadcasted_iota(jnp.int32, (AX, AY), 0)
     lanes = lax.broadcasted_iota(jnp.int32, (AX, AY), 1)
     n_rec = rcol_ref.shape[0]
@@ -360,7 +373,7 @@
                 for s in range(NT - 1):
                     image = image + qs[s, j] * lap[NT - 1 - s, j]
                 image = image + result * lap[0, j]
-                img_ref[j] = IMAGE_SCALE * image
+                img_loc[j] = IMAGE_SCALE * image
             return carry
 
         lax.fori_loop(0, depth, plane, 0)
@@ -378,6 +391,25 @@
         if r < NT - 1:
             adj = exchange(r + 1, 1)
             build_injection(NT - 2 - r)
+    image_copy = pltpu.make_async_remote_copy(
+        src_ref=img_loc,
+        dst_ref=img_scr,
+        send_sem=image_sem.at[0],
+        recv_sem=image_sem.at[1],
+        device_id={"sub": me},
+        device_id_type=mesh_id,
+    )
+
+    @pl.when(moved)
+    def _():
+        image_copy.start()
+        image_copy.wait_send()
+        image_copy.wait_recv()
+        img_ref[...] = img_scr[...]
+
+    @pl.when(jnp.logical_not(moved))
+    def _():
+        img_ref[...] = img_loc[...]
 
 
 def migrate(model, state_fwd, state_adj, wave, source, receivers, resid):
@@ -408,8 +440,11 @@
             pltpu.VMEM(field, jnp.float32),
             pltpu.VMEM(field, jnp.float32),
             pltpu.VMEM(model.shape, jnp.float32),
+            pltpu.VMEM(model.shape, jnp.float32),
+            pltpu.VMEM(model.shape, jnp.float32),
             pltpu.SemaphoreType.DMA((NT, 2, 2)),
             pltpu.SemaphoreType.DMA((NT, 2, 2)),
+            pltpu.SemaphoreType.DMA((2,)),
         ],
         compiler_params=pltpu.CompilerParams(collective_id=0, has_side_effects=True),
     )(
@@ -475,7 +510,6 @@
             receiver_cell[k],
             residual[k],
         )
-        image = lax.ppermute(image, ("shot", "sub"), [(b, a) for a, b in outbound])
         images.append(disperse(image, row_start, col_start, groups, own_cols, caps))
     returned = lax.all_to_all(images[0], "shot", split_axis=0, concat_axis=0, tiled=True)
     gradient = accumulate(

time: 150 us -> 149 us (level)
  Pallas kernels: 31.5 us -> 40.6 us
  starting transfers between devices: 42 us -> 34.4 us
  waiting for transfers between devices: 40.3 us -> 36.6 us
    pallas_call x1, Pallas kernels: 31.5 us -> 40.6 us  [migrate(): pl.pallas_call(migrate_kernel, out_shape=jax.ShapeDtypeStruct(model.shape...]
    ppermute x1 -> x0, starting transfers between devices: 4.25 us -> none  [body(): image = lax.ppermute(image, ('shot', 'sub'), [(b, a) for a, b in outbound])]
    all_to_all x1, starting transfers between devices: 22.1 us -> 18.6 us  [body(): lax.all_to_all(images[0], 'shot', split_axis=0, concat_axis=0, tiled=True)]
    ppermute x1 -> x0, waiting for transfers between devices: 3.42 us -> none  [body(): image = lax.ppermute(image, ('shot', 'sub'), [(b, a) for a, b in outbound])]
  transfers between devices with their start and end apart: 5 -> 4, of which waited for: 5 -> 4; matrix products, arithmetic and copies ran while one was open for 11% -> 11% of each run, Pallas kernels for 0% -> 0%
where the time goes in v10:
time: 149 us; the launch traced here: 148 us
  Pallas kernels  40.6 us (27%)
  waiting for transfers between devices  36.6 us (25%)
  starting transfers between devices  34.4 us (23%)
  local copies, waits for them, and re-layouts  23.7 us (16%)
  other arithmetic  8.07 us (5%)
  between operations  3.75 us (3%)
    pallas_call x1, Pallas kernels, migrate(): pl.pallas_call(migrate_kernel, out_shape=jax.ShapeDtypeStruct(model.shape...  40.6 us
    ppermute x1, waiting for transfers between devices, body(): model = lax.ppermute(model, ('shot', 'sub'), outbound)  24 us
    all_to_all x1, starting transfers between devices, body(): lax.all_to_all(images[0], 'shot', split_axis=0, concat_axis=0, tiled=True)  18.6 us
    all_to_all x1, waiting for transfers between devices, body(): lax.all_to_all(images[0], 'shot', split_axis=0, concat_axis=0, tiled=True)  10.7 us
    all_to_all x1, starting transfers between devices, body(): lax.all_to_all(sending, 'shot', split_axis=0, concat_axis=0, tiled=True)  9.36 us
    ppermute x1, starting transfers between devices, body(): model = lax.ppermute(model, ('shot', 'sub'), outbound)  4.3 us
  transfers between devices with their start and end apart: 4, of which 4 were waited for; matrix products, arithmetic and copies ran while one was open for 11% of the time, Pallas kernels for 0%

profile of v10, /device:TPU:5, one launch (start us, length us, event | category | flops | bytes accessed | tf_op | source)
XLA Modules:
  0.0 147.6 jit_solution(13257417452225625839)
XLA Ops:
  0.0 1.3 dynamic_slice.9
  3.3 0.7 and_select_fusion.14
  4.2 0.7 fusion.22
  6.0 0.6 gather_fusion
  6.9 0.7 slice_select_fusion.1
  7.6 9.4 %all-to-all-start = ((f32[32,1,8,256]{3,2,1,0:T(8,128)}), f32[32,1,8,256]{3,2,1,0:T(8,128)S(1)}, u32[]{:S(2)}, u32[]{:S(2)}) async-start(f32[32,1,8,256]{3,2,1,0:T(8,128)} %slice_select_fusion.1), calls=%async_computation | async-start | bytes 524288 | tf_op jit(solution)/shard_map/all_to_all | solution.py:495
  17.0 1.1 maximum_convert_fusion
  18.0 2.2 %collective-permute-start.1 = (f32[4,8,64,128]{3,2,1,0:T(8,128)}, f32[4,8,64,128]{3,2,1,0:T(8,128)}, u32[]{:S(2)}, u32[]{:S(2)}) collective-permute-start(f32[4,8,64,128]{3,2,1,0:T(8,128)} %maximum_convert_fusion), channel_id=1, source_target_pairs={{0,2},{1,4},{2,6},{3,0},{4,1},{5,7},{6,5},{7,3},{8,13},{9,15},{10,... | collective-permute-start | bytes 3145736 | tf_op jit(solution)/shard_map/ppermute | solution.py:491
  20.8 0.7 fusion.11
  21.5 0.7 fusion.13
  24.7 0.8 copy.18
  25.6 0.7 add_select_fusion.rcol_ref
  26.3 1.8 %all-to-all-done = f32[32,1,8,256]{3,2,1,0:T(8,128)S(1)} async-done(((f32[32,1,8,256]{3,2,1,0:T(8,128)}), f32[32,1,8,256]{3,2,1,0:T(8,128)S(1)}, u32[]{:S(2)}, u32[]{:S(2)}) %all-to-all-start) | async-done | bytes 262176 | tf_op jit(solution)/shard_map/all_to_all | solution.py:495
  28.1 0.6 gather_fusion.1
  28.7 0.7 reshape.707
  29.4 2.5 %copy.20 = f32[8,4,16,9,16]{2,1,4,3,0:T(4,128)} copy(f32[8,4,16,9,16]{4,2,0,3,1:T(8,128)S(1)} %bitcast.73) | data formatting | bytes 589824 | tf_op jit(solution)/shard_map/transpose | solution.py:151
  31.9 2.5 %reshape.708 = f32[8,64,144]{1,2,0:T(8,128)S(1)} reshape(f32[8,4,16,9,16]{2,1,4,3,0:T(4,128)} %copy.20) | data formatting | bytes 589824 | tf_op jit(solution)/shard_map/reshape | solution.py:151
  34.7 4.3 %collective-permute-start = (f32[8,64,128]{2,1,0:T(8,128)S(1)}, f32[8,64,128]{2,1,0:T(8,128)S(1)}, u32[]{:S(2)}, u32[]{:S(2)}) collective-permute-start(f32[8,64,128]{2,1,0:T(8,128)S(1)} %copy.26), channel_id=1, source_target_pairs={{0,2},{1,4},{2,6},{3,0},{4,1},{5,7},{6,5},{7,3},{8,13},{9,15},{10,... | collective-permute-start | bytes 786440 | tf_op jit(solution)/shard_map/ppermute | solution.py:502
  39.1 2.3 %fusion.23 = (f32[2,8,64,128]{3,2,1,0:T(8,128)}, f32[2,8,64,128]{3,2,1,0:T(8,128)}) fusion(f32[4,8,64,128]{3,2,1,0:T(8,128)} %collective-permute-done.1), kind=kLoop, calls=%fused_computation.109 | loop fusion | bytes 2097152 | tf_op jit(solution)/shard_map/slice | solution.py:507
  41.4 24.0 %collective-permute-done.model_ref = f32[8,64,128]{2,1,0:T(8,128)S(1)} collective-permute-done((f32[8,64,128]{2,1,0:T(8,128)S(1)}, f32[8,64,128]{2,1,0:T(8,128)S(1)}, u32[]{:S(2)}, u32[]{:S(2)}) %collective-permute-start) | collective-permute-done | bytes 262176 | tf_op jit(solution)/shard_map/ppermute | solution.py:502
  65.5 0.7 copy-done.3
  66.2 40.6 %shard_map.91 = f32[8,64,128]{2,1,0:T(8,128)} custom-call(s32[3]{0:T(128)} %pad_add_fusion.1.src_ref, f32[4]{0:T(128)} %bitcast.83, s32[2,256]{1,0:T(2,128)} %pad_add_fusion.rrow_ref, s32[256,1]{1,0:T(8,128)} %add_select_fusion.rcol_ref, f32[256,4]{1,0:T(8,128)} %bitcast.79, f32[8,64,128]{2,1,0:T(8,128)} %copy-done.3, ...), custom_call_target="tpu_custom_call" | custom-call | tf_op jit(solution)/shard_map/pallas_call | solution.py:432
  106.8 1.1 copy.22
  108.0 1.1 dynamic_update_slice.3
  109.1 1.0 reshape.709
  110.2 2.5 %copy.23 = f32[4,9,8,16,16]{4,3,2,1,0:T(8,128)} copy(f32[4,9,8,16,16]{3,0,4,1,2:T(4,128)S(1)} %bitcast.74) | data formatting | bytes 589824 | tf_op jit(solution)/shard_map/transpose | solution.py:160
  112.6 2.5 %reshape.710 = f32[36,8,256]{2,1,0:T(8,128)S(1)} reshape(f32[4,9,8,16,16]{4,3,2,1,0:T(8,128)} %copy.23) | data formatting | bytes 589824 | tf_op jit(solution)/shard_map/reshape | solution.py:160
  115.2 0.6 gather_fusion.2
  116.0 0.7 slice_select_fusion
  116.7 18.6 %all-to-all-start.1 = ((f32[32,1,8,256]{3,2,1,0:T(8,128)}), f32[32,1,8,256]{3,2,1,0:T(8,128)S(1)}, u32[]{:S(2)}, u32[]{:S(2)}) async-start(f32[32,1,8,256]{3,2,1,0:T(8,128)} %slice_select_fusion), calls=%async_computation.1 | async-start | bytes 524288 | tf_op jit(solution)/shard_map/all_to_all | solution.py:514
  135.7 10.7 %all-to-all-done.1 = f32[32,1,8,256]{3,2,1,0:T(8,128)S(1)} async-done(((f32[32,1,8,256]{3,2,1,0:T(8,128)}), f32[32,1,8,256]{3,2,1,0:T(8,128)S(1)}, u32[]{:S(2)}, u32[]{:S(2)}) %all-to-all-start.1) | async-done | bytes 262176 | tf_op jit(solution)/shard_map/all_to_all | solution.py:514
  146.9 0.7 copy.25
  (56 shorter events, 4.7 us)
Async XLA Ops:
  0.0 6.0 %copy-start = (f32[12,8,256]{2,1,0:T(8,128)S(1)}, f32[12,8,256]{2,1,0:T(8,128)}, u32[]{:S(2)}) copy-start(f32[12,8,256]{2,1,0:T(8,128)} %param.9) | copy-start | bytes 294916
  0.0 17.0 %copy-start.2 = (bf16[1,2,8,64,128]{4,3,2,1,0:T(8,128)(2,1)S(1)}, bf16[1,2,8,64,128]{4,3,2,1,0:T(8,128)(2,1)}, u32[]{:S(2)}) copy-start(bf16[1,2,8,64,128]{4,3,2,1,0:T(8,128)(2,1)} %param.10) | copy-start | bytes 786436
  0.0 17.0 %copy-start.1 = (bf16[1,2,8,64,128]{4,3,2,1,0:T(8,128)(2,1)S(1)}, bf16[1,2,8,64,128]{4,3,2,1,0:T(8,128)(2,1)}, u32[]{:S(2)}) copy-start(bf16[1,2,8,64,128]{4,3,2,1,0:T(8,128)(2,1)} %param.11) | copy-start | bytes 786436
  6.0 14.3 %copy-start.6 = (s32[32]{0:T(128)S(1)}, s32[32]{0:T(128)}, u32[]{:S(2)}) copy-start(s32[32]{0:T(128)} %param.16) | copy-start | bytes 388
  6.0 16.4 %copy-start.4 = (s32[1,256]{1,0:T(1,128)S(1)}, s32[1,256]{1,0:T(1,128)}, u32[]{:S(2)}) copy-start(s32[1,256]{1,0:T(1,128)} %param.14) | copy-start | bytes 3076
  6.6 18.1 %copy-start.5 = (f32[1,4,256]{2,1,0:T(4,128)S(1)}, f32[1,4,256]{2,1,0:T(4,128)}, u32[]{:S(2)}) copy-start(f32[1,4,256]{2,1,0:T(4,128)} %param.15) | copy-start | bytes 12292
  7.6 20.5 %all-to-all-start = ((f32[32,1,8,256]{3,2,1,0:T(8,128)}), f32[32,1,8,256]{3,2,1,0:T(8,128)S(1)}, u32[]{:S(2)}, u32[]{:S(2)}) async-start(f32[32,1,8,256]{3,2,1,0:T(8,128)} %slice_select_fusion.1), calls=%async_computation | async-start | bytes 524288 | tf_op jit(solution)/shard_map/all_to_all | solution.py:495
  18.0 21.1 %collective-permute-start.1 = (f32[4,8,64,128]{3,2,1,0:T(8,128)}, f32[4,8,64,128]{3,2,1,0:T(8,128)}, u32[]{:S(2)}, u32[]{:S(2)}) collective-permute-start(f32[4,8,64,128]{3,2,1,0:T(8,128)} %maximum_convert_fusion), channel_id=1, source_target_pairs={{0,2},{1,4},{2,6},{3,0},{4,1},{5,7},{6,5},{7,3},{8,13},{9,15},{10,... | collective-permute-start | bytes 3145736 | tf_op jit(solution)/shard_map/ppermute | solution.py:491
  34.7 30.8 %collective-permute-start = (f32[8,64,128]{2,1,0:T(8,128)S(1)}, f32[8,64,128]{2,1,0:T(8,128)S(1)}, u32[]{:S(2)}, u32[]{:S(2)}) collective-permute-start(f32[8,64,128]{2,1,0:T(8,128)S(1)} %copy.26), channel_id=1, source_target_pairs={{0,2},{1,4},{2,6},{3,0},{4,1},{5,7},{6,5},{7,3},{8,13},{9,15},{10,... | collective-permute-start | bytes 786440 | tf_op jit(solution)/shard_map/ppermute | solution.py:502
  65.5 0.7 copy-start.3
  116.7 29.7 %all-to-all-start.1 = ((f32[32,1,8,256]{3,2,1,0:T(8,128)}), f32[32,1,8,256]{3,2,1,0:T(8,128)S(1)}, u32[]{:S(2)}, u32[]{:S(2)}) async-start(f32[32,1,8,256]{3,2,1,0:T(8,128)} %slice_select_fusion), calls=%async_computation.1 | async-start | bytes 524288 | tf_op jit(solution)/shard_map/all_to_all | solution.py:514

commit v11 on v10

--- a/solution.py
+++ b/solution.py
@@ -493,13 +493,13 @@
         velocity_tiles, aperture_row, aperture_col, every_shot, groups, own_cols, caps
     )
     fetched = lax.all_to_all(sending, "shot", split_axis=0, concat_axis=0, tiled=True)
+    fetched = lax.ppermute(fetched, ("shot", "sub"), outbound)
     images = []
     for k in every_shot:
         shot_id = myself * SHOTS_DEV + k
         row_start = aperture_row[shot_id]
         col_start = aperture_col[shot_id]
         model = assemble(fetched, row_start, col_start, own_cols)
-        model = lax.ppermute(model, ("shot", "sub"), outbound)
         states = states_moved[k]
         image = migrate(
             model,

time: 149 us -> 155 us (1.040)
  waiting for transfers between devices: 36.6 us -> 43.2 us
    ppermute x1, waiting for transfers between devices: 24 us -> 28.4 us  [body(): fetched = lax.ppermute(fetched, ('shot', 'sub'), outbound)]
    all_to_all x1, waiting for transfers between devices: 1.8 us -> 4.11 us  [body(): lax.all_to_all(sending, 'shot', split_axis=0, concat_axis=0, tiled=True)]
    ppermute x1, starting transfers between devices: 4.3 us -> 2.15 us  [body(): fetched = lax.ppermute(fetched, ('shot', 'sub'), outbound)]
  transfers between devices with their start and end apart: 4 -> 4, of which waited for: 4 -> 3; matrix products, arithmetic and copies ran while one was open for 11% -> 9% of each run, Pallas kernels for 0% -> 0%
where the time goes in v11:
time: 155 us; the launch traced here: 154 us
  waiting for transfers between devices  43.2 us (28%)
  Pallas kernels  41.6 us (27%)
  starting transfers between devices  33.1 us (21%)
  local copies, waits for them, and re-layouts  23.7 us (15%)
  other arithmetic  8.03 us (5%)
  between operations  3.77 us (2%)
    pallas_call x1, Pallas kernels, migrate(): pl.pallas_call(migrate_kernel, out_shape=jax.ShapeDtypeStruct(model.shape...  41.6 us
    ppermute x1, waiting for transfers between devices, body(): fetched = lax.ppermute(fetched, ('shot', 'sub'), outbound)  28.4 us
    all_to_all x1, starting transfers between devices, body(): lax.all_to_all(images[0], 'shot', split_axis=0, concat_axis=0, tiled=True)  19.5 us
    all_to_all x1, waiting for transfers between devices, body(): lax.all_to_all(images[0], 'shot', split_axis=0, concat_axis=0, tiled=True)  10.7 us
    all_to_all x1, starting transfers between devices, body(): lax.all_to_all(sending, 'shot', split_axis=0, concat_axis=0, tiled=True)  9.36 us
    all_to_all x1, waiting for transfers between devices, body(): lax.all_to_all(sending, 'shot', split_axis=0, concat_axis=0, tiled=True)  4.11 us
  transfers between devices with their start and end apart: 4, of which 3 were waited for; matrix products, arithmetic and copies ran while one was open for 9% of the time, Pallas kernels for 0%

profile of v11, /device:TPU:5, one launch (start us, length us, event | category | flops | bytes accessed | tf_op | source)
XLA Modules:
  0.0 153.9 jit_solution(12209554556514157896)
XLA Ops:
  0.0 1.3 dynamic_slice.9
  3.3 0.7 and_select_fusion.14
  4.2 0.7 fusion.22
  6.0 0.6 gather_fusion
  6.9 0.7 slice_select_fusion.1
  7.6 9.4 %all-to-all-start = ((f32[32,1,8,256]{3,2,1,0:T(8,128)}), f32[32,1,8,256]{3,2,1,0:T(8,128)S(1)}, u32[]{:S(2)}, u32[]{:S(2)}) async-start(f32[32,1,8,256]{3,2,1,0:T(8,128)} %slice_select_fusion.1), calls=%async_computation | async-start | bytes 524288 | tf_op jit(solution)/shard_map/all_to_all | solution.py:495
  17.0 1.0 maximum_convert_fusion
  18.0 2.2 %collective-permute-start.1 = (f32[4,8,64,128]{3,2,1,0:T(8,128)}, f32[4,8,64,128]{3,2,1,0:T(8,128)}, u32[]{:S(2)}, u32[]{:S(2)}) collective-permute-start(f32[4,8,64,128]{3,2,1,0:T(8,128)} %maximum_convert_fusion), channel_id=1, source_target_pairs={{0,2},{1,4},{2,6},{3,0},{4,1},{5,7},{6,5},{7,3},{8,13},{9,15},{10,... | collective-permute-start | bytes 3145736 | tf_op jit(solution)/shard_map/ppermute | solution.py:491
  20.8 0.7 fusion.11
  21.5 0.7 fusion.13
  23.9 4.1 %all-to-all-done = f32[32,1,8,256]{3,2,1,0:T(8,128)S(1)} async-done(((f32[32,1,8,256]{3,2,1,0:T(8,128)}), f32[32,1,8,256]{3,2,1,0:T(8,128)S(1)}, u32[]{:S(2)}, u32[]{:S(2)}) %all-to-all-start) | async-done | bytes 262176 | tf_op jit(solution)/shard_map/all_to_all | solution.py:495
  28.1 2.2 %collective-permute-start = (f32[32,1,8,256]{3,2,1,0:T(8,128)S(1)}, f32[32,1,8,256]{3,2,1,0:T(8,128)S(1)}, u32[]{:S(2)}, u32[]{:S(2)}) collective-permute-start(f32[32,1,8,256]{3,2,1,0:T(8,128)S(1)} %all-to-all-done), channel_id=1, source_target_pairs={{0,2},{1,4},{2,6},{3,0},{4,1},{5,7},{6,5},{7,3},{8,13},{9,15},{10,... | collective-permute-start | bytes 786440 | tf_op jit(solution)/shard_map/ppermute | solution.py:496
  31.1 0.8 copy.18
  31.9 0.7 add_select_fusion.rcol_ref
  32.6 28.4 %collective-permute-done = f32[32,1,8,256]{3,2,1,0:T(8,128)S(1)} collective-permute-done((f32[32,1,8,256]{3,2,1,0:T(8,128)S(1)}, f32[32,1,8,256]{3,2,1,0:T(8,128)S(1)}, u32[]{:S(2)}, u32[]{:S(2)}) %collective-permute-start) | collective-permute-done | bytes 262176 | tf_op jit(solution)/shard_map/ppermute | solution.py:496
  61.0 0.6 gather_fusion.1
  61.6 0.7 reshape.707
  62.3 2.5 %copy.20 = f32[8,4,16,9,16]{2,1,4,3,0:T(4,128)} copy(f32[8,4,16,9,16]{4,2,0,3,1:T(8,128)S(1)} %bitcast.73) | data formatting | bytes 589824 | tf_op jit(solution)/shard_map/transpose | solution.py:151
  64.8 2.5 %reshape.708 = f32[8,64,144]{1,2,0:T(8,128)S(1)} reshape(f32[8,4,16,9,16]{2,1,4,3,0:T(4,128)} %copy.20) | data formatting | bytes 589824 | tf_op jit(solution)/shard_map/reshape | solution.py:151
  67.4 0.9 copy.26.model_ref
  68.3 2.3 %fusion.23 = (f32[2,8,64,128]{3,2,1,0:T(8,128)}, f32[2,8,64,128]{3,2,1,0:T(8,128)}) fusion(f32[4,8,64,128]{3,2,1,0:T(8,128)} %collective-permute-done.1), kind=kLoop, calls=%fused_computation.109 | loop fusion | bytes 2097152 | tf_op jit(solution)/shard_map/slice | solution.py:507
  70.6 41.6 %shard_map.91 = f32[8,64,128]{2,1,0:T(8,128)} custom-call(s32[3]{0:T(128)} %pad_add_fusion.1.src_ref, f32[4]{0:T(128)} %bitcast.83, s32[2,256]{1,0:T(2,128)} %pad_add_fusion.rrow_ref, s32[256,1]{1,0:T(8,128)} %add_select_fusion.rcol_ref, f32[256,4]{1,0:T(8,128)} %bitcast.78, f32[8,64,128]{2,1,0:T(8,128)} %copy.26.model_ref, ...), custom_call_target="tpu_custom_call" | custom-call | tf_op jit(solution)/shard_map/pallas_call | solution.py:432
  112.2 1.1 copy.22
  113.4 1.1 dynamic_update_slice.3
  114.5 1.0 reshape.709
  115.5 2.5 %copy.23 = f32[4,9,8,16,16]{4,3,2,1,0:T(8,128)} copy(f32[4,9,8,16,16]{3,0,4,1,2:T(4,128)S(1)} %bitcast.74) | data formatting | bytes 589824 | tf_op jit(solution)/shard_map/transpose | solution.py:160
  118.0 2.5 %reshape.710 = f32[36,8,256]{2,1,0:T(8,128)S(1)} reshape(f32[4,9,8,16,16]{4,3,2,1,0:T(8,128)} %copy.23) | data formatting | bytes 589824 | tf_op jit(solution)/shard_map/reshape | solution.py:160
  120.5 0.6 gather_fusion.2
  121.3 0.7 slice_select_fusion
  122.0 19.5 %all-to-all-start.1 = ((f32[32,1,8,256]{3,2,1,0:T(8,128)}), f32[32,1,8,256]{3,2,1,0:T(8,128)S(1)}, u32[]{:S(2)}, u32[]{:S(2)}) async-start(f32[32,1,8,256]{3,2,1,0:T(8,128)} %slice_select_fusion), calls=%async_computation.1 | async-start | bytes 524288 | tf_op jit(solution)/shard_map/all_to_all | solution.py:514
  142.0 10.7 %all-to-all-done.1 = f32[32,1,8,256]{3,2,1,0:T(8,128)S(1)} async-done(((f32[32,1,8,256]{3,2,1,0:T(8,128)}), f32[32,1,8,256]{3,2,1,0:T(8,128)S(1)}, u32[]{:S(2)}, u32[]{:S(2)}) %all-to-all-start.1) | async-done | bytes 262176 | tf_op jit(solution)/shard_map/all_to_all | solution.py:514
  153.2 0.7 copy.25
  (54 shorter events, 4.4 us)
Async XLA Ops:
  0.0 6.0 %copy-start = (f32[12,8,256]{2,1,0:T(8,128)S(1)}, f32[12,8,256]{2,1,0:T(8,128)}, u32[]{:S(2)}) copy-start(f32[12,8,256]{2,1,0:T(8,128)} %param.9) | copy-start | bytes 294916
  0.0 17.0 %copy-start.2 = (bf16[1,2,8,64,128]{4,3,2,1,0:T(8,128)(2,1)S(1)}, bf16[1,2,8,64,128]{4,3,2,1,0:T(8,128)(2,1)}, u32[]{:S(2)}) copy-start(bf16[1,2,8,64,128]{4,3,2,1,0:T(8,128)(2,1)} %param.10) | copy-start | bytes 786436
  0.0 17.0 %copy-start.1 = (bf16[1,2,8,64,128]{4,3,2,1,0:T(8,128)(2,1)S(1)}, bf16[1,2,8,64,128]{4,3,2,1,0:T(8,128)(2,1)}, u32[]{:S(2)}) copy-start(bf16[1,2,8,64,128]{4,3,2,1,0:T(8,128)(2,1)} %param.11) | copy-start | bytes 786436
  6.0 14.2 %copy-start.5 = (s32[32]{0:T(128)S(1)}, s32[32]{0:T(128)}, u32[]{:S(2)}) copy-start(s32[32]{0:T(128)} %param.16) | copy-start | bytes 388
  6.0 16.4 %copy-start.3 = (s32[1,256]{1,0:T(1,128)S(1)}, s32[1,256]{1,0:T(1,128)}, u32[]{:S(2)}) copy-start(s32[1,256]{1,0:T(1,128)} %param.14) | copy-start | bytes 3076
  6.6 24.4 %copy-start.4 = (f32[1,4,256]{2,1,0:T(4,128)S(1)}, f32[1,4,256]{2,1,0:T(4,128)}, u32[]{:S(2)}) copy-start(f32[1,4,256]{2,1,0:T(4,128)} %param.15) | copy-start | bytes 12292
  7.6 20.5 %all-to-all-start = ((f32[32,1,8,256]{3,2,1,0:T(8,128)}), f32[32,1,8,256]{3,2,1,0:T(8,128)S(1)}, u32[]{:S(2)}, u32[]{:S(2)}) async-start(f32[32,1,8,256]{3,2,1,0:T(8,128)} %slice_select_fusion.1), calls=%async_computation | async-start | bytes 524288 | tf_op jit(solution)/shard_map/all_to_all | solution.py:495
  18.0 50.3 %collective-permute-start.1 = (f32[4,8,64,128]{3,2,1,0:T(8,128)}, f32[4,8,64,128]{3,2,1,0:T(8,128)}, u32[]{:S(2)}, u32[]{:S(2)}) collective-permute-start(f32[4,8,64,128]{3,2,1,0:T(8,128)} %maximum_convert_fusion), channel_id=1, source_target_pairs={{0,2},{1,4},{2,6},{3,0},{4,1},{5,7},{6,5},{7,3},{8,13},{9,15},{10,... | collective-permute-start | bytes 3145736 | tf_op jit(solution)/shard_map/ppermute | solution.py:491
  28.1 32.9 %collective-permute-start = (f32[32,1,8,256]{3,2,1,0:T(8,128)S(1)}, f32[32,1,8,256]{3,2,1,0:T(8,128)S(1)}, u32[]{:S(2)}, u32[]{:S(2)}) collective-permute-start(f32[32,1,8,256]{3,2,1,0:T(8,128)S(1)} %all-to-all-done), channel_id=1, source_target_pairs={{0,2},{1,4},{2,6},{3,0},{4,1},{5,7},{6,5},{7,3},{8,13},{9,15},{10,... | collective-permute-start | bytes 786440 | tf_op jit(solution)/shard_map/ppermute | solution.py:496
  122.0 30.6 %all-to-all-start.1 = ((f32[32,1,8,256]{3,2,1,0:T(8,128)}), f32[32,1,8,256]{3,2,1,0:T(8,128)S(1)}, u32[]{:S(2)}, u32[]{:S(2)}) async-start(f32[32,1,8,256]{3,2,1,0:T(8,128)} %slice_select_fusion), calls=%async_computation.1 | async-start | bytes 524288 | tf_op jit(solution)/shard_map/all_to_all | solution.py:514

commit v12 on v10

--- a/solution.py
+++ b/solution.py
@@ -138,36 +138,32 @@
     return gradient + summed.reshape(gradient.shape)
 
 
+def owner_tiles(row_start, col_start, own_cols):
+    owner = jnp.arange(AP_ROWS * own_cols, dtype=jnp.int32)
+    rel_row = (owner // own_cols - row_start) % AP_ROWS
+    rel_col = (owner % own_cols - col_start // TILE) % own_cols
+    return rel_row * own_cols + rel_col
+
+
 def assemble(received, row_start, col_start, own_cols):
     depth_cells = received.shape[2]
-    rel_row = jnp.arange(AP_ROWS, dtype=jnp.int32)[:, None]
-    rel_col = jnp.arange(AP_COLS + 1, dtype=jnp.int32)[None, :]
-    source_owner = (row_start + rel_row) % AP_ROWS * own_cols + (
-        col_start // TILE + rel_col
-    ) % own_cols
-    flat_index = source_owner.reshape(-1)
-    pieces = received.reshape(-1, depth_cells, TILE * TILE)[flat_index]
-    block = pieces.reshape(AP_ROWS, AP_COLS + 1, depth_cells, TILE, TILE)
-    block = block.transpose(2, 0, 3, 1, 4).reshape(depth_cells, AX, (AP_COLS + 1) * TILE)
-    return lax.dynamic_slice_in_dim(block, col_start % TILE, AY, 2)
+    owner = (
+        (row_start + jnp.arange(AP_ROWS, dtype=jnp.int32)[:, None]) % AP_ROWS * own_cols
+        + (col_start // TILE + jnp.arange(own_cols, dtype=jnp.int32)[None, :]) % own_cols
+    )
+    pieces = received.reshape(-1, depth_cells, TILE * TILE)[owner.reshape(-1)]
+    block = pieces.reshape(AP_ROWS, own_cols, depth_cells, TILE, TILE)
+    block = block.transpose(2, 0, 3, 1, 4).reshape(depth_cells, AX, AY)
+    return jnp.roll(block, -(col_start % TILE), axis=2)
 
 
 def disperse(image, row_start, col_start, groups, own_cols, caps):
     depth_cells = image.shape[0]
-    wide = jnp.zeros((depth_cells, AX, (AP_COLS + 1) * TILE), jnp.float32)
-    wide = lax.dynamic_update_slice_in_dim(wide, image, col_start % TILE, 2)
-    pieces = wide.reshape(depth_cells, AP_ROWS, TILE, AP_COLS + 1, TILE)
-    pieces = pieces.transpose(1, 3, 0, 2, 4).reshape(
-        AP_ROWS * (AP_COLS + 1), depth_cells, TILE * TILE
-    )
-    owners = jnp.arange(groups, dtype=jnp.int32)[:, None]
-    block_row, block_col, usable = slot_layout(
-        row_start, col_start, owners // own_cols, owners % own_cols, own_cols, caps
-    )
-    position = jnp.clip(block_row * (AP_COLS + 1) + block_col, 0, AP_ROWS * (AP_COLS + 1) - 1)
-    chosen = jnp.where(usable[..., None, None], pieces[position], 0.0)
-    merged = merge_slots(chosen, usable[:, 1, None, None], col_start % TILE)
-    return merged.reshape(groups, 1, depth_cells, TILE * TILE)
+    rolled = jnp.roll(image, col_start % TILE, axis=2)
+    pieces = rolled.reshape(depth_cells, AP_ROWS, TILE, own_cols, TILE)
+    pieces = pieces.transpose(1, 3, 0, 2, 4).reshape(AP_ROWS * own_cols, depth_cells, TILE * TILE)
+    chosen = pieces[owner_tiles(row_start, col_start, own_cols)]
+    return chosen.reshape(groups, 1, depth_cells, TILE * TILE)
 
 
 X_CHIPS = 4

time: 149 us -> 146 us (0.980)
  local copies, waits for them, and re-layouts: 23.7 us -> 19.3 us
  waiting for transfers between devices: 36.6 us -> 38.2 us
    ppermute x1, waiting for transfers between devices: 24 us -> 27.4 us  [body(): model = lax.ppermute(model, ('shot', 'sub'), outbound)]
    ppermute x1, starting transfers between devices: 4.3 us -> 6.07 us  [body(): model = lax.ppermute(model, ('shot', 'sub'), outbound)]
    all_to_all x1, waiting for transfers between devices: 1.8 us -> 0.02 us  [body(): lax.all_to_all(sending, 'shot', split_axis=0, concat_axis=0, tiled=True)]
  transfers between devices with their start and end apart: 4 -> 4, of which waited for: 4 -> 2; matrix products, arithmetic and copies ran while one was open for 11% -> 10% of each run, Pallas kernels for 0% -> 0%
where the time goes in v12:
time: 146 us
  Pallas kernels  41.4 us (28%)
  waiting for transfers between devices  38.2 us (26%)
  starting transfers between devices  35.7 us (24%)
  local copies, waits for them, and re-layouts  19.3 us (13%)
  other arithmetic  6.78 us (5%)
  between operations  3.73 us (3%)
    pallas_call x1, Pallas kernels, migrate(): pl.pallas_call(migrate_kernel, out_shape=jax.ShapeDtypeStruct(model.shape...  41.4 us
    ppermute x1, waiting for transfers between devices, body(): model = lax.ppermute(model, ('shot', 'sub'), outbound)  27.4 us
    all_to_all x1, starting transfers between devices, body(): lax.all_to_all(images[0], 'shot', split_axis=0, concat_axis=0, tiled=True)  18.1 us
    all_to_all x1, waiting for transfers between devices, body(): lax.all_to_all(images[0], 'shot', split_axis=0, concat_axis=0, tiled=True)  10.8 us
    all_to_all x1, starting transfers between devices, body(): lax.all_to_all(sending, 'shot', split_axis=0, concat_axis=0, tiled=True)  9.36 us
    ppermute x1, starting transfers between devices, body(): model = lax.ppermute(model, ('shot', 'sub'), outbound)  6.07 us
  transfers between devices with their start and end apart: 4, of which 2 were waited for; matrix products, arithmetic and copies ran while one was open for 10% of the time, Pallas kernels for 0%

profile of v12, /device:TPU:5, one launch (start us, length us, event | category | flops | bytes accessed | tf_op | source)
XLA Modules:
  0.0 145.5 jit_solution(12741919843380497761)
XLA Ops:
  0.1 0.8 and_select_fusion.14
  1.4 0.6 gather_fusion
  2.3 0.7 slice_select_fusion
  3.1 9.4 %all-to-all-start = ((f32[32,1,8,256]{3,2,1,0:T(8,128)}), f32[32,1,8,256]{3,2,1,0:T(8,128)S(1)}, u32[]{:S(2)}, u32[]{:S(2)}) async-start(f32[32,1,8,256]{3,2,1,0:T(8,128)} %slice_select_fusion), calls=%async_computation | async-start | bytes 524288 | tf_op jit(solution)/shard_map/all_to_all | solution.py:491
  12.6 2.2 %collective-permute-start.1 = (f32[4,8,64,128]{3,2,1,0:T(8,128)S(1)}, f32[4,8,64,128]{3,2,1,0:T(8,128)}, u32[]{:S(2)}, u32[]{:S(2)}) collective-permute-start(f32[4,8,64,128]{3,2,1,0:T(8,128)S(1)} %maximum_convert_fusion), channel_id=1, source_target_pairs={{0,2},{1,4},{2,6},{3,0},{4,1},{5,7},{6,5},{7,3},{8,13},{9,15},{10,... | collective-permute-start | bytes 3145736 | tf_op jit(solution)/shard_map/ppermute | solution.py:487
  14.7 0.6 dynamic_slice.10
  17.3 0.6 dynamic_slice.9
  18.6 0.6 fusion.15
  19.3 0.6 fusion.23
  20.6 0.6 pad_add_fusion.rrow_ref
  21.2 0.7 pad_add_fusion.1.src_ref
  22.0 0.8 copy.23
  22.8 0.7 add_select_fusion.rcol_ref
  23.6 0.6 gather_fusion.1
  24.1 0.6 reshape.608
  24.8 2.6 %copy.25 = f32[8,4,16,8,16]{4,3,2,1,0:T(8,128)} copy(f32[8,4,16,8,16]{4,2,0,3,1:T(8,128)S(1)} %bitcast.69) | data formatting | bytes 524288 | tf_op jit(solution)/shard_map/transpose | solution.py:156
  27.4 2.2 %reshape.609 = f32[8,64,128]{2,1,0:T(8,128)S(1)} reshape(f32[8,4,16,8,16]{4,3,2,1,0:T(8,128)} %copy.25) | data formatting | bytes 524288 | tf_op jit(solution)/shard_map/reshape | solution.py:156
  29.5 0.2 fusion.4
  29.7 6.1 %collective-permute-start = (f32[8,64,128]{2,1,0:T(8,128)S(1)}, f32[8,64,128]{2,1,0:T(8,128)S(1)}, u32[]{:S(2)}, u32[]{:S(2)}) collective-permute-start(f32[8,64,128]{2,1,0:T(8,128)S(1)} %fusion.4), channel_id=1, source_target_pairs={{0,2},{1,4},{2,6},{3,0},{4,1},{5,7},{6,5},{7,3},{8,13},{9,15},{10,... | collective-permute-start | bytes 786440 | tf_op jit(solution)/shard_map/ppermute | solution.py:498
  35.8 2.3 %fusion.27 = (f32[2,8,64,128]{3,2,1,0:T(8,128)}, f32[2,8,64,128]{3,2,1,0:T(8,128)}) fusion(f32[4,8,64,128]{3,2,1,0:T(8,128)} %collective-permute-done.1), kind=kLoop, calls=%fused_computation.110 | loop fusion | bytes 2097152 | tf_op jit(solution)/shard_map/slice | solution.py:503
  38.1 27.4 %collective-permute-done.model_ref = f32[8,64,128]{2,1,0:T(8,128)S(1)} collective-permute-done((f32[8,64,128]{2,1,0:T(8,128)S(1)}, f32[8,64,128]{2,1,0:T(8,128)S(1)}, u32[]{:S(2)}, u32[]{:S(2)}) %collective-permute-start) | collective-permute-done | bytes 262176 | tf_op jit(solution)/shard_map/ppermute | solution.py:498
  65.6 0.7 copy-done.3
  66.3 41.4 %shard_map.91 = f32[8,64,128]{2,1,0:T(8,128)} custom-call(s32[3]{0:T(128)} %pad_add_fusion.1.src_ref, f32[4]{0:T(128)} %bitcast.78, s32[2,256]{1,0:T(2,128)} %pad_add_fusion.rrow_ref, s32[256,1]{1,0:T(8,128)} %add_select_fusion.rcol_ref, f32[256,4]{1,0:T(8,128)} %bitcast.74, f32[8,64,128]{2,1,0:T(8,128)} %copy-done.3, ...), custom_call_target="tpu_custom_call" | custom-call | tf_op jit(solution)/shard_map/pallas_call | solution.py:428
  107.7 1.2 fusion.3
  109.0 0.6 reshape.610
  109.6 1.7 %copy.26 = f32[4,8,8,16,16]{4,3,2,1,0:T(8,128)} copy(f32[4,8,8,16,16]{4,1,3,0,2:T(8,128)S(1)} %bitcast.70) | data formatting | bytes 524288 | tf_op jit(solution)/shard_map/transpose | solution.py:164
  111.3 2.4 %reshape.611 = f32[32,8,256]{2,1,0:T(8,128)S(1)} reshape(f32[4,8,8,16,16]{4,3,2,1,0:T(8,128)} %copy.26) | data formatting | bytes 524288 | tf_op jit(solution)/shard_map/reshape | solution.py:164
  113.7 1.3 gather_fusion.2
  115.0 18.1 %all-to-all-start.1 = ((f32[32,1,8,256]{3,2,1,0:T(8,128)}), f32[32,1,8,256]{3,2,1,0:T(8,128)S(1)}, u32[]{:S(2)}, u32[]{:S(2)}) async-start(f32[32,1,8,256]{3,2,1,0:T(8,128)} %bitcast.21), calls=%async_computation.1 | async-start | bytes 524288 | tf_op jit(solution)/shard_map/all_to_all | solution.py:510
  133.5 10.8 %all-to-all-done.1 = f32[32,1,8,256]{3,2,1,0:T(8,128)S(1)} async-done(((f32[32,1,8,256]{3,2,1,0:T(8,128)}), f32[32,1,8,256]{3,2,1,0:T(8,128)S(1)}, u32[]{:S(2)}, u32[]{:S(2)}) %all-to-all-start.1) | async-done | bytes 262176 | tf_op jit(solution)/shard_map/all_to_all | solution.py:510
  144.4 0.4 fusion
  144.8 0.7 copy.28
  (50 shorter events, 1.7 us)
Async XLA Ops:
  0.0 1.4 copy-start
  0.0 12.4 %copy-start.2 = (bf16[1,2,8,64,128]{4,3,2,1,0:T(8,128)(2,1)S(1)}, bf16[1,2,8,64,128]{4,3,2,1,0:T(8,128)(2,1)}, u32[]{:S(2)}) copy-start(bf16[1,2,8,64,128]{4,3,2,1,0:T(8,128)(2,1)} %param.12) | copy-start | bytes 786436
  0.0 12.5 %copy-start.1 = (bf16[1,2,8,64,128]{4,3,2,1,0:T(8,128)(2,1)S(1)}, bf16[1,2,8,64,128]{4,3,2,1,0:T(8,128)(2,1)}, u32[]{:S(2)}) copy-start(bf16[1,2,8,64,128]{4,3,2,1,0:T(8,128)(2,1)} %param.13) | copy-start | bytes 786436
  0.0 1.2 copy-start.6
  2.1 12.6 %copy-start.8 = (s32[32]{0:T(128)S(1)}, s32[32]{0:T(128)}, u32[]{:S(2)}) copy-start(s32[32]{0:T(128)} %param.19) | copy-start | bytes 388
  2.1 15.2 %copy-start.9 = (s32[32]{0:T(128)S(1)}, s32[32]{0:T(128)}, u32[]{:S(2)}) copy-start(s32[32]{0:T(128)} %param.18) | copy-start | bytes 388
  2.1 17.1 %copy-start.4 = (s32[1,256]{1,0:T(1,128)S(1)}, s32[1,256]{1,0:T(1,128)}, u32[]{:S(2)}) copy-start(s32[1,256]{1,0:T(1,128)} %param.16) | copy-start | bytes 3076
  2.1 19.9 %copy-start.5 = (f32[1,4,256]{2,1,0:T(4,128)S(1)}, f32[1,4,256]{2,1,0:T(4,128)}, u32[]{:S(2)}) copy-start(f32[1,4,256]{2,1,0:T(4,128)} %param.17) | copy-start | bytes 12292
  3.1 20.5 %all-to-all-start = ((f32[32,1,8,256]{3,2,1,0:T(8,128)}), f32[32,1,8,256]{3,2,1,0:T(8,128)S(1)}, u32[]{:S(2)}, u32[]{:S(2)}) async-start(f32[32,1,8,256]{3,2,1,0:T(8,128)} %slice_select_fusion), calls=%async_computation | async-start | bytes 524288 | tf_op jit(solution)/shard_map/all_to_all | solution.py:491
  12.6 23.3 %collective-permute-start.1 = (f32[4,8,64,128]{3,2,1,0:T(8,128)S(1)}, f32[4,8,64,128]{3,2,1,0:T(8,128)}, u32[]{:S(2)}, u32[]{:S(2)}) collective-permute-start(f32[4,8,64,128]{3,2,1,0:T(8,128)S(1)} %maximum_convert_fusion), channel_id=1, source_target_pairs={{0,2},{1,4},{2,6},{3,0},{4,1},{5,7},{6,5},{7,3},{8,13},{9,15},{10,... | collective-permute-start | bytes 3145736 | tf_op jit(solution)/shard_map/ppermute | solution.py:487
  29.7 35.8 %collective-permute-start = (f32[8,64,128]{2,1,0:T(8,128)S(1)}, f32[8,64,128]{2,1,0:T(8,128)S(1)}, u32[]{:S(2)}, u32[]{:S(2)}) collective-permute-start(f32[8,64,128]{2,1,0:T(8,128)S(1)} %fusion.4), channel_id=1, source_target_pairs={{0,2},{1,4},{2,6},{3,0},{4,1},{5,7},{6,5},{7,3},{8,13},{9,15},{10,... | collective-permute-start | bytes 786440 | tf_op jit(solution)/shard_map/ppermute | solution.py:498
  65.6 0.7 copy-start.3
  111.3 22.0 %copy-start.7 = (s32[2]{0:T(128)S(1)}, s32[2]{0:T(128)}, u32[]{:S(2)}) copy-start(s32[2]{0:T(128)} %copy-done.6) | copy-start | bytes 28
  115.0 29.3 %all-to-all-start.1 = ((f32[32,1,8,256]{3,2,1,0:T(8,128)}), f32[32,1,8,256]{3,2,1,0:T(8,128)S(1)}, u32[]{:S(2)}, u32[]{:S(2)}) async-start(f32[32,1,8,256]{3,2,1,0:T(8,128)} %bitcast.21), calls=%async_computation.1 | async-start | bytes 524288 | tf_op jit(solution)/shard_map/all_to_all | solution.py:510

commit v13 on v12

--- a/solution.py
+++ b/solution.py
@@ -138,32 +138,21 @@
     return gradient + summed.reshape(gradient.shape)
 
 
-def owner_tiles(row_start, col_start, own_cols):
-    owner = jnp.arange(AP_ROWS * own_cols, dtype=jnp.int32)
-    rel_row = (owner // own_cols - row_start) % AP_ROWS
-    rel_col = (owner % own_cols - col_start // TILE) % own_cols
-    return rel_row * own_cols + rel_col
-
-
 def assemble(received, row_start, col_start, own_cols):
     depth_cells = received.shape[2]
-    owner = (
-        (row_start + jnp.arange(AP_ROWS, dtype=jnp.int32)[:, None]) % AP_ROWS * own_cols
-        + (col_start // TILE + jnp.arange(own_cols, dtype=jnp.int32)[None, :]) % own_cols
-    )
-    pieces = received.reshape(-1, depth_cells, TILE * TILE)[owner.reshape(-1)]
-    block = pieces.reshape(AP_ROWS, own_cols, depth_cells, TILE, TILE)
+    block = received.reshape(AP_ROWS, own_cols, depth_cells, TILE, TILE)
     block = block.transpose(2, 0, 3, 1, 4).reshape(depth_cells, AX, AY)
-    return jnp.roll(block, -(col_start % TILE), axis=2)
+    block = jnp.roll(block, -(row_start * TILE), axis=1)
+    return jnp.roll(block, -col_start, axis=2)
 
 
 def disperse(image, row_start, col_start, groups, own_cols, caps):
     depth_cells = image.shape[0]
-    rolled = jnp.roll(image, col_start % TILE, axis=2)
+    rolled = jnp.roll(image, row_start * TILE, axis=1)
+    rolled = jnp.roll(rolled, col_start, axis=2)
     pieces = rolled.reshape(depth_cells, AP_ROWS, TILE, own_cols, TILE)
-    pieces = pieces.transpose(1, 3, 0, 2, 4).reshape(AP_ROWS * own_cols, depth_cells, TILE * TILE)
-    chosen = pieces[owner_tiles(row_start, col_start, own_cols)]
-    return chosen.reshape(groups, 1, depth_cells, TILE * TILE)
+    pieces = pieces.transpose(1, 3, 0, 2, 4)
+    return pieces.reshape(groups, 1, depth_cells, TILE * TILE)
 
 
 X_CHIPS = 4

time: 146 us -> 144 us (0.986)
  waiting for transfers between devices: 38.2 us -> 33.9 us
  starting transfers between devices: 35.7 us -> 38.9 us
    ppermute x1, waiting for transfers between devices: 27.4 us -> 9.35 us  [body(): model = lax.ppermute(model, ('shot', 'sub'), outbound)]
    all_to_all x1, waiting for transfers between devices: 0.02 us -> 13.9 us  [body(): lax.all_to_all(sending, 'shot', split_axis=0, concat_axis=0, tiled=True)]
    all_to_all x1, starting transfers between devices: 9.36 us -> 13.6 us  [body(): lax.all_to_all(sending, 'shot', split_axis=0, concat_axis=0, tiled=True)]
    ppermute x1, starting transfers between devices: 6.07 us -> 3.36 us  [body(): model = lax.ppermute(model, ('shot', 'sub'), outbound)]
    gather x2 -> x0, local copies, waits for them, and re-layouts: 1.86 us -> none  [the longest x1 1.27 us: disperse(): chosen = pieces[owner_tiles(row_start, col_start, own_cols)]]
    all_to_all x1, starting transfers between devices: 18.1 us -> 19.6 us  [body(): lax.all_to_all(images[0], 'shot', split_axis=0, concat_axis=0, tiled=True)]
  transfers between devices with their start and end apart: 4 -> 4, of which waited for: 2 -> 3; matrix products, arithmetic and copies ran while one was open for 10% -> 11% of each run, Pallas kernels for 0% -> 0%
where the time goes in v13:
time: 144 us
  Pallas kernels  41.7 us (29%)
  starting transfers between devices  38.9 us (27%)
  waiting for transfers between devices  33.9 us (24%)
  local copies, waits for them, and re-layouts  17.9 us (12%)
  other arithmetic  6.5 us (5%)
  between operations  4.44 us (3%)
    pallas_call x1, Pallas kernels, migrate(): pl.pallas_call(migrate_kernel, out_shape=jax.ShapeDtypeStruct(model.shape...  41.7 us
    all_to_all x1, starting transfers between devices, body(): lax.all_to_all(images[0], 'shot', split_axis=0, concat_axis=0, tiled=True)  19.6 us
    all_to_all x1, waiting for transfers between devices, body(): lax.all_to_all(sending, 'shot', split_axis=0, concat_axis=0, tiled=True)  13.9 us
    all_to_all x1, starting transfers between devices, body(): lax.all_to_all(sending, 'shot', split_axis=0, concat_axis=0, tiled=True)  13.6 us
    all_to_all x1, waiting for transfers between devices, body(): lax.all_to_all(images[0], 'shot', split_axis=0, concat_axis=0, tiled=True)  10.7 us
    ppermute x1, waiting for transfers between devices, body(): model = lax.ppermute(model, ('shot', 'sub'), outbound)  9.35 us
    ppermute x1, starting transfers between devices, body(): model = lax.ppermute(model, ('shot', 'sub'), outbound)  3.36 us
    reshape x1, local copies, waits for them, and re-layouts, disperse(): return pieces.reshape(groups, 1, depth_cells, TILE * TILE)  3.05 us
  transfers between devices with their start and end apart: 4, of which 3 were waited for; matrix products, arithmetic and copies ran while one was open for 11% of the time, Pallas kernels for 0%

profile of v13, /device:TPU:5, one launch (start us, length us, event | category | flops | bytes accessed | tf_op | source)
XLA Modules:
  0.0 143.7 jit_solution(10747369340614234920)
XLA Ops:
  0.0 1.1 maximum_convert_fusion
  1.2 2.3 %collective-permute-start.1 = (f32[4,8,64,128]{3,2,1,0:T(8,128)S(1)}, f32[4,8,64,128]{3,2,1,0:T(8,128)}, u32[]{:S(2)}, u32[]{:S(2)}) collective-permute-start(f32[4,8,64,128]{3,2,1,0:T(8,128)S(1)} %maximum_convert_fusion), channel_id=1, source_target_pairs={{0,2},{1,4},{2,6},{3,0},{4,1},{5,7},{6,5},{7,3},{8,13},{9,15},{10,... | collective-permute-start | bytes 3145736 | tf_op jit(solution)/shard_map/ppermute | solution.py:476
  3.5 0.7 and_select_fusion.8
  4.8 0.6 gather_fusion
  5.5 0.1 broadcast_select_fusion
  5.7 0.7 slice_select_fusion
  6.5 13.6 %all-to-all-start = ((f32[32,1,8,256]{3,2,1,0:T(8,128)}), f32[32,1,8,256]{3,2,1,0:T(8,128)S(1)}, u32[]{:S(2)}, u32[]{:S(2)}) async-start(f32[32,1,8,256]{3,2,1,0:T(8,128)} %slice_select_fusion), calls=%async_computation | async-start | bytes 524288 | tf_op jit(solution)/shard_map/all_to_all | solution.py:480
  20.2 0.6 dynamic_slice.12
  21.5 0.6 dynamic_slice.13
  25.6 0.8 copy.33
  26.4 0.6 pad_add_fusion.1.src_ref
  26.9 0.6 pad_add_fusion.rrow_ref
  27.5 0.7 add_select_fusion.rcol_ref
  28.2 13.9 %all-to-all-done = f32[32,1,8,256]{3,2,1,0:T(8,128)S(1)} async-done(((f32[32,1,8,256]{3,2,1,0:T(8,128)}), f32[32,1,8,256]{3,2,1,0:T(8,128)S(1)}, u32[]{:S(2)}, u32[]{:S(2)}) %all-to-all-start) | async-done | bytes 262176 | tf_op jit(solution)/shard_map/all_to_all | solution.py:480
  42.1 0.6 reshape.391
  42.7 2.6 %copy.35 = f32[8,4,16,8,16]{4,3,2,1,0:T(8,128)} copy(f32[8,4,16,8,16]{4,2,0,3,1:T(8,128)S(1)} %bitcast.66) | data formatting | bytes 524288 | tf_op jit(solution)/shard_map/transpose | solution.py:144
  45.3 2.2 %reshape.392 = f32[8,64,128]{2,1,0:T(8,128)S(1)} reshape(f32[8,4,16,8,16]{4,3,2,1,0:T(8,128)} %copy.35) | data formatting | bytes 524288 | tf_op jit(solution)/shard_map/reshape | solution.py:144
  47.5 0.2 fusion.5
  47.7 3.4 %collective-permute-start = (f32[8,64,128]{2,1,0:T(8,128)S(1)}, f32[8,64,128]{2,1,0:T(8,128)S(1)}, u32[]{:S(2)}, u32[]{:S(2)}) collective-permute-start(f32[8,64,128]{2,1,0:T(8,128)S(1)} %fusion.5), channel_id=1, source_target_pairs={{0,2},{1,4},{2,6},{3,0},{4,1},{5,7},{6,5},{7,3},{8,13},{9,15},{10,... | collective-permute-start | bytes 786440 | tf_op jit(solution)/shard_map/ppermute | solution.py:487
  51.1 2.3 %fusion.18 = (f32[2,8,64,128]{3,2,1,0:T(8,128)}, f32[2,8,64,128]{3,2,1,0:T(8,128)}) fusion(f32[4,8,64,128]{3,2,1,0:T(8,128)} %collective-permute-done.1), kind=kLoop, calls=%fused_computation.81 | loop fusion | bytes 2097152 | tf_op jit(solution)/shard_map/slice | solution.py:492
  53.4 9.4 %collective-permute-done.model_ref = f32[8,64,128]{2,1,0:T(8,128)S(1)} collective-permute-done((f32[8,64,128]{2,1,0:T(8,128)S(1)}, f32[8,64,128]{2,1,0:T(8,128)S(1)}, u32[]{:S(2)}, u32[]{:S(2)}) %collective-permute-start) | collective-permute-done | bytes 262176 | tf_op jit(solution)/shard_map/ppermute | solution.py:487
  62.8 0.7 copy-done.1
  63.5 41.7 %shard_map.91 = f32[8,64,128]{2,1,0:T(8,128)} custom-call(s32[3]{0:T(128)} %pad_add_fusion.1.src_ref, f32[4]{0:T(128)} %bitcast.74, s32[2,256]{1,0:T(2,128)} %pad_add_fusion.rrow_ref, s32[256,1]{1,0:T(8,128)} %add_select_fusion.rcol_ref, f32[256,4]{1,0:T(8,128)} %bitcast.70, f32[8,64,128]{2,1,0:T(8,128)} %copy-done.1, ...), custom_call_target="tpu_custom_call" | custom-call | tf_op jit(solution)/shard_map/pallas_call | solution.py:417
  105.2 1.0 fusion.4
  106.2 0.2 fusion.3
  106.4 0.6 reshape.393
  107.0 1.7 %copy.36 = f32[4,8,8,16,16]{4,3,2,1,0:T(8,128)} copy(f32[4,8,8,16,16]{4,1,3,0,2:T(8,128)S(1)} %bitcast.67) | data formatting | bytes 524288 | tf_op jit(solution)/shard_map/transpose | solution.py:154
  108.7 3.0 %reshape.394 = f32[32,1,8,256]{3,2,0,1:T(8,128)} reshape(f32[4,8,8,16,16]{4,3,2,1,0:T(8,128)} %copy.36) | data formatting | bytes 524288 | tf_op jit(solution)/shard_map/reshape | solution.py:155
  111.7 19.6 %all-to-all-start.1 = ((f32[32,1,8,256]{3,2,1,0:T(8,128)}), f32[32,1,8,256]{3,2,1,0:T(8,128)S(1)}, u32[]{:S(2)}, u32[]{:S(2)}) async-start(f32[32,1,8,256]{3,2,1,0:T(8,128)} %bitcast.18), calls=%async_computation.1 | async-start | bytes 524288 | tf_op jit(solution)/shard_map/all_to_all | solution.py:499
  131.8 10.7 %all-to-all-done.1 = f32[32,1,8,256]{3,2,1,0:T(8,128)S(1)} async-done(((f32[32,1,8,256]{3,2,1,0:T(8,128)}), f32[32,1,8,256]{3,2,1,0:T(8,128)S(1)}, u32[]{:S(2)}, u32[]{:S(2)}) %all-to-all-start.1) | async-done | bytes 262176 | tf_op jit(solution)/shard_map/all_to_all | solution.py:499
  142.6 0.4 fusion
  143.0 0.7 copy.39
  (34 shorter events, 1.4 us)
Async XLA Ops:
  0.0 4.8 %copy-start = (f32[12,8,256]{2,1,0:T(8,128)S(1)}, f32[12,8,256]{2,1,0:T(8,128)}, u32[]{:S(2)}) copy-start(f32[12,8,256]{2,1,0:T(8,128)} %param.13) | copy-start | bytes 294916
  1.1 19.0 %copy-start.2 = (s32[1,256]{1,0:T(1,128)S(1)}, s32[1,256]{1,0:T(1,128)}, u32[]{:S(2)}) copy-start(s32[1,256]{1,0:T(1,128)} %param.18) | copy-start | bytes 3076
  1.2 19.0 %copy-start.4 = (s32[32]{0:T(128)S(1)}, s32[32]{0:T(128)}, u32[]{:S(2)}) copy-start(s32[32]{0:T(128)} %param.20) | copy-start | bytes 388
  1.2 20.3 %copy-start.5 = (s32[32]{0:T(128)S(1)}, s32[32]{0:T(128)}, u32[]{:S(2)}) copy-start(s32[32]{0:T(128)} %param.21) | copy-start | bytes 388
  1.2 24.4 %copy-start.3 = (f32[1,4,256]{2,1,0:T(4,128)S(1)}, f32[1,4,256]{2,1,0:T(4,128)}, u32[]{:S(2)}) copy-start(f32[1,4,256]{2,1,0:T(4,128)} %param.19) | copy-start | bytes 12292
  1.2 49.9 %collective-permute-start.1 = (f32[4,8,64,128]{3,2,1,0:T(8,128)S(1)}, f32[4,8,64,128]{3,2,1,0:T(8,128)}, u32[]{:S(2)}, u32[]{:S(2)}) collective-permute-start(f32[4,8,64,128]{3,2,1,0:T(8,128)S(1)} %maximum_convert_fusion), channel_id=1, source_target_pairs={{0,2},{1,4},{2,6},{3,0},{4,1},{5,7},{6,5},{7,3},{8,13},{9,15},{10,... | collective-permute-start | bytes 3145736 | tf_op jit(solution)/shard_map/ppermute | solution.py:476
  6.5 35.6 %all-to-all-start = ((f32[32,1,8,256]{3,2,1,0:T(8,128)}), f32[32,1,8,256]{3,2,1,0:T(8,128)S(1)}, u32[]{:S(2)}, u32[]{:S(2)}) async-start(f32[32,1,8,256]{3,2,1,0:T(8,128)} %slice_select_fusion), calls=%async_computation | async-start | bytes 524288 | tf_op jit(solution)/shard_map/all_to_all | solution.py:480
  47.7 15.0 %collective-permute-start = (f32[8,64,128]{2,1,0:T(8,128)S(1)}, f32[8,64,128]{2,1,0:T(8,128)S(1)}, u32[]{:S(2)}, u32[]{:S(2)}) collective-permute-start(f32[8,64,128]{2,1,0:T(8,128)S(1)} %fusion.5), channel_id=1, source_target_pairs={{0,2},{1,4},{2,6},{3,0},{4,1},{5,7},{6,5},{7,3},{8,13},{9,15},{10,... | collective-permute-start | bytes 786440 | tf_op jit(solution)/shard_map/ppermute | solution.py:487
  62.8 0.7 copy-start.1
  111.7 30.8 %all-to-all-start.1 = ((f32[32,1,8,256]{3,2,1,0:T(8,128)}), f32[32,1,8,256]{3,2,1,0:T(8,128)S(1)}, u32[]{:S(2)}, u32[]{:S(2)}) async-start(f32[32,1,8,256]{3,2,1,0:T(8,128)} %bitcast.18), calls=%async_computation.1 | async-start | bytes 524288 | tf_op jit(solution)/shard_map/all_to_all | solution.py:499

commit v14 on v13

--- a/solution.py
+++ b/solution.py
@@ -1,3 +1,5 @@
+import functools
+
 import jax
 import jax.numpy as jnp
 from jax import lax
@@ -281,7 +283,7 @@
 
         lax.fori_loop(0, depth, plane, 0)
 
-    def exchange(r, f):
+    def exchange(r, f, halves=(True, True)):
         buf = (pad_p, pad_q)[f]
         down = pltpu.make_async_remote_copy(
             src_ref=buf.at[r, RADIUS : 2 * RADIUS],
@@ -300,15 +302,21 @@
             device_id_type=pl.DeviceIdType.MESH,
         )
 
+        if halves[0]:
+            start_down(down)
+        if halves[1]:
+            start_up(up)
+        return (down, up)
+
+    def start_down(down):
         @pl.when(me > 0)
         def _():
             down.start()
 
+    def start_up(up):
         @pl.when(me < n_sub - 1)
         def _():
             up.start()
-
-        return (down, up)
 
     def finish(pair):
         down, up = pair
@@ -323,7 +331,7 @@
             up.wait_send()
             down.wait_recv()
 
-    def forward_round(r):
+    def forward_round(r, midway=None):
         def plane(j, carry):
             p = j + RADIUS
             lp = plane_stencil(pad_p, r, p, rows, lanes)
@@ -335,9 +343,13 @@
                 pad_p[r + 1, p] = following + source
             return carry
 
-        lax.fori_loop(0, depth, plane, 0)
-
-    def adjoint_round(r):
+        half = depth // 2
+        lax.fori_loop(0, half, plane, 0)
+        if midway is not None:
+            midway()
+        lax.fori_loop(half, depth, plane, 0)
+
+    def adjoint_round(r, midway=None):
         def plane(j, carry):
             p = j + RADIUS
             lq = plane_stencil(pad_q, r, p, rows, lanes)
@@ -361,21 +373,31 @@
                 img_loc[j] = IMAGE_SCALE * image
             return carry
 
-        lax.fori_loop(0, depth, plane, 0)
+        half = depth // 2
+        lax.fori_loop(0, half, plane, 0)
+        if midway is not None:
+            midway()
+        lax.fori_loop(half, depth, plane, 0)
 
     fwd = exchange(0, 0)
     adj = exchange(0, 1)
     build_injection(NT - 1)
     for r in range(NT):
         finish(fwd)
-        forward_round(r)
         if r < NT - 1:
-            fwd = exchange(r + 1, 0)
+            fwd = exchange(r + 1, 0, (False, False))
+            forward_round(r, functools.partial(start_down, fwd[0]))
+            start_up(fwd[1])
+        else:
+            forward_round(r)
         finish(adj)
-        adjoint_round(r)
         if r < NT - 1:
-            adj = exchange(r + 1, 1)
+            adj = exchange(r + 1, 1, (False, False))
+            adjoint_round(r, functools.partial(start_down, adj[0]))
+            start_up(adj[1])
             build_injection(NT - 2 - r)
+        else:
+            adjoint_round(r)
     image_copy = pltpu.make_async_remote_copy(
         src_ref=img_loc,
         dst_ref=img_scr,

time: 144 us -> 145 us (level)
  starting transfers between devices: 38.9 us -> 40.4 us
    all_to_all x1, starting transfers between devices: 19.6 us -> 21.1 us  [body(): lax.all_to_all(images[0], 'shot', split_axis=0, concat_axis=0, tiled=True)]
  transfers between devices with their start and end apart: 4 -> 4, of which waited for: 3 -> 3; matrix products, arithmetic and copies ran while one was open for 11% -> 10% of each run, Pallas kernels for 0% -> 0%
where the time goes in v14:
time: 145 us
  Pallas kernels  41.1 us (28%)
  starting transfers between devices  40.4 us (28%)
  waiting for transfers between devices  33.9 us (23%)
  local copies, waits for them, and re-layouts  17.9 us (12%)
  other arithmetic  6.51 us (4%)
  between operations  4.44 us (3%)
    pallas_call x1, Pallas kernels, migrate(): pl.pallas_call(migrate_kernel, out_shape=jax.ShapeDtypeStruct(model.shape...  41.1 us
    all_to_all x1, starting transfers between devices, body(): lax.all_to_all(images[0], 'shot', split_axis=0, concat_axis=0, tiled=True)  21.1 us
    all_to_all x1, waiting for transfers between devices, body(): lax.all_to_all(sending, 'shot', split_axis=0, concat_axis=0, tiled=True)  13.9 us
    all_to_all x1, starting transfers between devices, body(): lax.all_to_all(sending, 'shot', split_axis=0, concat_axis=0, tiled=True)  13.6 us
    all_to_all x1, waiting for transfers between devices, body(): lax.all_to_all(images[0], 'shot', split_axis=0, concat_axis=0, tiled=True)  10.7 us
    ppermute x1, waiting for transfers between devices, body(): model = lax.ppermute(model, ('shot', 'sub'), outbound)  9.35 us
    ppermute x1, starting transfers between devices, body(): model = lax.ppermute(model, ('shot', 'sub'), outbound)  3.36 us
    reshape x1, local copies, waits for them, and re-layouts, disperse(): return pieces.reshape(groups, 1, depth_cells, TILE * TILE)  3.05 us
  transfers between devices with their start and end apart: 4, of which 3 were waited for; matrix products, arithmetic and copies ran while one was open for 10% of the time, Pallas kernels for 0%

profile of v14, /device:TPU:5, one launch (start us, length us, event | category | flops | bytes accessed | tf_op | source)
XLA Modules:
  0.0 144.7 jit_solution(3705726776475686705)
XLA Ops:
  0.0 1.1 maximum_convert_fusion
  1.2 2.3 %collective-permute-start.1 = (f32[4,8,64,128]{3,2,1,0:T(8,128)S(1)}, f32[4,8,64,128]{3,2,1,0:T(8,128)}, u32[]{:S(2)}, u32[]{:S(2)}) collective-permute-start(f32[4,8,64,128]{3,2,1,0:T(8,128)S(1)} %maximum_convert_fusion), channel_id=1, source_target_pairs={{0,2},{1,4},{2,6},{3,0},{4,1},{5,7},{6,5},{7,3},{8,13},{9,15},{10,... | collective-permute-start | bytes 3145736 | tf_op jit(solution)/shard_map/ppermute | solution.py:498
  3.5 0.7 and_select_fusion.8
  4.8 0.6 gather_fusion
  5.5 0.1 broadcast_select_fusion
  5.7 0.7 slice_select_fusion
  6.5 13.6 %all-to-all-start = ((f32[32,1,8,256]{3,2,1,0:T(8,128)}), f32[32,1,8,256]{3,2,1,0:T(8,128)S(1)}, u32[]{:S(2)}, u32[]{:S(2)}) async-start(f32[32,1,8,256]{3,2,1,0:T(8,128)} %slice_select_fusion), calls=%async_computation | async-start | bytes 524288 | tf_op jit(solution)/shard_map/all_to_all | solution.py:502
  20.2 0.6 dynamic_slice.12
  21.5 0.6 dynamic_slice.13
  25.6 0.8 copy.33
  26.4 0.6 pad_add_fusion.1.src_ref
  26.9 0.6 pad_add_fusion.rrow_ref
  27.5 0.7 add_select_fusion.rcol_ref
  28.2 13.9 %all-to-all-done = f32[32,1,8,256]{3,2,1,0:T(8,128)S(1)} async-done(((f32[32,1,8,256]{3,2,1,0:T(8,128)}), f32[32,1,8,256]{3,2,1,0:T(8,128)S(1)}, u32[]{:S(2)}, u32[]{:S(2)}) %all-to-all-start) | async-done | bytes 262176 | tf_op jit(solution)/shard_map/all_to_all | solution.py:502
  42.1 0.6 reshape.391
  42.7 2.6 %copy.35 = f32[8,4,16,8,16]{4,3,2,1,0:T(8,128)} copy(f32[8,4,16,8,16]{4,2,0,3,1:T(8,128)S(1)} %bitcast.66) | data formatting | bytes 524288 | tf_op jit(solution)/shard_map/transpose | solution.py:146
  45.3 2.2 %reshape.392 = f32[8,64,128]{2,1,0:T(8,128)S(1)} reshape(f32[8,4,16,8,16]{4,3,2,1,0:T(8,128)} %copy.35) | data formatting | bytes 524288 | tf_op jit(solution)/shard_map/reshape | solution.py:146
  47.5 0.2 fusion.5
  47.7 3.4 %collective-permute-start = (f32[8,64,128]{2,1,0:T(8,128)S(1)}, f32[8,64,128]{2,1,0:T(8,128)S(1)}, u32[]{:S(2)}, u32[]{:S(2)}) collective-permute-start(f32[8,64,128]{2,1,0:T(8,128)S(1)} %fusion.5), channel_id=1, source_target_pairs={{0,2},{1,4},{2,6},{3,0},{4,1},{5,7},{6,5},{7,3},{8,13},{9,15},{10,... | collective-permute-start | bytes 786440 | tf_op jit(solution)/shard_map/ppermute | solution.py:509
  51.1 2.3 %fusion.18 = (f32[2,8,64,128]{3,2,1,0:T(8,128)}, f32[2,8,64,128]{3,2,1,0:T(8,128)}) fusion(f32[4,8,64,128]{3,2,1,0:T(8,128)} %collective-permute-done.1), kind=kLoop, calls=%fused_computation.81 | loop fusion | bytes 2097152 | tf_op jit(solution)/shard_map/slice | solution.py:514
  53.4 9.4 %collective-permute-done.model_ref = f32[8,64,128]{2,1,0:T(8,128)S(1)} collective-permute-done((f32[8,64,128]{2,1,0:T(8,128)S(1)}, f32[8,64,128]{2,1,0:T(8,128)S(1)}, u32[]{:S(2)}, u32[]{:S(2)}) %collective-permute-start) | collective-permute-done | bytes 262176 | tf_op jit(solution)/shard_map/ppermute | solution.py:509
  62.8 0.7 copy-done.1
  63.5 41.1 %shard_map.91 = f32[8,64,128]{2,1,0:T(8,128)} custom-call(s32[3]{0:T(128)} %pad_add_fusion.1.src_ref, f32[4]{0:T(128)} %bitcast.74, s32[2,256]{1,0:T(2,128)} %pad_add_fusion.rrow_ref, s32[256,1]{1,0:T(8,128)} %add_select_fusion.rcol_ref, f32[256,4]{1,0:T(8,128)} %bitcast.70, f32[8,64,128]{2,1,0:T(8,128)} %copy-done.1, ...), custom_call_target="tpu_custom_call" | custom-call | tf_op jit(solution)/shard_map/pallas_call | solution.py:439
  104.6 1.0 fusion.4
  105.6 0.2 fusion.3
  105.9 0.6 reshape.393
  106.5 1.7 %copy.36 = f32[4,8,8,16,16]{4,3,2,1,0:T(8,128)} copy(f32[4,8,8,16,16]{4,1,3,0,2:T(8,128)S(1)} %bitcast.67) | data formatting | bytes 524288 | tf_op jit(solution)/shard_map/transpose | solution.py:156
  108.2 3.0 %reshape.394 = f32[32,1,8,256]{3,2,0,1:T(8,128)} reshape(f32[4,8,8,16,16]{4,3,2,1,0:T(8,128)} %copy.36) | data formatting | bytes 524288 | tf_op jit(solution)/shard_map/reshape | solution.py:157
  111.2 21.1 %all-to-all-start.1 = ((f32[32,1,8,256]{3,2,1,0:T(8,128)}), f32[32,1,8,256]{3,2,1,0:T(8,128)S(1)}, u32[]{:S(2)}, u32[]{:S(2)}) async-start(f32[32,1,8,256]{3,2,1,0:T(8,128)} %bitcast.18), calls=%async_computation.1 | async-start | bytes 524288 | tf_op jit(solution)/shard_map/all_to_all | solution.py:521
  132.8 10.7 %all-to-all-done.1 = f32[32,1,8,256]{3,2,1,0:T(8,128)S(1)} async-done(((f32[32,1,8,256]{3,2,1,0:T(8,128)}), f32[32,1,8,256]{3,2,1,0:T(8,128)S(1)}, u32[]{:S(2)}, u32[]{:S(2)}) %all-to-all-start.1) | async-done | bytes 262176 | tf_op jit(solution)/shard_map/all_to_all | solution.py:521
  143.6 0.4 fusion
  144.0 0.7 copy.39
  (34 shorter events, 1.4 us)
Async XLA Ops:
  0.0 4.8 %copy-start = (f32[12,8,256]{2,1,0:T(8,128)S(1)}, f32[12,8,256]{2,1,0:T(8,128)}, u32[]{:S(2)}) copy-start(f32[12,8,256]{2,1,0:T(8,128)} %param.13) | copy-start | bytes 294916
  1.1 19.0 %copy-start.2 = (s32[1,256]{1,0:T(1,128)S(1)}, s32[1,256]{1,0:T(1,128)}, u32[]{:S(2)}) copy-start(s32[1,256]{1,0:T(1,128)} %param.18) | copy-start | bytes 3076
  1.2 19.0 %copy-start.4 = (s32[32]{0:T(128)S(1)}, s32[32]{0:T(128)}, u32[]{:S(2)}) copy-start(s32[32]{0:T(128)} %param.20) | copy-start | bytes 388
  1.2 20.3 %copy-start.5 = (s32[32]{0:T(128)S(1)}, s32[32]{0:T(128)}, u32[]{:S(2)}) copy-start(s32[32]{0:T(128)} %param.21) | copy-start | bytes 388
  1.2 24.4 %copy-start.3 = (f32[1,4,256]{2,1,0:T(4,128)S(1)}, f32[1,4,256]{2,1,0:T(4,128)}, u32[]{:S(2)}) copy-start(f32[1,4,256]{2,1,0:T(4,128)} %param.19) | copy-start | bytes 12292
  1.2 49.9 %collective-permute-start.1 = (f32[4,8,64,128]{3,2,1,0:T(8,128)S(1)}, f32[4,8,64,128]{3,2,1,0:T(8,128)}, u32[]{:S(2)}, u32[]{:S(2)}) collective-permute-start(f32[4,8,64,128]{3,2,1,0:T(8,128)S(1)} %maximum_convert_fusion), channel_id=1, source_target_pairs={{0,2},{1,4},{2,6},{3,0},{4,1},{5,7},{6,5},{7,3},{8,13},{9,15},{10,... | collective-permute-start | bytes 3145736 | tf_op jit(solution)/shard_map/ppermute | solution.py:498
  6.5 35.6 %all-to-all-start = ((f32[32,1,8,256]{3,2,1,0:T(8,128)}), f32[32,1,8,256]{3,2,1,0:T(8,128)S(1)}, u32[]{:S(2)}, u32[]{:S(2)}) async-start(f32[32,1,8,256]{3,2,1,0:T(8,128)} %slice_select_fusion), calls=%async_computation | async-start | bytes 524288 | tf_op jit(solution)/shard_map/all_to_all | solution.py:502
  47.7 15.0 %collective-permute-start = (f32[8,64,128]{2,1,0:T(8,128)S(1)}, f32[8,64,128]{2,1,0:T(8,128)S(1)}, u32[]{:S(2)}, u32[]{:S(2)}) collective-permute-start(f32[8,64,128]{2,1,0:T(8,128)S(1)} %fusion.5), channel_id=1, source_target_pairs={{0,2},{1,4},{2,6},{3,0},{4,1},{5,7},{6,5},{7,3},{8,13},{9,15},{10,... | collective-permute-start | bytes 786440 | tf_op jit(solution)/shard_map/ppermute | solution.py:509
  62.8 0.7 copy-start.1
  111.2 32.2 %all-to-all-start.1 = ((f32[32,1,8,256]{3,2,1,0:T(8,128)}), f32[32,1,8,256]{3,2,1,0:T(8,128)S(1)}, u32[]{:S(2)}, u32[]{:S(2)}) async-start(f32[32,1,8,256]{3,2,1,0:T(8,128)} %bitcast.18), calls=%async_computation.1 | async-start | bytes 524288 | tf_op jit(solution)/shard_map/all_to_all | solution.py:521

commit v15 on v13

--- a/solution.py
+++ b/solution.py
@@ -130,10 +130,13 @@
     spare = usable[:, 1, None, None]
     first = jnp.where(spare & lower, 0.0, piece)
     second = jnp.where(spare & lower, piece, 0.0)
-    pieces = jnp.stack([first, second], axis=1).reshape(groups * caps, -1)
     hot = (local[:, None] == jnp.arange(gradient.shape[0], dtype=jnp.int32)[None, :]) & usable.reshape(-1)[:, None]
+    hot = hot.astype(jnp.float32).reshape(groups, caps, -1)
     summed = jnp.einsum(
-        "st,sf->tf", hot.astype(jnp.float32), pieces, precision=lax.Precision.HIGHEST
+        "st,sf->tf", hot[:, 0], first.reshape(groups, -1), precision=lax.Precision.HIGHEST
+    )
+    summed = summed + jnp.einsum(
+        "st,sf->tf", hot[:, 1], second.reshape(groups, -1), precision=lax.Precision.HIGHEST
     )
     return gradient + summed.reshape(gradient.shape)
 

time: 144 us -> 144 us (level)
  transfers between devices with their start and end apart: 4 -> 4, of which waited for: 3 -> 3; matrix products, arithmetic and copies ran while one was open for 11% -> 10% of each run, Pallas kernels for 0% -> 0%
where the time goes in v15:
time: 144 us
  Pallas kernels  41.7 us (29%)
  starting transfers between devices  38.9 us (27%)
  waiting for transfers between devices  34.2 us (24%)
  local copies, waits for them, and re-layouts  17.7 us (12%)
  other arithmetic  6.45 us (4%)
  between operations  4.45 us (3%)
    pallas_call x1, Pallas kernels, migrate(): pl.pallas_call(migrate_kernel, out_shape=jax.ShapeDtypeStruct(model.shape...  41.7 us
    all_to_all x1, starting transfers between devices, body(): lax.all_to_all(images[0], 'shot', split_axis=0, concat_axis=0, tiled=True)  19.7 us
    all_to_all x1, waiting for transfers between devices, body(): lax.all_to_all(sending, 'shot', split_axis=0, concat_axis=0, tiled=True)  13.9 us
    all_to_all x1, starting transfers between devices, body(): lax.all_to_all(sending, 'shot', split_axis=0, concat_axis=0, tiled=True)  13.6 us
    all_to_all x1, waiting for transfers between devices, body(): lax.all_to_all(images[0], 'shot', split_axis=0, concat_axis=0, tiled=True)  11 us
    ppermute x1, waiting for transfers between devices, body(): model = lax.ppermute(model, ('shot', 'sub'), outbound)  9.35 us
    ppermute x1, starting transfers between devices, body(): model = lax.ppermute(model, ('shot', 'sub'), outbound)  3.36 us
    reshape x1, local copies, waits for them, and re-layouts, disperse(): return pieces.reshape(groups, 1, depth_cells, TILE * TILE)  3.05 us
  transfers between devices with their start and end apart: 4, of which 3 were waited for; matrix products, arithmetic and copies ran while one was open for 10% of the time, Pallas kernels for 0%

profile of v15, /device:TPU:5, one launch (start us, length us, event | category | flops | bytes accessed | tf_op | source)
XLA Modules:
  0.0 143.9 jit_solution(7621714288618195605)
XLA Ops:
  0.0 1.1 maximum_convert_fusion
  1.2 2.3 %collective-permute-start.1 = (f32[4,8,64,128]{3,2,1,0:T(8,128)S(1)}, f32[4,8,64,128]{3,2,1,0:T(8,128)}, u32[]{:S(2)}, u32[]{:S(2)}) collective-permute-start(f32[4,8,64,128]{3,2,1,0:T(8,128)S(1)} %maximum_convert_fusion), channel_id=1, source_target_pairs={{0,2},{1,4},{2,6},{3,0},{4,1},{5,7},{6,5},{7,3},{8,13},{9,15},{10,... | collective-permute-start | bytes 3145736 | tf_op jit(solution)/shard_map/ppermute | solution.py:479
  3.5 0.7 and_select_fusion.8
  4.8 0.6 gather_fusion
  5.7 0.7 slice_select_fusion
  6.5 13.6 %all-to-all-start = ((f32[32,1,8,256]{3,2,1,0:T(8,128)}), f32[32,1,8,256]{3,2,1,0:T(8,128)S(1)}, u32[]{:S(2)}, u32[]{:S(2)}) async-start(f32[32,1,8,256]{3,2,1,0:T(8,128)} %slice_select_fusion), calls=%async_computation | async-start | bytes 524288 | tf_op jit(solution)/shard_map/all_to_all | solution.py:483
  20.2 0.6 dynamic_slice.12
  21.5 0.6 dynamic_slice.13
  25.6 0.8 copy.30
  26.4 0.6 pad_add_fusion.1.src_ref
  26.9 0.6 pad_add_fusion.rrow_ref
  27.5 0.7 add_select_fusion.rcol_ref
  28.2 13.9 %all-to-all-done = f32[32,1,8,256]{3,2,1,0:T(8,128)S(1)} async-done(((f32[32,1,8,256]{3,2,1,0:T(8,128)}), f32[32,1,8,256]{3,2,1,0:T(8,128)S(1)}, u32[]{:S(2)}, u32[]{:S(2)}) %all-to-all-start) | async-done | bytes 262176 | tf_op jit(solution)/shard_map/all_to_all | solution.py:483
  42.1 0.6 reshape.435
  42.7 2.6 %copy.32 = f32[8,4,16,8,16]{4,3,2,1,0:T(8,128)} copy(f32[8,4,16,8,16]{4,2,0,3,1:T(8,128)S(1)} %bitcast.57) | data formatting | bytes 524288 | tf_op jit(solution)/shard_map/transpose | solution.py:147
  45.3 2.2 %reshape.436 = f32[8,64,128]{2,1,0:T(8,128)S(1)} reshape(f32[8,4,16,8,16]{4,3,2,1,0:T(8,128)} %copy.32) | data formatting | bytes 524288 | tf_op jit(solution)/shard_map/reshape | solution.py:147
  47.5 0.2 fusion.2
  47.7 3.4 %collective-permute-start = (f32[8,64,128]{2,1,0:T(8,128)S(1)}, f32[8,64,128]{2,1,0:T(8,128)S(1)}, u32[]{:S(2)}, u32[]{:S(2)}) collective-permute-start(f32[8,64,128]{2,1,0:T(8,128)S(1)} %fusion.2), channel_id=1, source_target_pairs={{0,2},{1,4},{2,6},{3,0},{4,1},{5,7},{6,5},{7,3},{8,13},{9,15},{10,... | collective-permute-start | bytes 786440 | tf_op jit(solution)/shard_map/ppermute | solution.py:490
  51.1 2.3 %fusion.14 = (f32[2,8,64,128]{3,2,1,0:T(8,128)}, f32[2,8,64,128]{3,2,1,0:T(8,128)}) fusion(f32[4,8,64,128]{3,2,1,0:T(8,128)} %collective-permute-done.1), kind=kLoop, calls=%fused_computation.80 | loop fusion | bytes 2097152 | tf_op jit(solution)/shard_map/slice | solution.py:495
  53.4 9.4 %collective-permute-done.model_ref = f32[8,64,128]{2,1,0:T(8,128)S(1)} collective-permute-done((f32[8,64,128]{2,1,0:T(8,128)S(1)}, f32[8,64,128]{2,1,0:T(8,128)S(1)}, u32[]{:S(2)}, u32[]{:S(2)}) %collective-permute-start) | collective-permute-done | bytes 262176 | tf_op jit(solution)/shard_map/ppermute | solution.py:490
  62.8 0.7 copy-done.1
  63.5 41.7 %shard_map.91 = f32[8,64,128]{2,1,0:T(8,128)} custom-call(s32[3]{0:T(128)} %pad_add_fusion.1.src_ref, f32[4]{0:T(128)} %bitcast.70, s32[2,256]{1,0:T(2,128)} %pad_add_fusion.rrow_ref, s32[256,1]{1,0:T(8,128)} %add_select_fusion.rcol_ref, f32[256,4]{1,0:T(8,128)} %bitcast.65, f32[8,64,128]{2,1,0:T(8,128)} %copy-done.1, ...), custom_call_target="tpu_custom_call" | custom-call | tf_op jit(solution)/shard_map/pallas_call | solution.py:420
  105.2 1.0 fusion.1
  106.2 0.2 fusion
  106.4 0.6 reshape.437
  107.0 1.7 %copy.33 = f32[4,8,8,16,16]{4,3,2,1,0:T(8,128)} copy(f32[4,8,8,16,16]{4,1,3,0,2:T(8,128)S(1)} %bitcast.58) | data formatting | bytes 524288 | tf_op jit(solution)/shard_map/transpose | solution.py:157
  108.7 3.0 %reshape.438 = f32[32,1,8,256]{3,2,0,1:T(8,128)} reshape(f32[4,8,8,16,16]{4,3,2,1,0:T(8,128)} %copy.33) | data formatting | bytes 524288 | tf_op jit(solution)/shard_map/reshape | solution.py:158
  111.7 19.7 %all-to-all-start.1 = ((f32[32,1,8,256]{3,2,1,0:T(8,128)}), f32[32,1,8,256]{3,2,1,0:T(8,128)S(1)}, u32[]{:S(2)}, u32[]{:S(2)}) async-start(f32[32,1,8,256]{3,2,1,0:T(8,128)} %bitcast.18), calls=%async_computation.1 | async-start | bytes 524288 | tf_op jit(solution)/shard_map/all_to_all | solution.py:502
  131.5 11.0 %all-to-all-done.1 = f32[32,1,8,256]{3,2,1,0:T(8,128)S(1)} async-done(((f32[32,1,8,256]{3,2,1,0:T(8,128)}), f32[32,1,8,256]{3,2,1,0:T(8,128)S(1)}, u32[]{:S(2)}, u32[]{:S(2)}) %all-to-all-start.1) | async-done | bytes 262176 | tf_op jit(solution)/shard_map/all_to_all | solution.py:502
  142.7 0.2 fusion.6
  142.9 0.2 convolution_add_fusion
  143.2 0.6 slice.37
  (34 shorter events, 1.4 us)
Async XLA Ops:
  0.0 4.8 %copy-start = (f32[12,8,256]{2,1,0:T(8,128)S(1)}, f32[12,8,256]{2,1,0:T(8,128)}, u32[]{:S(2)}) copy-start(f32[12,8,256]{2,1,0:T(8,128)} %param.13) | copy-start | bytes 294916
  1.1 19.0 %copy-start.2 = (s32[1,256]{1,0:T(1,128)S(1)}, s32[1,256]{1,0:T(1,128)}, u32[]{:S(2)}) copy-start(s32[1,256]{1,0:T(1,128)} %param.18) | copy-start | bytes 3076
  1.2 19.0 %copy-start.4 = (s32[32]{0:T(128)S(1)}, s32[32]{0:T(128)}, u32[]{:S(2)}) copy-start(s32[32]{0:T(128)} %param.20) | copy-start | bytes 388
  1.2 20.3 %copy-start.5 = (s32[32]{0:T(128)S(1)}, s32[32]{0:T(128)}, u32[]{:S(2)}) copy-start(s32[32]{0:T(128)} %param.21) | copy-start | bytes 388
  1.2 24.4 %copy-start.3 = (f32[1,4,256]{2,1,0:T(4,128)S(1)}, f32[1,4,256]{2,1,0:T(4,128)}, u32[]{:S(2)}) copy-start(f32[1,4,256]{2,1,0:T(4,128)} %param.19) | copy-start | bytes 12292
  1.2 49.9 %collective-permute-start.1 = (f32[4,8,64,128]{3,2,1,0:T(8,128)S(1)}, f32[4,8,64,128]{3,2,1,0:T(8,128)}, u32[]{:S(2)}, u32[]{:S(2)}) collective-permute-start(f32[4,8,64,128]{3,2,1,0:T(8,128)S(1)} %maximum_convert_fusion), channel_id=1, source_target_pairs={{0,2},{1,4},{2,6},{3,0},{4,1},{5,7},{6,5},{7,3},{8,13},{9,15},{10,... | collective-permute-start | bytes 3145736 | tf_op jit(solution)/shard_map/ppermute | solution.py:479
  6.5 35.6 %all-to-all-start = ((f32[32,1,8,256]{3,2,1,0:T(8,128)}), f32[32,1,8,256]{3,2,1,0:T(8,128)S(1)}, u32[]{:S(2)}, u32[]{:S(2)}) async-start(f32[32,1,8,256]{3,2,1,0:T(8,128)} %slice_select_fusion), calls=%async_computation | async-start | bytes 524288 | tf_op jit(solution)/shard_map/all_to_all | solution.py:483
  47.7 15.0 %collective-permute-start = (f32[8,64,128]{2,1,0:T(8,128)S(1)}, f32[8,64,128]{2,1,0:T(8,128)S(1)}, u32[]{:S(2)}, u32[]{:S(2)}) collective-permute-start(f32[8,64,128]{2,1,0:T(8,128)S(1)} %fusion.2), channel_id=1, source_target_pairs={{0,2},{1,4},{2,6},{3,0},{4,1},{5,7},{6,5},{7,3},{8,13},{9,15},{10,... | collective-permute-start | bytes 786440 | tf_op jit(solution)/shard_map/ppermute | solution.py:490
  62.8 0.7 copy-start.1
  111.7 30.8 %all-to-all-start.1 = ((f32[32,1,8,256]{3,2,1,0:T(8,128)}), f32[32,1,8,256]{3,2,1,0:T(8,128)S(1)}, u32[]{:S(2)}, u32[]{:S(2)}) async-start(f32[32,1,8,256]{3,2,1,0:T(8,128)} %bitcast.18), calls=%async_computation.1 | async-start | bytes 524288 | tf_op jit(solution)/shard_map/all_to_all | solution.py:502
